TPU v7x, 256 devices: a whole 4x4x8 slice. The times are simulated.
256 devices in a mesh: row: 8 (over y, z_hi), col: 32 (over z_lo, x, core).
Axes of the slice: x: 4, y: 4, z: 8 (z_hi: 2, z_lo: 4; z = z_hi * 4 + z_lo), core: 2. Of those that a mesh axis runs over, the one named last changes fastest.
Arguments:
- embedding: bfloat16 [98304, 256], P(('col', 'row')), may hold values from -6 to 6
- weight: bfloat16 [256, 256], replicated, may hold values from -0.375 to 0.375
- grad_out: bfloat16 [98304, 256], P(('row', 'col')), may hold values from -6 to 6
- in_degree: int32 [98304], P(('row', 'col')), may hold values from 4 to 64
- out_degree: int32 [98304], P(('col', 'row')), may hold values from 4 to 64
- tile_edges: bfloat16 [8, 32, 192, 128, 128], P('row', 'col'), may hold values from 0 to 2, as said below
- tile_coords: int32 [8, 32, 192, 2], P('row', 'col'), may hold values from 0 to 95, as said below
- tile_count: int32 [8, 32], P('row', 'col'), may hold values from 48 to 192, as said below
Outputs:
- hidden: bfloat16 [98304, 256], P(('row', 'col'))
- grad_embedding: float32 [98304, 256], P(('col', 'row'))
- grad_weight: float32 [256, 256], replicated
Inputs may be any that keep to these rules, and one draw needn't show every extreme that they name: `tile_coords`: slots of one block name distinct tiles; entry 0 is a tile row below 96, entry 1 a tile column below 24. The live slots of a block are its first tile_count slots; some block has all 192 slots live. `tile_edges`: each entry is zero or a positive edge weight.
All inputs are finite; a program needn't handle non-finite values.
Results may differ from a plain program's by a relative error of at most 0.033.
Values may be sent and summed in bfloat16 or wider, within the bound.
No kernel may reach another device: no remote copies, remote signals or barrier semaphores. Data moves between devices by JAX's collectives and lax.ppermute only.
A program may use at most 128 MiB of HBM per device.

v0:
```python
import functools
import math

import jax
import jax.numpy as jnp
from jax import lax
from jax.experimental import pallas as pl
from jax.experimental.pallas import tpu as pltpu
from jax.sharding import PartitionSpec as P

decay_rate = 0.01
f32 = jnp.float32
bf16 = jnp.bfloat16

chunks = ((0,), (1, 2))
unroll = 8
padded = 256

x_bit, z_bit, y_bit = 1, 3, 1


def exchange(value, axis, mask):
    size = lax.axis_size(axis)
    return lax.ppermute(value, axis, [(i, i ^ mask) for i in range(size)])


def after(value, earlier):
    return lax.optimization_barrier((value, earlier))[0]


def group_kernel(table, tiles, *rest, spans, group, flipped, carried):
    pieces = rest[: len(spans)]
    previous = rest[len(spans)] if carried else None
    out, source = rest[-2:]
    slots, edge, _ = tiles.shape
    row = 0
    for piece, span in zip(pieces, spans):

        def move(i, _, piece=piece, row=row):
            source[pl.ds(row + i * 64, 64)] = piece[pl.ds(i * 64, 64)]
            return 0

        lax.fori_loop(0, span // 64, move, 0)
        row += span

    def clear(i, _):
        if carried:
            out[i] = previous[i].astype(out.dtype)
        else:
            out[i] = jnp.zeros(out.shape[1:], out.dtype)
        return 0

    lax.fori_loop(0, out.shape[0], clear, 0)
    start = table[0, slots + group]
    stop = table[0, slots + group + 1]
    dims = (((0,), (0,)), ((), ())) if flipped else (((1,), (0,)), ((), ()))

    def advance(number, total):
        for step in range(unroll):
            index = start + number * unroll + step
            real = index < stop
            entry = table[0, jnp.minimum(index, stop - 1)]
            slot = entry & 255
            place = (entry >> 8) & 255
            origin = pl.multiple_of(((entry >> 16) & 255) * edge, edge)
            fresh = jnp.logical_and(real, (entry >> 24) == 1)
            product = lax.dot_general(
                tiles[slot], source[pl.ds(origin, edge)], dims, preferred_element_type=f32
            )
            product = product * real.astype(f32)
            if carried:
                total = jnp.where(fresh, previous[place], total) + product
            else:
                total = total * (1.0 - fresh.astype(f32)) + product
            out[place] = total.astype(out.dtype)
        return total

    steps = (stop - start + unroll - 1) // unroll
    lax.fori_loop(0, steps, advance, jnp.zeros(out.shape[1:], f32))


def group_products(table, tiles, pieces, count, group, flipped, previous=None, dtype=bf16):
    slots, edge, _ = tiles.shape
    arrays = [array for array, _ in pieces]
    spans = [span for _, span in pieces]
    width = arrays[0].shape[1]
    operands = [table, tiles] + arrays + ([] if previous is None else [previous])
    whole = pl.BlockSpec(memory_space=pltpu.VMEM)
    return pl.pallas_call(
        functools.partial(
            group_kernel,
            spans=spans,
            group=group,
            flipped=flipped,
            carried=previous is not None,
        ),
        out_shape=jax.ShapeDtypeStruct((count, edge, width), dtype),
        in_specs=[pl.BlockSpec(memory_space=pltpu.SMEM)] + [whole] * (len(operands) - 1),
        out_specs=whole,
        scratch_shapes=[pltpu.VMEM((sum(spans), width), bf16)],
        compiler_params=pltpu.CompilerParams(vmem_limit_bytes=24 << 20),
        cost_estimate=pl.CostEstimate(
            flops=2 * slots * edge * edge * width // 4,
            bytes_accessed=count * edge * width * 4,
            transcendentals=0,
        ),
        name=("backward" if flipped else "forward") + str(group),
    )(*operands)


def order_kernel(coords, place_info, tiles, forward, backward, *, per_owner):
    del tiles
    slots = coords.shape[0]
    shape = (slots, padded)
    own_col = place_info[0]
    own_row = place_info[1]
    live_count = place_info[2]
    number = lax.broadcasted_iota(jnp.int32, (slots, 1), 0)
    alive = number < live_count
    tile_row = coords[:, 0:1]
    tile_col = coords[:, 1:2]
    owner_row = ((tile_row.astype(f32) + 0.5) * (1.0 / per_owner)).astype(jnp.int32)
    owner_col = ((tile_col.astype(f32) + 0.5) * (1.0 / per_owner)).astype(jnp.int32)
    apart = owner_row ^ own_col
    part = tile_row - owner_row * per_owner
    core = apart & 1
    x = (apart >> x_bit) & 3
    z = (apart >> z_bit) & 3
    block = (z >> 1) * 8 + x * 2 + (z & 1)
    chunk = jnp.zeros_like(part)
    inner = jnp.zeros_like(part)
    breadth = jnp.zeros_like(part)
    for k, members in enumerate(chunks):
        for i, member in enumerate(members):
            chunk = jnp.where(part == member, k, chunk)
            inner = jnp.where(part == member, i, inner)
            breadth = jnp.where(part == member, len(members), breadth)
    row_apart = owner_col ^ own_row
    source_place = ((row_apart & 1) * 4 + (row_apart >> y_bit)) * per_owner
    source_place = source_place + tile_col - owner_col * per_owner
    forward_place = block * breadth + inner
    forward_key = (chunk * 2 + 1 - core) * 128 + forward_place
    backward_origin = (core * 16 + x * 4 + z) * breadth + inner
    backward_key = chunk * 128 + source_place

    lane = lax.broadcasted_iota(jnp.int32, shape, 1)
    sub = lax.broadcasted_iota(jnp.int32, shape, 0)
    limit = ((lane[0:1] - slots) * 128).astype(f32)
    lane_number = lane[0:1].astype(f32)

    def table(key, place, origin, groups, out):
        key = jnp.where(alive, key, 1 << 20).astype(f32)
        place = jnp.where(alive, place, 0)
        origin = jnp.where(alive, origin, 0)
        across = jnp.sum(jnp.where(lane == sub, key, 0.0), axis=0, keepdims=True)
        same = jnp.logical_and(across == key, lane < sub)
        ahead = jnp.logical_and(jnp.logical_or(across < key, same), lane < slots)
        rank = jnp.sum(jnp.where(ahead, 1.0, 0.0), axis=1, keepdims=True)
        repeats = jnp.sum(jnp.where(same, 1.0, 0.0), axis=1, keepdims=True)
        fresh = (repeats == 0.0).astype(jnp.int32)
        low = (number | (place << 8)).astype(f32)
        high = (origin | (fresh << 8)).astype(f32)
        hit = rank == lane_number
        low = jnp.sum(jnp.where(hit, low, 0.0), axis=0, keepdims=True).astype(jnp.int32)
        high = jnp.sum(jnp.where(hit, high, 0.0), axis=0, keepdims=True).astype(jnp.int32)
        bound = jnp.minimum(limit, groups * 128.0)
        bounds = jnp.sum(jnp.where(key < bound, 1.0, 0.0), axis=0, keepdims=True)
        out[...] = jnp.where(lane[0:1] < slots, low | (high << 16), bounds.astype(jnp.int32))

    table(forward_key, forward_place, source_place, 2 * len(chunks), forward)
    table(backward_key, source_place, backward_origin, len(chunks), backward)


def slot_tables(coords, live_count, own_col, own_row, per_owner, tiles):
    place_info = jnp.stack([own_col, own_row, live_count])
    whole = pl.BlockSpec(memory_space=pltpu.VMEM)
    result = jax.ShapeDtypeStruct((1, padded), jnp.int32)
    return pl.pallas_call(
        functools.partial(order_kernel, per_owner=per_owner),
        out_shape=(result, result),
        in_specs=[whole, pl.BlockSpec(memory_space=pltpu.SMEM), whole],
        out_specs=(whole, whole),
        compiler_params=pltpu.CompilerParams(vmem_limit_bytes=8 << 20),
        name="order",
    )(coords, place_info, tiles)


def ring_gather(block, axis, bit, half, earlier=None):
    near, far = 1 << bit, 3 << bit
    first = exchange(block, axis, near)
    third = exchange(block, axis, far)
    if earlier is not None:
        first, third = after((first, third), earlier)
    second_low = exchange(first[:half], axis, far)
    second_high = exchange(third[half:], axis, near)
    return [block, first, second_low, second_high, third]


def wide(value):
    return value.astype(f32)


def reduce_row(terms, share):
    near, far = 1 << y_bit, 3 << y_bit
    rows, width = terms.shape[2:]
    low, high = terms[0], terms[1]

    def send(value, mask):
        message = jnp.concatenate([value.reshape(-1, width), share.astype(bf16)], axis=0)
        message = exchange(message, "row", mask)
        split = message.shape[0] - share.shape[0]
        return message[:split].reshape(value.shape), share + wide(message[split:])

    high_in = exchange(high[2:4], "row", far)
    low_in, share = send(low[1:3], near)
    high_next = exchange((wide(high[1]) + wide(high_in[0])).astype(bf16), "row", near)
    low_next, share = send((wide(low[3]) + wide(low_in[1])).astype(bf16), far)
    leaving = (wide(high[0]) + wide(high_in[1]) + wide(high_next)).astype(bf16)
    arrived = exchange(leaving, "row", 1)
    return wide(low[0]) + wide(low_in[0]) + wide(low_next) + wide(arrived), share


def per_device(
    embedding, weight, grad_out, in_degree, out_degree, tile_edges, tile_coords, tile_count
):
    tiles = tile_edges[0, 0]
    n_row = lax.axis_size("row")
    n_col = lax.axis_size("col")
    own_row = lax.axis_index("row").astype(jnp.int32)
    own_col = lax.axis_index("col").astype(jnp.int32)
    own_rows, width = embedding.shape
    edge = tiles.shape[1]
    per_owner = own_rows // edge
    total_nodes = own_rows * n_row * n_col

    scale_out = lax.rsqrt(out_degree.astype(f32))
    scale_in = lax.rsqrt(in_degree.astype(f32))
    scaled = (scale_out[:, None] * wide(embedding)).astype(bf16)
    forward_table, backward_table = slot_tables(
        tile_coords[0, 0], tile_count[0, 0], own_col, own_row, per_owner, tiles
    )
    source = ring_gather(scaled, "row", y_bit, own_rows // 2)
    across = exchange(scaled, "row", 1)
    source += ring_gather(across, "row", y_bit, own_rows // 2, forward_table)
    source = [(piece, piece.shape[0]) for piece in source]

    near, far = 1 << x_bit, 3 << x_bit
    z = (own_col >> z_bit) & 3
    share_rows = width // 4
    number = range(len(chunks))
    heights = [len(members) * edge for members in chunks]

    def own(k, value):
        return jnp.concatenate([value[m * edge : (m + 1) * edge] for m in chunks[k]], axis=0)

    first_messages = []
    both = []
    for k in number:
        table = after(forward_table, first_messages[-1]) if k else forward_table
        count = 16 * len(chunks[k])
        shape = (2, 4, 2, heights[k], width)
        leaving = group_products(table, tiles, source, count, 2 * k, False)
        core_in = exchange(leaving, "col", 1).reshape(shape)
        kept = group_products(table, tiles, source, count, 2 * k + 1, False).reshape(shape)

        def sums(half, low, high, kept=kept, core_in=core_in):
            return wide(kept[half, low:high]) + wide(core_in[half, low:high])

        both.append(sums)
        first_messages.append((sums(0, 1, 3).astype(bf16), sums(1, 2, 4).astype(bf16)))
    reduced = []
    second_messages = None
    for k in number:
        messages = first_messages[k]
        if k:
            messages = after(messages, second_messages)
        low_in = exchange(messages[0], "col", near)
        high_in = exchange(messages[1], "col", far)
        second_messages = (
            (both[k](0, 3, 4)[0] + wide(low_in[1])).astype(bf16),
            (both[k](1, 1, 2)[0] + wide(high_in[0])).astype(bf16),
        )
        low_next = exchange(second_messages[0], "col", far)
        high_next = exchange(second_messages[1], "col", near)
        low = both[k](0, 0, 1)[0] + wide(low_in[0]) + wide(low_next)
        high = both[k](1, 0, 1)[0] + wide(high_in[1]) + wide(high_next)
        reduced.append((low[0], low[1].astype(bf16), high[0].astype(bf16), high[1].astype(bf16)))

    hidden_parts = []
    local_weight = jnp.zeros((width, width), f32)
    stacks = []
    upstream = None
    for k in number:
        rows = heights[k]
        last = k == len(chunks) - 1
        blocks = reduced[k]
        if k:
            blocks = after(blocks, upstream)
        summed = blocks[0]
        for distance in (1, 2, 3):
            summed = summed + wide(exchange(blocks[distance], "col", distance << z_bit))
        if k:
            summed = after(summed, stacks[-1])
        chunk_scale = own(k, scale_in)
        aggregate = (chunk_scale[:, None] * summed).astype(bf16)
        preact = jnp.dot(aggregate, weight, preferred_element_type=f32)
        gates = jax.nn.sigmoid(preact)
        hidden_parts.append((preact * gates).astype(bf16))
        delta = (wide(own(k, grad_out)) * gates * (1.0 + preact * (1.0 - gates))).astype(bf16)
        local_weight = local_weight + lax.dot_general(
            aggregate, delta, (((0,), (0,)), ((), ())), preferred_element_type=f32
        )
        projected = lax.dot_general(
            delta, weight, (((1,), (1,)), ((), ())), preferred_element_type=f32
        )
        upstream = (chunk_scale[:, None] * projected).astype(bf16)

        def weight_share(distance):
            return lax.dynamic_slice_in_dim(
                local_weight, (z ^ distance) * share_rows, share_rows, 0
            )

        stack = [upstream]
        if last:
            share = weight_share(0)
        for distance in (1, 2, 3):
            message = upstream
            if last:
                message = jnp.concatenate([upstream, weight_share(distance).astype(bf16)], axis=0)
            message = exchange(message, "col", distance << z_bit)
            stack.append(message[:rows])
            if last:
                share = share + wide(message[rows:])
        if last:
            stack.append(share.astype(bf16))
        stacks.append(jnp.concatenate(stack, axis=0))

    terms = None
    for k in number:
        rows = heights[k]
        last = k == len(chunks) - 1
        stack = stacks[k]
        if k:
            stack = after(stack, (second_low, second_high))
        first = exchange(stack, "col", near)
        third = exchange(stack, "col", far)
        if k:
            terms = products(k - 1)
            first, third = after((first, third), terms)
        low = first[: 2 * rows]
        if last:
            low = jnp.concatenate([low, first[4 * rows :]], axis=0)
        second_low = exchange(low, "col", far)
        second_high = exchange(third[2 * rows : 4 * rows], "col", near)
        if last:
            share = share + wide(first[4 * rows :]) + wide(third[4 * rows :])
            share = share + wide(second_low[2 * rows :])
        pieces = [
            (stack, 4 * rows),
            (first, 4 * rows),
            (second_low, 2 * rows),
            (second_high, 2 * rows),
            (third, 4 * rows),
        ]

        def products(k, last=last, pieces=pieces, terms=terms):
            arrived = [(exchange(piece[:span], "col", 1), span) for piece, span in pieces]
            return group_products(
                backward_table,
                tiles,
                pieces + arrived,
                n_row * per_owner,
                k,
                True,
                terms,
                bf16 if last else f32,
            )

    for axis, mask in (("col", 1), ("row", 1)):
        share = share + exchange(share, axis, mask)
    terms = products(len(chunks) - 1)
    source_total, share = reduce_row(terms.reshape(2, 4, own_rows, width), share)
    grad_weight = jnp.zeros((width, width), f32)
    for distance in (0, 1, 2, 3):
        piece = exchange(share, "col", distance << z_bit) if distance else share
        grad_weight = lax.dynamic_update_slice_in_dim(
            grad_weight, piece, (z ^ distance) * share_rows, 0
        )
    grad_weight = grad_weight / math.sqrt(total_nodes)
    decay = decay_rate * jnp.sqrt(out_degree.astype(f32))
    grad_embedding = scale_out[:, None] * source_total + decay[:, None] * wide(embedding)

    hidden = jnp.concatenate(hidden_parts, axis=0)
    return (hidden, grad_embedding, grad_weight)


def solution(mesh):
    in_specs = (
        P(("col", "row"), None),
        P(),
        P(("row", "col"), None),
        P(("row", "col")),
        P(("col", "row")),
        P("row", "col", None, None, None),
        P("row", "col", None, None),
        P("row", "col"),
    )
    out_specs = (P(("row", "col"), None), P(("col", "row"), None), P())
    return jax.shard_map(
        per_device, mesh=mesh, in_specs=in_specs, out_specs=out_specs, check_vma=False
    )
```

profile of v0, /device:TPU:1, one launch (start us, length us, event | category | flops | bytes accessed | tf_op | source)
XLA Modules:
  0.0 220.8 jit_solution(5194080458454454721)
XLA Ops:
  2.4 7.8 %collective-permute-start.4 = (bf16[384,256]{1,0:T(8,128)(2,1)S(1)}, bf16[384,256]{1,0:T(8,128)(2,1)S(1)}, u32[]{:S(2)}, u32[]{:S(2)}) collective-permute-start(bf16[384,256]{1,0:T(8,128)(2,1)S(1)} %fusion.9.rest_0_), channel_id=1, source_target_pairs={{0,32},{32,0},{64,96},{96,64},{128,160},{160,128},{192,224},{224,1... | collective-permute-start | bytes 589832 | tf_op jit(solution)/shard_map/ppermute | solution.py:24
  19.6 2.8 %copy-done.1 = bf16[1,1,192,128,128]{4,3,2,1,0:T(8,128)(2,1)S(1)} copy-done((bf16[1,1,192,128,128]{4,3,2,1,0:T(8,128)(2,1)S(1)}, bf16[1,1,192,128,128]{4,3,2,1,0:T(8,128)(2,1)}, u32[]{:S(2)}) %copy-start.1) | copy-done | bytes 6291480
  32.6 2.8 %collective-permute-start.9 = (bf16[16,128,256]{2,1,0:T(8,128)(2,1)S(1)}, bf16[16,128,256]{2,1,0:T(8,128)(2,1)S(1)}, u32[]{:S(2)}, u32[]{:S(2)}) collective-permute-start(bf16[16,128,256]{2,1,0:T(8,128)(2,1)S(1)} %forward0.1), channel_id=1, source_target_pairs={{0,1},{1,0},{2,3},{3,2},{4,5},{5,4},{6,7},{7,6},{8,9},{9,8},{10,11... | collective-permute-start | bytes 3145736 | tf_op jit(solution)/shard_map/ppermute | solution.py:24
  40.6 4.2 %collective-permute-start.13 = (bf16[2,2,128,256]{3,2,1,0:T(8,128)(2,1)S(1)}, bf16[2,2,128,256]{3,2,1,0:T(8,128)(2,1)S(1)}, u32[]{:S(2)}, u32[]{:S(2)}) collective-permute-start(bf16[2,2,128,256]{3,2,1,0:T(8,128)(2,1)S(1)} %get-tuple-element.43), channel_id=1, source_target_pairs={{0,6},{1,7},{2,4},{3,5},{4,2},{5,3},{6,0},{7,1},{8,14},{9,15},{10,... | collective-permute-start | bytes 786440 | tf_op jit(solution)/shard_map/ppermute | solution.py:24
  44.8 6.3 %collective-permute-done.13 = bf16[2,2,128,256]{3,2,1,0:T(8,128)(2,1)S(1)} collective-permute-done((bf16[2,2,128,256]{3,2,1,0:T(8,128)(2,1)S(1)}, bf16[2,2,128,256]{3,2,1,0:T(8,128)(2,1)S(1)}, u32[]{:S(2)}, u32[]{:S(2)}) %collective-permute-start.13) | collective-permute-done | bytes 262176 | tf_op jit(solution)/shard_map/ppermute | solution.py:24
  51.3 2.2 %forward3.1 = bf16[32,128,256]{2,1,0:T(8,128)(2,1)S(1)} custom-call(s32[1,256]{1,0:T(1,128)S(1)} %get-tuple-element.21.table, bf16[192,128,128]{2,1,0:T(8,128)(2,1)S(1)} %bitcast.136, bf16[384,256]{1,0:T(8,128)(2,1)S(1)} %fusion.9.rest_0_, bf16[384,256]{1,0:T(8,128)(2,1)S(1)} %collective-permute-done.rest_1_, ...), custom_call_target="tpu_custom_call" | custom-call | flops 402653184 | bytes 4194304 | tf_op jit(solution)/shard_map/forward3/pallas_call | solution.py:89
  55.2 2.4 %collective-permute-start.11 = (bf16[2,128,256]{2,1,0:T(8,128)(2,1)S(1)}, bf16[2,128,256]{2,1,0:T(8,128)(2,1)S(1)}, u32[]{:S(2)}, u32[]{:S(2)}) collective-permute-start(bf16[2,128,256]{2,1,0:T(8,128)(2,1)S(1)} %get-tuple-element.42), channel_id=1, source_target_pairs={{0,6},{1,7},{2,4},{3,5},{4,2},{5,3},{6,0},{7,1},{8,14},{9,15},{10,... | collective-permute-start | bytes 393224 | tf_op jit(solution)/shard_map/ppermute | solution.py:24
  58.4 5.2 %collective-permute-start.16 = (bf16[128,256]{1,0:T(8,128)(2,1)S(1)}, bf16[128,256]{1,0:T(8,128)(2,1)S(1)}, u32[]{:S(2)}, u32[]{:S(2)}) collective-permute-start(bf16[128,256]{1,0:T(8,128)(2,1)S(1)} %get-tuple-element.62), channel_id=1, source_target_pairs={{0,24},{1,25},{2,26},{3,27},{4,28},{5,29},{6,30},{7,31},{8,16},{9,... | collective-permute-start | bytes 196616 | tf_op jit(solution)/shard_map/ppermute | solution.py:24
  65.5 7.0 %collective-permute-done.20 = bf16[2,2,256,256]{3,2,1,0:T(8,128)(2,1)S(1)} collective-permute-done((bf16[2,2,256,256]{3,2,1,0:T(8,128)(2,1)S(1)}, bf16[2,2,256,256]{3,2,1,0:T(8,128)(2,1)S(1)}, u32[]{:S(2)}, u32[]{:S(2)}) %collective-permute-start.20) | collective-permute-done | bytes 524320 | tf_op jit(solution)/shard_map/ppermute | solution.py:24
  73.0 2.7 %collective-permute-done.18 = bf16[2,2,256,256]{3,2,1,0:T(8,128)(2,1)S(1)} collective-permute-done((bf16[2,2,256,256]{3,2,1,0:T(8,128)(2,1)S(1)}, bf16[2,2,256,256]{3,2,1,0:T(8,128)(2,1)S(1)}, u32[]{:S(2)}, u32[]{:S(2)}) %collective-permute-start.18) | collective-permute-done | bytes 524320 | tf_op jit(solution)/shard_map/ppermute | solution.py:24
  75.7 5.6 %collective-permute-done.21 = bf16[2,256,256]{2,1,0:T(8,128)(2,1)S(1)} collective-permute-done((bf16[2,256,256]{2,1,0:T(8,128)(2,1)S(1)}, bf16[2,256,256]{2,1,0:T(8,128)(2,1)S(1)}, u32[]{:S(2)}, u32[]{:S(2)}) %collective-permute-start.21) | collective-permute-done | bytes 262176 | tf_op jit(solution)/shard_map/ppermute | solution.py:24
  83.5 3.8 %collective-permute-start.27 = (bf16[128,256]{1,0:T(8,128)(2,1)S(1)}, bf16[128,256]{1,0:T(8,128)(2,1)S(1)}, u32[]{:S(2)}, u32[]{:S(2)}) collective-permute-start(bf16[128,256]{1,0:T(8,128)(2,1)S(1)} %fusion.1), channel_id=1, source_target_pairs={{0,24},{1,25},{2,26},{3,27},{4,28},{5,29},{6,30},{7,31},{8,16},{9,... | collective-permute-start | bytes 196616 | tf_op jit(solution)/shard_map/ppermute | solution.py:24
  89.2 4.2 %collective-permute-start.24 = (bf16[256,256]{1,0:T(8,128)(2,1)S(1)}, bf16[256,256]{1,0:T(8,128)(2,1)S(1)}, u32[]{:S(2)}, u32[]{:S(2)}) collective-permute-start(bf16[256,256]{1,0:T(8,128)(2,1)S(1)} %get-tuple-element.27), channel_id=1, source_target_pairs={{0,24},{1,25},{2,26},{3,27},{4,28},{5,29},{6,30},{7,31},{8,16},{9,... | collective-permute-start | bytes 393224 | tf_op jit(solution)/shard_map/ppermute | solution.py:24
  96.6 9.5 %collective-permute-done.23 = bf16[256,256]{1,0:T(8,128)(2,1)S(1)} collective-permute-done((bf16[256,256]{1,0:T(8,128)(2,1)S(1)}, bf16[256,256]{1,0:T(8,128)(2,1)S(1)}, u32[]{:S(2)}, u32[]{:S(2)}) %collective-permute-start.23) | collective-permute-done | bytes 131104 | tf_op jit(solution)/shard_map/ppermute | solution.py:24
  108.2 2.5 %collective-permute-start.29 = (bf16[320,256]{1,0:T(8,128)(2,1)S(1)}, bf16[320,256]{1,0:T(8,128)(2,1)S(1)}, u32[]{:S(2)}, u32[]{:S(2)}) collective-permute-start(bf16[320,256]{1,0:T(8,128)(2,1)S(1)} %get-tuple-element.59), channel_id=1, source_target_pairs={{0,16},{1,17},{2,18},{3,19},{4,20},{5,21},{6,22},{7,23},{8,24},{9,... | collective-permute-start | bytes 491528 | tf_op jit(solution)/shard_map/ppermute | solution.py:24
  111.8 2.3 %collective-permute-done.29 = bf16[320,256]{1,0:T(8,128)(2,1)S(1)} collective-permute-done((bf16[320,256]{1,0:T(8,128)(2,1)S(1)}, bf16[320,256]{1,0:T(8,128)(2,1)S(1)}, u32[]{:S(2)}, u32[]{:S(2)}) %collective-permute-start.29) | collective-permute-done | bytes 163872 | tf_op jit(solution)/shard_map/ppermute | solution.py:24
  114.1 6.4 %collective-permute-done.30 = bf16[320,256]{1,0:T(8,128)(2,1)S(1)} collective-permute-done((bf16[320,256]{1,0:T(8,128)(2,1)S(1)}, bf16[320,256]{1,0:T(8,128)(2,1)S(1)}, u32[]{:S(2)}, u32[]{:S(2)}) %collective-permute-start.30) | collective-permute-done | bytes 163872 | tf_op jit(solution)/shard_map/ppermute | solution.py:24
  120.6 2.3 %collective-permute-start.35 = (bf16[1088,256]{1,0:T(8,128)(2,1)S(1)}, bf16[1088,256]{1,0:T(8,128)(2,1)S(1)}, u32[]{:S(2)}, u32[]{:S(2)}) collective-permute-start(bf16[1088,256]{1,0:T(8,128)(2,1)S(1)} %convert_dynamic-update-slice_fusion.rest_0_), channel_id=1, source_target_pairs={{0,2},{1,3},{2,0},{3,1},{4,6},{5,7},{6,4},{7,5},{8,10},{9,11},{10,... | collective-permute-start | bytes 1671176 | tf_op jit(solution)/shard_map/ppermute | solution.py:24
  122.9 12.6 %collective-permute-start.36 = (bf16[1088,256]{1,0:T(8,128)(2,1)S(1)}, bf16[1088,256]{1,0:T(8,128)(2,1)S(1)}, u32[]{:S(2)}, u32[]{:S(2)}) collective-permute-start(bf16[1088,256]{1,0:T(8,128)(2,1)S(1)} %convert_dynamic-update-slice_fusion.rest_0_), channel_id=1, source_target_pairs={{0,6},{1,7},{2,4},{3,5},{4,2},{5,3},{6,0},{7,1},{8,14},{9,15},{10,... | collective-permute-start | bytes 1671176 | tf_op jit(solution)/shard_map/ppermute | solution.py:24
  135.5 2.6 %collective-permute-start.37 = (bf16[512,256]{1,0:T(8,128)(2,1)S(1)}, bf16[512,256]{1,0:T(8,128)(2,1)S(1)}, u32[]{:S(2)}, u32[]{:S(2)}) collective-permute-start(bf16[512,256]{1,0:T(8,128)(2,1)S(1)} %pad_maximum_fusion.2.rest_0_), channel_id=1, source_target_pairs={{0,1},{1,0},{2,3},{3,2},{4,5},{5,4},{6,7},{7,6},{8,9},{9,8},{10,11... | collective-permute-start | bytes 786440 | tf_op jit(solution)/shard_map/ppermute | solution.py:24
  141.0 2.8 %copy-done.3 = bf16[1,1,192,128,128]{4,3,2,1,0:T(8,128)(2,1)S(1)} copy-done((bf16[1,1,192,128,128]{4,3,2,1,0:T(8,128)(2,1)S(1)}, bf16[1,1,192,128,128]{4,3,2,1,0:T(8,128)(2,1)}, u32[]{:S(2)}) %copy-start.3) | copy-done | bytes 6291480
  143.8 2.9 %backward0.1.rest_10_ = f32[24,128,256]{2,1,0:T(8,128)S(1)} custom-call(s32[1,256]{1,0:T(1,128)S(1)} %get-tuple-element.29.table, bf16[192,128,128]{2,1,0:T(8,128)(2,1)S(1)} %bitcast.137, bf16[512,256]{1,0:T(8,128)(2,1)S(1)} %pad_maximum_fusion.2.rest_0_, bf16[512,256]{1,0:T(8,128)(2,1)S(1)} %collective-permute-done.31.rest_1_, ...), custom_call_target="tpu_custom_call" | custom-call | flops 402653184 | bytes 3145728 | tf_op jit(solution)/shard_map/backward0/pallas_call | solution.py:89
  148.7 3.6 %collective-permute-start.44 = (bf16[1024,256]{1,0:T(8,128)(2,1)S(1)}, bf16[1024,256]{1,0:T(8,128)(2,1)S(1)}, u32[]{:S(2)}, u32[]{:S(2)}) collective-permute-start(bf16[1024,256]{1,0:T(8,128)(2,1)S(1)} %slice.321), channel_id=1, source_target_pairs={{0,1},{1,0},{2,3},{3,2},{4,5},{5,4},{6,7},{7,6},{8,9},{9,8},{10,11... | collective-permute-start | bytes 1572872 | tf_op jit(solution)/shard_map/ppermute | solution.py:24
  154.2 3.4 %collective-permute-start.49 = (f32[64,256]{1,0:T(8,128)S(1)}, f32[64,256]{1,0:T(8,128)S(1)}, u32[]{:S(2)}, u32[]{:S(2)}) collective-permute-start(f32[64,256]{1,0:T(8,128)S(1)} %convert_add_fusion.15), channel_id=1, source_target_pairs={{0,1},{1,0},{2,3},{3,2},{4,5},{5,4},{6,7},{7,6},{8,9},{9,8},{10,11... | collective-permute-start | bytes 196616 | tf_op jit(solution)/shard_map/ppermute | solution.py:24
  158.5 5.4 %collective-permute-start.50 = (f32[64,256]{1,0:T(8,128)S(1)}, f32[64,256]{1,0:T(8,128)S(1)}, u32[]{:S(2)}, u32[]{:S(2)}) collective-permute-start(f32[64,256]{1,0:T(8,128)S(1)} %add.280), channel_id=1, source_target_pairs={{0,32},{32,0},{64,96},{96,64},{128,160},{160,128},{192,224},{224,1... | collective-permute-start | bytes 196616 | tf_op jit(solution)/shard_map/ppermute | solution.py:24
  168.3 3.9 %backward1.1 = bf16[24,128,256]{2,1,0:T(8,128)(2,1)S(1)} custom-call(s32[1,256]{1,0:T(1,128)S(1)} %get-tuple-element.29.table, bf16[192,128,128]{2,1,0:T(8,128)(2,1)S(1)} %bitcast.138, bf16[1088,256]{1,0:T(8,128)(2,1)S(1)} %convert_dynamic-update-slice_fusion.rest_0_, bf16[1088,256]{1,0:T(8,128)(2,1)S(1)} %collective-permute-done.35.rest_1_, ...), custom_call_target="tpu_custom_call" | custom-call | flops 402653184 | bytes 3145728 | tf_op jit(solution)/shard_map/backward1/pallas_call | solution.py:89
  172.4 2.8 %collective-permute-start.51 = (bf16[832,256]{1,0:T(8,128)(2,1)S(1)}, bf16[832,256]{1,0:T(8,128)(2,1)S(1)}, u32[]{:S(2)}, u32[]{:S(2)}) collective-permute-start(bf16[832,256]{1,0:T(8,128)(2,1)S(1)} %pad_maximum_fusion), channel_id=1, source_target_pairs={{0,64},{32,96},{64,0},{96,32},{128,192},{160,224},{192,128},{224,1... | collective-permute-start | bytes 1277960 | tf_op jit(solution)/shard_map/ppermute | solution.py:24
  175.9 8.7 %collective-permute-done.51 = bf16[832,256]{1,0:T(8,128)(2,1)S(1)} collective-permute-done((bf16[832,256]{1,0:T(8,128)(2,1)S(1)}, bf16[832,256]{1,0:T(8,128)(2,1)S(1)}, u32[]{:S(2)}, u32[]{:S(2)}) %collective-permute-start.51) | collective-permute-done | bytes 426016 | tf_op jit(solution)/shard_map/ppermute | solution.py:24
  186.8 5.0 %collective-permute-done.52 = bf16[448,256]{1,0:T(8,128)(2,1)S(1)} collective-permute-done((bf16[448,256]{1,0:T(8,128)(2,1)S(1)}, bf16[448,256]{1,0:T(8,128)(2,1)S(1)}, u32[]{:S(2)}, u32[]{:S(2)}) %collective-permute-start.52) | collective-permute-done | bytes 229408 | tf_op jit(solution)/shard_map/ppermute | solution.py:24
  191.9 5.9 %collective-permute-start.56 = (f32[64,256]{1,0:T(8,128)S(1)}, f32[64,256]{1,0:T(8,128)S(1)}, u32[]{:S(2)}, u32[]{:S(2)}) collective-permute-start(f32[64,256]{1,0:T(8,128)S(1)} %get-tuple-element.34), channel_id=1, source_target_pairs={{0,8},{1,9},{2,10},{3,11},{4,12},{5,13},{6,14},{7,15},{8,0},{9,1},... | collective-permute-start | bytes 196616 | tf_op jit(solution)/shard_map/ppermute | solution.py:24
  197.9 5.9 %collective-permute-start.55 = (bf16[384,256]{1,0:T(8,128)(2,1)S(1)}, bf16[384,256]{1,0:T(8,128)(2,1)S(1)}, u32[]{:S(2)}, u32[]{:S(2)}) collective-permute-start(bf16[384,256]{1,0:T(8,128)(2,1)S(1)} %fusion.13), channel_id=1, source_target_pairs={{0,32},{32,0},{64,96},{96,64},{128,160},{160,128},{192,224},{224,1... | collective-permute-start | bytes 589832 | tf_op jit(solution)/shard_map/ppermute | solution.py:24
  206.5 12.4 %collective-permute-done.57 = f32[64,256]{1,0:T(8,128)S(1)} collective-permute-done((f32[64,256]{1,0:T(8,128)S(1)}, f32[64,256]{1,0:T(8,128)S(1)}, u32[]{:S(2)}, u32[]{:S(2)}) %collective-permute-start.57) | collective-permute-done | bytes 65568 | tf_op jit(solution)/shard_map/ppermute | solution.py:24
  (175 shorter events, 60.7 us)
Async XLA Ops:
  2.4 11.9 %collective-permute-start.4 = (bf16[384,256]{1,0:T(8,128)(2,1)S(1)}, bf16[384,256]{1,0:T(8,128)(2,1)S(1)}, u32[]{:S(2)}, u32[]{:S(2)}) collective-permute-start(bf16[384,256]{1,0:T(8,128)(2,1)S(1)} %fusion.9.rest_0_), channel_id=1, source_target_pairs={{0,32},{32,0},{64,96},{96,64},{128,160},{160,128},{192,224},{224,1... | collective-permute-start | bytes 589832 | tf_op jit(solution)/shard_map/ppermute | solution.py:24
  10.2 13.3 %collective-permute-start = (bf16[384,256]{1,0:T(8,128)(2,1)S(1)}, bf16[384,256]{1,0:T(8,128)(2,1)S(1)}, u32[]{:S(2)}, u32[]{:S(2)}) collective-permute-start(bf16[384,256]{1,0:T(8,128)(2,1)S(1)} %fusion.9.rest_0_), channel_id=1, source_target_pairs={{0,64},{32,96},{64,0},{96,32},{128,192},{160,224},{192,128},{224,1... | collective-permute-start | bytes 589832 | tf_op jit(solution)/shard_map/ppermute | solution.py:24
  11.5 12.9 %collective-permute-start.2 = (bf16[384,256]{1,0:T(8,128)(2,1)S(1)}, bf16[384,256]{1,0:T(8,128)(2,1)S(1)}, u32[]{:S(2)}, u32[]{:S(2)}) collective-permute-start(bf16[384,256]{1,0:T(8,128)(2,1)S(1)} %fusion.9.rest_0_), channel_id=1, source_target_pairs={{0,192},{32,224},{64,128},{96,160},{128,64},{160,96},{192,0},{224,... | collective-permute-start | bytes 589832 | tf_op jit(solution)/shard_map/ppermute | solution.py:24
  14.3 10.3 %collective-permute-start.5 = (bf16[384,256]{1,0:T(8,128)(2,1)S(1)}, bf16[384,256]{1,0:T(8,128)(2,1)S(1)}, u32[]{:S(2)}, u32[]{:S(2)}) collective-permute-start(bf16[384,256]{1,0:T(8,128)(2,1)S(1)} %collective-permute-done.4.rest_5_), channel_id=1, source_target_pairs={{0,64},{32,96},{64,0},{96,32},{128,192},{160,224},{192,128},{224,1... | collective-permute-start | bytes 589832 | tf_op jit(solution)/shard_map/ppermute | solution.py:24
  39.9 17.8 %collective-permute-start.17 = (bf16[32,128,256]{2,1,0:T(8,128)(2,1)S(1)}, bf16[32,128,256]{2,1,0:T(8,128)(2,1)S(1)}, u32[]{:S(2)}, u32[]{:S(2)}) collective-permute-start(bf16[32,128,256]{2,1,0:T(8,128)(2,1)S(1)} %forward2.1), channel_id=1, source_target_pairs={{0,1},{1,0},{2,3},{3,2},{4,5},{5,4},{6,7},{7,6},{8,9},{9,8},{10,11... | collective-permute-start | bytes 6291464 | tf_op jit(solution)/shard_map/ppermute | solution.py:24
  40.6 10.5 %collective-permute-start.13 = (bf16[2,2,128,256]{3,2,1,0:T(8,128)(2,1)S(1)}, bf16[2,2,128,256]{3,2,1,0:T(8,128)(2,1)S(1)}, u32[]{:S(2)}, u32[]{:S(2)}) collective-permute-start(bf16[2,2,128,256]{3,2,1,0:T(8,128)(2,1)S(1)} %get-tuple-element.43), channel_id=1, source_target_pairs={{0,6},{1,7},{2,4},{3,5},{4,2},{5,3},{6,0},{7,1},{8,14},{9,15},{10,... | collective-permute-start | bytes 786440 | tf_op jit(solution)/shard_map/ppermute | solution.py:24
  55.2 9.9 %collective-permute-start.11 = (bf16[2,128,256]{2,1,0:T(8,128)(2,1)S(1)}, bf16[2,128,256]{2,1,0:T(8,128)(2,1)S(1)}, u32[]{:S(2)}, u32[]{:S(2)}) collective-permute-start(bf16[2,128,256]{2,1,0:T(8,128)(2,1)S(1)} %get-tuple-element.42), channel_id=1, source_target_pairs={{0,6},{1,7},{2,4},{3,5},{4,2},{5,3},{6,0},{7,1},{8,14},{9,15},{10,... | collective-permute-start | bytes 393224 | tf_op jit(solution)/shard_map/ppermute | solution.py:24
  57.9 14.5 %collective-permute-start.20 = (bf16[2,2,256,256]{3,2,1,0:T(8,128)(2,1)S(1)}, bf16[2,2,256,256]{3,2,1,0:T(8,128)(2,1)S(1)}, u32[]{:S(2)}, u32[]{:S(2)}) collective-permute-start(bf16[2,2,256,256]{3,2,1,0:T(8,128)(2,1)S(1)} %get-tuple-element.23), channel_id=1, source_target_pairs={{0,6},{1,7},{2,4},{3,5},{4,2},{5,3},{6,0},{7,1},{8,14},{9,15},{10,... | collective-permute-start | bytes 1572872 | tf_op jit(solution)/shard_map/ppermute | solution.py:24
  58.4 14.3 %collective-permute-start.16 = (bf16[128,256]{1,0:T(8,128)(2,1)S(1)}, bf16[128,256]{1,0:T(8,128)(2,1)S(1)}, u32[]{:S(2)}, u32[]{:S(2)}) collective-permute-start(bf16[128,256]{1,0:T(8,128)(2,1)S(1)} %get-tuple-element.62), channel_id=1, source_target_pairs={{0,24},{1,25},{2,26},{3,27},{4,28},{5,29},{6,30},{7,31},{8,16},{9,... | collective-permute-start | bytes 196616 | tf_op jit(solution)/shard_map/ppermute | solution.py:24
  63.6 9.1 %collective-permute-start.15 = (bf16[128,256]{1,0:T(8,128)(2,1)S(1)}, bf16[128,256]{1,0:T(8,128)(2,1)S(1)}, u32[]{:S(2)}, u32[]{:S(2)}) collective-permute-start(bf16[128,256]{1,0:T(8,128)(2,1)S(1)} %get-tuple-element.61), channel_id=1, source_target_pairs={{0,16},{1,17},{2,18},{3,19},{4,20},{5,21},{6,22},{7,23},{8,24},{9,... | collective-permute-start | bytes 196616 | tf_op jit(solution)/shard_map/ppermute | solution.py:24
  65.5 10.2 %collective-permute-start.18 = (bf16[2,2,256,256]{3,2,1,0:T(8,128)(2,1)S(1)}, bf16[2,2,256,256]{3,2,1,0:T(8,128)(2,1)S(1)}, u32[]{:S(2)}, u32[]{:S(2)}) collective-permute-start(bf16[2,2,256,256]{3,2,1,0:T(8,128)(2,1)S(1)} %get-tuple-element.22), channel_id=1, source_target_pairs={{0,2},{1,3},{2,0},{3,1},{4,6},{5,7},{6,4},{7,5},{8,10},{9,11},{10,... | collective-permute-start | bytes 1572872 | tf_op jit(solution)/shard_map/ppermute | solution.py:24
  83.5 9.9 %collective-permute-start.27 = (bf16[128,256]{1,0:T(8,128)(2,1)S(1)}, bf16[128,256]{1,0:T(8,128)(2,1)S(1)}, u32[]{:S(2)}, u32[]{:S(2)}) collective-permute-start(bf16[128,256]{1,0:T(8,128)(2,1)S(1)} %fusion.1), channel_id=1, source_target_pairs={{0,24},{1,25},{2,26},{3,27},{4,28},{5,29},{6,30},{7,31},{8,16},{9,... | collective-permute-start | bytes 196616 | tf_op jit(solution)/shard_map/ppermute | solution.py:24
  93.4 12.7 %collective-permute-start.23 = (bf16[256,256]{1,0:T(8,128)(2,1)S(1)}, bf16[256,256]{1,0:T(8,128)(2,1)S(1)}, u32[]{:S(2)}, u32[]{:S(2)}) collective-permute-start(bf16[256,256]{1,0:T(8,128)(2,1)S(1)} %get-tuple-element.26), channel_id=1, source_target_pairs={{0,16},{1,17},{2,18},{3,19},{4,20},{5,21},{6,22},{7,23},{8,24},{9,... | collective-permute-start | bytes 393224 | tf_op jit(solution)/shard_map/ppermute | solution.py:24
  93.4 12.7 %collective-permute-start.22 = (bf16[256,256]{1,0:T(8,128)(2,1)S(1)}, bf16[256,256]{1,0:T(8,128)(2,1)S(1)}, u32[]{:S(2)}, u32[]{:S(2)}) collective-permute-start(bf16[256,256]{1,0:T(8,128)(2,1)S(1)} %fusion.25), channel_id=1, source_target_pairs={{0,8},{1,9},{2,10},{3,11},{4,12},{5,13},{6,14},{7,15},{8,0},{9,1},... | collective-permute-start | bytes 393224 | tf_op jit(solution)/shard_map/ppermute | solution.py:24
  93.9 13.6 %collective-permute-start.31 = (bf16[512,256]{1,0:T(8,128)(2,1)S(1)}, bf16[512,256]{1,0:T(8,128)(2,1)S(1)}, u32[]{:S(2)}, u32[]{:S(2)}) collective-permute-start(bf16[512,256]{1,0:T(8,128)(2,1)S(1)} %pad_maximum_fusion.2.rest_0_), channel_id=1, source_target_pairs={{0,2},{1,3},{2,0},{3,1},{4,6},{5,7},{6,4},{7,5},{8,10},{9,11},{10,... | collective-permute-start | bytes 786440 | tf_op jit(solution)/shard_map/ppermute | solution.py:24
  94.4 13.7 %collective-permute-start.33 = (bf16[512,256]{1,0:T(8,128)(2,1)S(1)}, bf16[512,256]{1,0:T(8,128)(2,1)S(1)}, u32[]{:S(2)}, u32[]{:S(2)}) collective-permute-start(bf16[512,256]{1,0:T(8,128)(2,1)S(1)} %pad_maximum_fusion.2.rest_0_), channel_id=1, source_target_pairs={{0,6},{1,7},{2,4},{3,5},{4,2},{5,3},{6,0},{7,1},{8,14},{9,15},{10,... | collective-permute-start | bytes 786440 | tf_op jit(solution)/shard_map/ppermute | solution.py:24
  107.5 13.1 %collective-permute-start.32 = (bf16[256,256]{1,0:T(8,128)(2,1)S(1)}, bf16[256,256]{1,0:T(8,128)(2,1)S(1)}, u32[]{:S(2)}, u32[]{:S(2)}) collective-permute-start(bf16[256,256]{1,0:T(8,128)(2,1)S(1)} %slice.389), channel_id=1, source_target_pairs={{0,6},{1,7},{2,4},{3,5},{4,2},{5,3},{6,0},{7,1},{8,14},{9,15},{10,... | collective-permute-start | bytes 393224 | tf_op jit(solution)/shard_map/ppermute | solution.py:24
  108.1 12.5 %collective-permute-start.34 = (bf16[256,256]{1,0:T(8,128)(2,1)S(1)}, bf16[256,256]{1,0:T(8,128)(2,1)S(1)}, u32[]{:S(2)}, u32[]{:S(2)}) collective-permute-start(bf16[256,256]{1,0:T(8,128)(2,1)S(1)} %slice.390), channel_id=1, source_target_pairs={{0,2},{1,3},{2,0},{3,1},{4,6},{5,7},{6,4},{7,5},{8,10},{9,11},{10,... | collective-permute-start | bytes 393224 | tf_op jit(solution)/shard_map/ppermute | solution.py:24
  110.7 9.8 %collective-permute-start.30 = (bf16[320,256]{1,0:T(8,128)(2,1)S(1)}, bf16[320,256]{1,0:T(8,128)(2,1)S(1)}, u32[]{:S(2)}, u32[]{:S(2)}) collective-permute-start(bf16[320,256]{1,0:T(8,128)(2,1)S(1)} %get-tuple-element.58), channel_id=1, source_target_pairs={{0,24},{1,25},{2,26},{3,27},{4,28},{5,29},{6,30},{7,31},{8,16},{9,... | collective-permute-start | bytes 491528 | tf_op jit(solution)/shard_map/ppermute | solution.py:24
  120.6 26.1 %collective-permute-start.35 = (bf16[1088,256]{1,0:T(8,128)(2,1)S(1)}, bf16[1088,256]{1,0:T(8,128)(2,1)S(1)}, u32[]{:S(2)}, u32[]{:S(2)}) collective-permute-start(bf16[1088,256]{1,0:T(8,128)(2,1)S(1)} %convert_dynamic-update-slice_fusion.rest_0_), channel_id=1, source_target_pairs={{0,2},{1,3},{2,0},{3,1},{4,6},{5,7},{6,4},{7,5},{8,10},{9,11},{10,... | collective-permute-start | bytes 1671176 | tf_op jit(solution)/shard_map/ppermute | solution.py:24
  122.9 23.8 %collective-permute-start.36 = (bf16[1088,256]{1,0:T(8,128)(2,1)S(1)}, bf16[1088,256]{1,0:T(8,128)(2,1)S(1)}, u32[]{:S(2)}, u32[]{:S(2)}) collective-permute-start(bf16[1088,256]{1,0:T(8,128)(2,1)S(1)} %convert_dynamic-update-slice_fusion.rest_0_), channel_id=1, source_target_pairs={{0,6},{1,7},{2,4},{3,5},{4,2},{5,3},{6,0},{7,1},{8,14},{9,15},{10,... | collective-permute-start | bytes 1671176 | tf_op jit(solution)/shard_map/ppermute | solution.py:24
  148.7 18.4 %collective-permute-start.44 = (bf16[1024,256]{1,0:T(8,128)(2,1)S(1)}, bf16[1024,256]{1,0:T(8,128)(2,1)S(1)}, u32[]{:S(2)}, u32[]{:S(2)}) collective-permute-start(bf16[1024,256]{1,0:T(8,128)(2,1)S(1)} %slice.321), channel_id=1, source_target_pairs={{0,1},{1,0},{2,3},{3,2},{4,5},{5,4},{6,7},{7,6},{8,9},{9,8},{10,11... | collective-permute-start | bytes 1572872 | tf_op jit(solution)/shard_map/ppermute | solution.py:24
  152.4 11.5 %collective-permute-start.43 = (bf16[512,256]{1,0:T(8,128)(2,1)S(1)}, bf16[512,256]{1,0:T(8,128)(2,1)S(1)}, u32[]{:S(2)}, u32[]{:S(2)}) collective-permute-start(bf16[512,256]{1,0:T(8,128)(2,1)S(1)} %slice.320), channel_id=1, source_target_pairs={{0,2},{1,3},{2,0},{3,1},{4,6},{5,7},{6,4},{7,5},{8,10},{9,11},{10,... | collective-permute-start | bytes 786440 | tf_op jit(solution)/shard_map/ppermute | solution.py:24
  152.5 14.7 %collective-permute-start.45 = (bf16[1024,256]{1,0:T(8,128)(2,1)S(1)}, bf16[1024,256]{1,0:T(8,128)(2,1)S(1)}, u32[]{:S(2)}, u32[]{:S(2)}) collective-permute-start(bf16[1024,256]{1,0:T(8,128)(2,1)S(1)} %slice.322), channel_id=1, source_target_pairs={{0,1},{1,0},{2,3},{3,2},{4,5},{5,4},{6,7},{7,6},{8,9},{9,8},{10,11... | collective-permute-start | bytes 1572872 | tf_op jit(solution)/shard_map/ppermute | solution.py:24
  152.6 14.6 %collective-permute-start.48 = (bf16[1024,256]{1,0:T(8,128)(2,1)S(1)}, bf16[1024,256]{1,0:T(8,128)(2,1)S(1)}, u32[]{:S(2)}, u32[]{:S(2)}) collective-permute-start(bf16[1024,256]{1,0:T(8,128)(2,1)S(1)} %slice.324), channel_id=1, source_target_pairs={{0,1},{1,0},{2,3},{3,2},{4,5},{5,4},{6,7},{7,6},{8,9},{9,8},{10,11... | collective-permute-start | bytes 1572872 | tf_op jit(solution)/shard_map/ppermute | solution.py:24
  172.4 12.3 %collective-permute-start.51 = (bf16[832,256]{1,0:T(8,128)(2,1)S(1)}, bf16[832,256]{1,0:T(8,128)(2,1)S(1)}, u32[]{:S(2)}, u32[]{:S(2)}) collective-permute-start(bf16[832,256]{1,0:T(8,128)(2,1)S(1)} %pad_maximum_fusion), channel_id=1, source_target_pairs={{0,64},{32,96},{64,0},{96,32},{128,192},{160,224},{192,128},{224,1... | collective-permute-start | bytes 1277960 | tf_op jit(solution)/shard_map/ppermute | solution.py:24
  175.8 10.8 %collective-permute-start.53 = (bf16[2,384,256]{2,1,0:T(8,128)(2,1)S(1)}, bf16[2,384,256]{2,1,0:T(8,128)(2,1)S(1)}, u32[]{:S(2)}, u32[]{:S(2)}) collective-permute-start(bf16[2,384,256]{2,1,0:T(8,128)(2,1)S(1)} %bitcast.157), channel_id=1, source_target_pairs={{0,192},{32,224},{64,128},{96,160},{128,64},{160,96},{192,0},{224,... | collective-permute-start | bytes 1179656 | tf_op jit(solution)/shard_map/ppermute | solution.py:24
  186.7 11.1 %collective-permute-start.54 = (bf16[384,256]{1,0:T(8,128)(2,1)S(1)}, bf16[384,256]{1,0:T(8,128)(2,1)S(1)}, u32[]{:S(2)}, u32[]{:S(2)}) collective-permute-start(bf16[384,256]{1,0:T(8,128)(2,1)S(1)} %fusion.11), channel_id=1, source_target_pairs={{0,64},{32,96},{64,0},{96,32},{128,192},{160,224},{192,128},{224,1... | collective-permute-start | bytes 589832 | tf_op jit(solution)/shard_map/ppermute | solution.py:24
  191.9 14.6 %collective-permute-start.56 = (f32[64,256]{1,0:T(8,128)S(1)}, f32[64,256]{1,0:T(8,128)S(1)}, u32[]{:S(2)}, u32[]{:S(2)}) collective-permute-start(f32[64,256]{1,0:T(8,128)S(1)} %get-tuple-element.34), channel_id=1, source_target_pairs={{0,8},{1,9},{2,10},{3,11},{4,12},{5,13},{6,14},{7,15},{8,0},{9,1},... | collective-permute-start | bytes 196616 | tf_op jit(solution)/shard_map/ppermute | solution.py:24
  197.9 21.8 %collective-permute-start.55 = (bf16[384,256]{1,0:T(8,128)(2,1)S(1)}, bf16[384,256]{1,0:T(8,128)(2,1)S(1)}, u32[]{:S(2)}, u32[]{:S(2)}) collective-permute-start(bf16[384,256]{1,0:T(8,128)(2,1)S(1)} %fusion.13), channel_id=1, source_target_pairs={{0,32},{32,0},{64,96},{96,64},{128,160},{160,128},{192,224},{224,1... | collective-permute-start | bytes 589832 | tf_op jit(solution)/shard_map/ppermute | solution.py:24
  203.8 15.1 %collective-permute-start.57 = (f32[64,256]{1,0:T(8,128)S(1)}, f32[64,256]{1,0:T(8,128)S(1)}, u32[]{:S(2)}, u32[]{:S(2)}) collective-permute-start(f32[64,256]{1,0:T(8,128)S(1)} %get-tuple-element.34), channel_id=1, source_target_pairs={{0,16},{1,17},{2,18},{3,19},{4,20},{5,21},{6,22},{7,23},{8,24},{9,... | collective-permute-start | bytes 196616 | tf_op jit(solution)/shard_map/ppermute | solution.py:24
  205.1 13.8 %collective-permute-start.58 = (f32[64,256]{1,0:T(8,128)S(1)}, f32[64,256]{1,0:T(8,128)S(1)}, u32[]{:S(2)}, u32[]{:S(2)}) collective-permute-start(f32[64,256]{1,0:T(8,128)S(1)} %get-tuple-element.34), channel_id=1, source_target_pairs={{0,24},{1,25},{2,26},{3,27},{4,28},{5,29},{6,30},{7,31},{8,16},{9,... | collective-permute-start | bytes 196616 | tf_op jit(solution)/shard_map/ppermute | solution.py:24
  (34 other events, 300.6 us)
where the time goes:
time: 225 us; the launch traced here: 221 us
  starting transfers between devices  109 us (48%)
  waiting for transfers between devices  79.3 us (35%)
  Pallas kernels  15.6 us (7%)
  local copies, waits for them, and re-layouts  6.89 us (3%)
  other arithmetic  5.96 us (3%)
    ppermute x59, starting transfers between devices, exchange(): return lax.ppermute(value, axis, [(i, i ^ mask) for i in range(size)])  109 us
    ppermute x59, waiting for transfers between devices, exchange(): return lax.ppermute(value, axis, [(i, i ^ mask) for i in range(size)])  79.3 us
    pallas_call x6, Pallas kernels, group_products(): pl.pallas_call(functools.partial(group_kernel, spans=spans, group=group,...  14.4 us
    unnamed x18, local copies, waits for them, and re-layouts  6.42 us
  transfers between devices with their start and end apart: 59, of which 25 were waited for; matrix products, arithmetic and copies ran while one was open for 2% of the time, Pallas kernels for 4%

commit v1 on v0

--- a/solution.py
+++ b/solution.py
@@ -34,10 +34,10 @@
     out, source = rest[-2:]
     slots, edge, _ = tiles.shape
     row = 0
-    for piece, span in zip(pieces, spans):
-
-        def move(i, _, piece=piece, row=row):
-            source[pl.ds(row + i * 64, 64)] = piece[pl.ds(i * 64, 64)]
+    for piece, (first, span) in zip(pieces, spans):
+
+        def move(i, _, piece=piece, row=row, first=first):
+            source[pl.ds(row + i * 64, 64)] = piece[pl.ds(first + i * 64, 64)]
             return 0
 
         lax.fori_loop(0, span // 64, move, 0)
@@ -81,8 +81,8 @@
 
 def group_products(table, tiles, pieces, count, group, flipped, previous=None, dtype=bf16):
     slots, edge, _ = tiles.shape
-    arrays = [array for array, _ in pieces]
-    spans = [span for _, span in pieces]
+    arrays = [array for array, _, _ in pieces]
+    spans = [(first, span) for _, first, span in pieces]
     width = arrays[0].shape[1]
     operands = [table, tiles] + arrays + ([] if previous is None else [previous])
     whole = pl.BlockSpec(memory_space=pltpu.VMEM)
@@ -97,8 +97,8 @@
         out_shape=jax.ShapeDtypeStruct((count, edge, width), dtype),
         in_specs=[pl.BlockSpec(memory_space=pltpu.SMEM)] + [whole] * (len(operands) - 1),
         out_specs=whole,
-        scratch_shapes=[pltpu.VMEM((sum(spans), width), bf16)],
-        compiler_params=pltpu.CompilerParams(vmem_limit_bytes=24 << 20),
+        scratch_shapes=[pltpu.VMEM((sum(span for _, span in spans), width), bf16)],
+        compiler_params=pltpu.CompilerParams(vmem_limit_bytes=8 << 20),
         cost_estimate=pl.CostEstimate(
             flops=2 * slots * edge * edge * width // 4,
             bytes_accessed=count * edge * width * 4,
@@ -185,15 +185,28 @@
     )(coords, place_info, tiles)
 
 
-def ring_gather(block, axis, bit, half, earlier=None):
-    near, far = 1 << bit, 3 << bit
-    first = exchange(block, axis, near)
-    third = exchange(block, axis, far)
-    if earlier is not None:
-        first, third = after((first, third), earlier)
-    second_low = exchange(first[:half], axis, far)
-    second_high = exchange(third[half:], axis, near)
-    return [block, first, second_low, second_high, third]
+def gather_row(block, table):
+    near, far = 1 << y_bit, 3 << y_bit
+    rows = block.shape[0]
+    half = rows // 2
+    across = exchange(block, "row", 1)
+    first, third = exchange(block, "row", near), exchange(block, "row", far)
+    first_across, third_across = exchange(across, "row", near), exchange(across, "row", far)
+    first_across, third_across = after((first_across, third_across), table)
+    low = exchange(jnp.concatenate([first[:half], first_across[:half]], axis=0), "row", far)
+    high = exchange(jnp.concatenate([third[half:], third_across[half:]], axis=0), "row", near)
+    return [
+        (block, 0, rows),
+        (first, 0, rows),
+        (low, 0, half),
+        (high, 0, half),
+        (third, 0, rows),
+        (across, 0, rows),
+        (first_across, 0, rows),
+        (low, half, half),
+        (high, half, half),
+        (third_across, 0, rows),
+    ]
 
 
 def wide(value):
@@ -206,17 +219,18 @@
     low, high = terms[0], terms[1]
 
     def send(value, mask):
-        message = jnp.concatenate([value.reshape(-1, width), share.astype(bf16)], axis=0)
+        rounded = share.astype(bf16)
+        message = jnp.concatenate([value.reshape(-1, width), rounded], axis=0)
         message = exchange(message, "row", mask)
         split = message.shape[0] - share.shape[0]
-        return message[:split].reshape(value.shape), share + wide(message[split:])
+        return message[:split].reshape(value.shape), wide(rounded) + wide(message[split:])
 
     high_in = exchange(high[2:4], "row", far)
     low_in, share = send(low[1:3], near)
     high_next = exchange((wide(high[1]) + wide(high_in[0])).astype(bf16), "row", near)
     low_next, share = send((wide(low[3]) + wide(low_in[1])).astype(bf16), far)
     leaving = (wide(high[0]) + wide(high_in[1]) + wide(high_next)).astype(bf16)
-    arrived = exchange(leaving, "row", 1)
+    arrived, share = send(leaving, 1)
     return wide(low[0]) + wide(low_in[0]) + wide(low_next) + wide(arrived), share
 
 
@@ -239,10 +253,7 @@
     forward_table, backward_table = slot_tables(
         tile_coords[0, 0], tile_count[0, 0], own_col, own_row, per_owner, tiles
     )
-    source = ring_gather(scaled, "row", y_bit, own_rows // 2)
-    across = exchange(scaled, "row", 1)
-    source += ring_gather(across, "row", y_bit, own_rows // 2, forward_table)
-    source = [(piece, piece.shape[0]) for piece in source]
+    source = gather_row(scaled, forward_table)
 
     near, far = 1 << x_bit, 3 << x_bit
     z = (own_col >> z_bit) & 3
@@ -270,21 +281,26 @@
         first_messages.append((sums(0, 1, 3).astype(bf16), sums(1, 2, 4).astype(bf16)))
     reduced = []
     second_messages = None
+    all_second = []
     for k in number:
         messages = first_messages[k]
         if k:
             messages = after(messages, second_messages)
         low_in = exchange(messages[0], "col", near)
         high_in = exchange(messages[1], "col", far)
+        low_in, high_in = lax.optimization_barrier((low_in, high_in))
         second_messages = (
             (both[k](0, 3, 4)[0] + wide(low_in[1])).astype(bf16),
             (both[k](1, 1, 2)[0] + wide(high_in[0])).astype(bf16),
         )
+        second_messages = lax.optimization_barrier(second_messages)
+        all_second.append(second_messages)
         low_next = exchange(second_messages[0], "col", far)
         high_next = exchange(second_messages[1], "col", near)
         low = both[k](0, 0, 1)[0] + wide(low_in[0]) + wide(low_next)
         high = both[k](1, 0, 1)[0] + wide(high_in[1]) + wide(high_next)
-        reduced.append((low[0], low[1].astype(bf16), high[0].astype(bf16), high[1].astype(bf16)))
+        blocks = (low[0], low[1].astype(bf16), high[0].astype(bf16), high[1].astype(bf16))
+        reduced.append(after(blocks, first_messages[k + 1 :]))
 
     hidden_parts = []
     local_weight = jnp.zeros((width, width), f32)
@@ -333,7 +349,7 @@
                 share = share + wide(message[rows:])
         if last:
             stack.append(share.astype(bf16))
-        stacks.append(jnp.concatenate(stack, axis=0))
+        stacks.append(after(jnp.concatenate(stack, axis=0), all_second[k + 1 :]))
 
     terms = None
     for k in number:
@@ -353,18 +369,35 @@
         second_low = exchange(low, "col", far)
         second_high = exchange(third[2 * rows : 4 * rows], "col", near)
         if last:
-            share = share + wide(first[4 * rows :]) + wide(third[4 * rows :])
-            share = share + wide(second_low[2 * rows :])
+            share = (wide(stack[4 * rows :]) + wide(first[4 * rows :])) + (
+                wide(second_low[2 * rows :]) + wide(third[4 * rows :])
+            )
+        blocks = [stack[: 4 * rows], first[: 4 * rows], third[: 4 * rows]]
+        seconds = [second_low[: 2 * rows], second_high]
         pieces = [
-            (stack, 4 * rows),
-            (first, 4 * rows),
-            (second_low, 2 * rows),
-            (second_high, 2 * rows),
-            (third, 4 * rows),
+            (stack, 0, 4 * rows),
+            (first, 0, 4 * rows),
+            (second_low, 0, 2 * rows),
+            (second_high, 0, 2 * rows),
+            (third, 0, 4 * rows),
         ]
 
-        def products(k, last=last, pieces=pieces, terms=terms):
-            arrived = [(exchange(piece[:span], "col", 1), span) for piece, span in pieces]
+        def products(
+            k, last=last, rows=rows, pieces=pieces, blocks=blocks, seconds=seconds, terms=terms
+        ):
+            if last:
+                main = exchange(jnp.concatenate(blocks, axis=0), "col", 1)
+                second, base = exchange(jnp.concatenate(seconds, axis=0), "col", 1), 0
+            else:
+                main = exchange(jnp.concatenate(blocks + seconds, axis=0), "col", 1)
+                second, base = main, 12 * rows
+            arrived = [
+                (main, 0, 4 * rows),
+                (main, 4 * rows, 4 * rows),
+                (second, base, 2 * rows),
+                (second, base + 2 * rows, 2 * rows),
+                (main, 8 * rows, 4 * rows),
+            ]
             return group_products(
                 backward_table,
                 tiles,
@@ -376,15 +409,15 @@
                 bf16 if last else f32,
             )
 
-    for axis, mask in (("col", 1), ("row", 1)):
-        share = share + exchange(share, axis, mask)
+    share = share + exchange(share, "col", 1)
     terms = products(len(chunks) - 1)
     source_total, share = reduce_row(terms.reshape(2, 4, own_rows, width), share)
+    share = share.astype(bf16)
     grad_weight = jnp.zeros((width, width), f32)
     for distance in (0, 1, 2, 3):
         piece = exchange(share, "col", distance << z_bit) if distance else share
         grad_weight = lax.dynamic_update_slice_in_dim(
-            grad_weight, piece, (z ^ distance) * share_rows, 0
+            grad_weight, wide(piece), (z ^ distance) * share_rows, 0
         )
     grad_weight = grad_weight / math.sqrt(total_nodes)
     decay = decay_rate * jnp.sqrt(out_degree.astype(f32))

time: 225 us -> 200 us (0.89)
  the two profiles are of different devices: /device:TPU:1 before, /device:TPU:2 now
where the time goes in v1:
time: 200 us; the launch traced here: 199 us
  starting transfers between devices  85.7 us (43%)
  waiting for transfers between devices  73.5 us (37%)
  Pallas kernels  18.9 us (9%)
  other arithmetic  8.21 us (4%)
  local copies, waits for them, and re-layouts  7.68 us (4%)
  matrix products  2.97 us (1%)
  between operations  2.1 us (1%)
    ppermute x49, starting transfers between devices, exchange(): return lax.ppermute(value, axis, [(i, i ^ mask) for i in range(size)])  85.7 us
    ppermute x49, waiting for transfers between devices, exchange(): return lax.ppermute(value, axis, [(i, i ^ mask) for i in range(size)])  73.5 us
    pallas_call x6, Pallas kernels, group_products(): pl.pallas_call(functools.partial(group_kernel, spans=spans, group=group,...  17.7 us
    unnamed x42, local copies, waits for them, and re-layouts  6.54 us
  transfers between devices with their start and end apart: 49, of which 27 were waited for; matrix products, arithmetic and copies ran while one was open for 5% of the time, Pallas kernels for 7%

profile of v1, /device:TPU:2, one launch (start us, length us, event | category | flops | bytes accessed | tf_op | source)
XLA Modules:
  0.0 199.1 jit_solution(9810034190134851860)
XLA Ops:
  2.4 7.3 %collective-permute-start.1 = (bf16[384,256]{1,0:T(8,128)(2,1)S(1)}, bf16[384,256]{1,0:T(8,128)(2,1)S(1)}, u32[]{:S(2)}, u32[]{:S(2)}) collective-permute-start(bf16[384,256]{1,0:T(8,128)(2,1)S(1)} %fusion.9.rest_0_), channel_id=1, source_target_pairs={{0,32},{32,0},{64,96},{96,64},{128,160},{160,128},{192,224},{224,1... | collective-permute-start | bytes 589832 | tf_op jit(solution)/shard_map/ppermute | solution.py:24
  9.7 3.0 %collective-permute-start.5 = (bf16[384,256]{1,0:T(8,128)(2,1)S(1)}, bf16[384,256]{1,0:T(8,128)(2,1)S(1)}, u32[]{:S(2)}, u32[]{:S(2)}) collective-permute-start(bf16[384,256]{1,0:T(8,128)(2,1)S(1)} %fusion.9.rest_0_), channel_id=1, source_target_pairs={{0,192},{32,224},{64,128},{96,160},{128,64},{160,96},{192,0},{224,... | collective-permute-start | bytes 589832 | tf_op jit(solution)/shard_map/ppermute | solution.py:24
  14.7 3.0 %collective-permute-start.3 = (bf16[384,256]{1,0:T(8,128)(2,1)S(1)}, bf16[384,256]{1,0:T(8,128)(2,1)S(1)}, u32[]{:S(2)}, u32[]{:S(2)}) collective-permute-start(bf16[384,256]{1,0:T(8,128)(2,1)S(1)} %collective-permute-done.1.rest_5_), channel_id=1, source_target_pairs={{0,192},{32,224},{64,128},{96,160},{128,64},{160,96},{192,0},{224,... | collective-permute-start | bytes 589832 | tf_op jit(solution)/shard_map/ppermute | solution.py:24
  19.4 2.8 %copy-done.1 = bf16[1,1,192,128,128]{4,3,2,1,0:T(8,128)(2,1)S(1)} copy-done((bf16[1,1,192,128,128]{4,3,2,1,0:T(8,128)(2,1)S(1)}, bf16[1,1,192,128,128]{4,3,2,1,0:T(8,128)(2,1)}, u32[]{:S(2)}) %copy-start.1) | copy-done | bytes 6291480
  25.8 3.5 %collective-permute-done.6.rest_3_.rest_8_ = bf16[384,256]{1,0:T(8,128)(2,1)S(1)} collective-permute-done((bf16[384,256]{1,0:T(8,128)(2,1)S(1)}, bf16[384,256]{1,0:T(8,128)(2,1)S(1)}, u32[]{:S(2)}, u32[]{:S(2)}) %collective-permute-start.6) | collective-permute-done | bytes 196640 | tf_op jit(solution)/shard_map/ppermute | solution.py:24
  29.3 3.2 %collective-permute-done.4.rest_2_.rest_7_ = bf16[384,256]{1,0:T(8,128)(2,1)S(1)} collective-permute-done((bf16[384,256]{1,0:T(8,128)(2,1)S(1)}, bf16[384,256]{1,0:T(8,128)(2,1)S(1)}, u32[]{:S(2)}, u32[]{:S(2)}) %collective-permute-start.4) | collective-permute-done | bytes 196640 | tf_op jit(solution)/shard_map/ppermute | solution.py:24
  37.2 3.2 %forward2.1 = bf16[32,128,256]{2,1,0:T(8,128)(2,1)S(1)} custom-call(s32[1,256]{1,0:T(1,128)S(1)} %get-tuple-element.42.table, bf16[192,128,128]{2,1,0:T(8,128)(2,1)S(1)} %bitcast.109, bf16[384,256]{1,0:T(8,128)(2,1)S(1)} %fusion.9.rest_0_, bf16[384,256]{1,0:T(8,128)(2,1)S(1)} %collective-permute-done.rest_1_, ...), custom_call_target="tpu_custom_call" | custom-call | flops 402653184 | bytes 4194304 | tf_op jit(solution)/shard_map/forward2/pallas_call | solution.py:89
  40.5 2.7 %collective-permute-start.9 = (bf16[2,2,128,256]{3,2,1,0:T(8,128)(2,1)S(1)}, bf16[2,2,128,256]{3,2,1,0:T(8,128)(2,1)S(1)}, u32[]{:S(2)}, u32[]{:S(2)}) collective-permute-start(bf16[2,2,128,256]{3,2,1,0:T(8,128)(2,1)S(1)} %get-tuple-element.79), channel_id=1, source_target_pairs={{0,6},{1,7},{2,4},{3,5},{4,2},{5,3},{6,0},{7,1},{8,14},{9,15},{10,... | collective-permute-start | bytes 786440 | tf_op jit(solution)/shard_map/ppermute | solution.py:24
  43.3 6.5 %collective-permute-done.9 = bf16[2,2,128,256]{3,2,1,0:T(8,128)(2,1)S(1)} collective-permute-done((bf16[2,2,128,256]{3,2,1,0:T(8,128)(2,1)S(1)}, bf16[2,2,128,256]{3,2,1,0:T(8,128)(2,1)S(1)}, u32[]{:S(2)}, u32[]{:S(2)}) %collective-permute-start.9) | collective-permute-done | bytes 262176 | tf_op jit(solution)/shard_map/ppermute | solution.py:24
  57.3 4.2 %collective-permute-start.13 = (bf16[128,256]{1,0:T(8,128)(2,1)S(1)}, bf16[128,256]{1,0:T(8,128)(2,1)S(1)}, u32[]{:S(2)}, u32[]{:S(2)}) collective-permute-start(bf16[128,256]{1,0:T(8,128)(2,1)S(1)} %fusion.26), channel_id=1, source_target_pairs={{0,8},{1,9},{2,10},{3,11},{4,12},{5,13},{6,14},{7,15},{8,0},{9,1},... | collective-permute-start | bytes 196616 | tf_op jit(solution)/shard_map/ppermute | solution.py:24
  61.4 3.3 %collective-permute-start.14 = (bf16[128,256]{1,0:T(8,128)(2,1)S(1)}, bf16[128,256]{1,0:T(8,128)(2,1)S(1)}, u32[]{:S(2)}, u32[]{:S(2)}) collective-permute-start(bf16[128,256]{1,0:T(8,128)(2,1)S(1)} %get-tuple-element.45), channel_id=1, source_target_pairs={{0,16},{1,17},{2,18},{3,19},{4,20},{5,21},{6,22},{7,23},{8,24},{9,... | collective-permute-start | bytes 196616 | tf_op jit(solution)/shard_map/ppermute | solution.py:24
  68.0 2.8 %collective-permute-done.15 = bf16[128,256]{1,0:T(8,128)(2,1)S(1)} collective-permute-done((bf16[128,256]{1,0:T(8,128)(2,1)S(1)}, bf16[128,256]{1,0:T(8,128)(2,1)S(1)}, u32[]{:S(2)}, u32[]{:S(2)}) %collective-permute-start.15) | collective-permute-done | bytes 65568 | tf_op jit(solution)/shard_map/ppermute | solution.py:24
  73.9 3.4 %collective-permute-start.23 = (bf16[128,256]{1,0:T(8,128)(2,1)S(1)}, bf16[128,256]{1,0:T(8,128)(2,1)S(1)}, u32[]{:S(2)}, u32[]{:S(2)}) collective-permute-start(bf16[128,256]{1,0:T(8,128)(2,1)S(1)} %fusion.1), channel_id=1, source_target_pairs={{0,8},{1,9},{2,10},{3,11},{4,12},{5,13},{6,14},{7,15},{8,0},{9,1},... | collective-permute-start | bytes 196616 | tf_op jit(solution)/shard_map/ppermute | solution.py:24
  82.6 2.4 %collective-permute-start.29 = (bf16[512,256]{1,0:T(8,128)(2,1)S(1)}, bf16[512,256]{1,0:T(8,128)(2,1)S(1)}, u32[]{:S(2)}, u32[]{:S(2)}) collective-permute-start(bf16[512,256]{1,0:T(8,128)(2,1)S(1)} %pad_maximum_fusion.4.rest_0_), channel_id=1, source_target_pairs={{0,2},{1,3},{2,0},{3,1},{4,6},{5,7},{6,4},{7,5},{8,10},{9,11},{10,... | collective-permute-start | bytes 786440 | tf_op jit(solution)/shard_map/ppermute | solution.py:24
  87.2 3.1 %collective-permute-done.31.rest_4_ = bf16[512,256]{1,0:T(8,128)(2,1)S(1)} collective-permute-done((bf16[512,256]{1,0:T(8,128)(2,1)S(1)}, bf16[512,256]{1,0:T(8,128)(2,1)S(1)}, u32[]{:S(2)}, u32[]{:S(2)}) %collective-permute-start.31) | collective-permute-done | bytes 262176 | tf_op jit(solution)/shard_map/ppermute | solution.py:24
  90.4 3.4 %collective-permute-start.32 = (bf16[256,256]{1,0:T(8,128)(2,1)S(1)}, bf16[256,256]{1,0:T(8,128)(2,1)S(1)}, u32[]{:S(2)}, u32[]{:S(2)}) collective-permute-start(bf16[256,256]{1,0:T(8,128)(2,1)S(1)} %slice.394), channel_id=1, source_target_pairs={{0,2},{1,3},{2,0},{3,1},{4,6},{5,7},{6,4},{7,5},{8,10},{9,11},{10,... | collective-permute-start | bytes 393224 | tf_op jit(solution)/shard_map/ppermute | solution.py:24
  98.1 3.1 %collective-permute-start.22 = (bf16[256,256]{1,0:T(8,128)(2,1)S(1)}, bf16[256,256]{1,0:T(8,128)(2,1)S(1)}, u32[]{:S(2)}, u32[]{:S(2)}) collective-permute-start(bf16[256,256]{1,0:T(8,128)(2,1)S(1)} %get-tuple-element.60), channel_id=1, source_target_pairs={{0,24},{1,25},{2,26},{3,27},{4,28},{5,29},{6,30},{7,31},{8,16},{9,... | collective-permute-start | bytes 393224 | tf_op jit(solution)/shard_map/ppermute | solution.py:24
  103.2 3.4 %collective-permute-done.22 = bf16[256,256]{1,0:T(8,128)(2,1)S(1)} collective-permute-done((bf16[256,256]{1,0:T(8,128)(2,1)S(1)}, bf16[256,256]{1,0:T(8,128)(2,1)S(1)}, u32[]{:S(2)}, u32[]{:S(2)}) %collective-permute-start.22) | collective-permute-done | bytes 131104 | tf_op jit(solution)/shard_map/ppermute | solution.py:24
  107.9 3.1 %collective-permute-start.28 = (bf16[320,256]{1,0:T(8,128)(2,1)S(1)}, bf16[320,256]{1,0:T(8,128)(2,1)S(1)}, u32[]{:S(2)}, u32[]{:S(2)}) collective-permute-start(bf16[320,256]{1,0:T(8,128)(2,1)S(1)} %get-tuple-element.94), channel_id=1, source_target_pairs={{0,24},{1,25},{2,26},{3,27},{4,28},{5,29},{6,30},{7,31},{8,16},{9,... | collective-permute-start | bytes 491528 | tf_op jit(solution)/shard_map/ppermute | solution.py:24
  111.0 4.3 %collective-permute-start.27 = (bf16[320,256]{1,0:T(8,128)(2,1)S(1)}, bf16[320,256]{1,0:T(8,128)(2,1)S(1)}, u32[]{:S(2)}, u32[]{:S(2)}) collective-permute-start(bf16[320,256]{1,0:T(8,128)(2,1)S(1)} %get-tuple-element.95), channel_id=1, source_target_pairs={{0,16},{1,17},{2,18},{3,19},{4,20},{5,21},{6,22},{7,23},{8,24},{9,... | collective-permute-start | bytes 491528 | tf_op jit(solution)/shard_map/ppermute | solution.py:24
  115.5 6.9 %collective-permute-done.26 = bf16[320,256]{1,0:T(8,128)(2,1)S(1)} collective-permute-done((bf16[320,256]{1,0:T(8,128)(2,1)S(1)}, bf16[320,256]{1,0:T(8,128)(2,1)S(1)}, u32[]{:S(2)}, u32[]{:S(2)}) %collective-permute-start.26) | collective-permute-done | bytes 163872 | tf_op jit(solution)/shard_map/ppermute | solution.py:24
  126.4 2.8 %copy-done.3 = bf16[1,1,192,128,128]{4,3,2,1,0:T(8,128)(2,1)S(1)} copy-done((bf16[1,1,192,128,128]{4,3,2,1,0:T(8,128)(2,1)S(1)}, bf16[1,1,192,128,128]{4,3,2,1,0:T(8,128)(2,1)}, u32[]{:S(2)}) %copy-start.3) | copy-done | bytes 6291480
  129.2 3.3 %backward0.1.rest_10_ = f32[24,128,256]{2,1,0:T(8,128)S(1)} custom-call(s32[1,256]{1,0:T(1,128)S(1)} %get-tuple-element.63.table, bf16[192,128,128]{2,1,0:T(8,128)(2,1)S(1)} %bitcast.111, bf16[512,256]{1,0:T(8,128)(2,1)S(1)} %pad_maximum_fusion.4.rest_0_, bf16[512,256]{1,0:T(8,128)(2,1)S(1)} %collective-permute-done.29.rest_1_, ...), custom_call_target="tpu_custom_call" | custom-call | flops 402653184 | bytes 3145728 | tf_op jit(solution)/shard_map/backward0/pallas_call | solution.py:89
  134.9 2.7 %collective-permute-start.37 = (bf16[512,256]{1,0:T(8,128)(2,1)S(1)}, bf16[512,256]{1,0:T(8,128)(2,1)S(1)}, u32[]{:S(2)}, u32[]{:S(2)}) collective-permute-start(bf16[512,256]{1,0:T(8,128)(2,1)S(1)} %slice.329), channel_id=1, source_target_pairs={{0,2},{1,3},{2,0},{3,1},{4,6},{5,7},{6,4},{7,5},{8,10},{9,11},{10,... | collective-permute-start | bytes 786440 | tf_op jit(solution)/shard_map/ppermute | solution.py:24
  137.7 6.0 %collective-permute-done.36.rest_2_ = bf16[576,256]{1,0:T(8,128)(2,1)S(1)} collective-permute-done((bf16[576,256]{1,0:T(8,128)(2,1)S(1)}, bf16[576,256]{1,0:T(8,128)(2,1)S(1)}, u32[]{:S(2)}, u32[]{:S(2)}) %collective-permute-start.36) | collective-permute-done | bytes 294944 | tf_op jit(solution)/shard_map/ppermute | solution.py:24
  146.4 5.0 %backward1.1 = bf16[24,128,256]{2,1,0:T(8,128)(2,1)S(1)} custom-call(s32[1,256]{1,0:T(1,128)S(1)} %get-tuple-element.63.table, bf16[192,128,128]{2,1,0:T(8,128)(2,1)S(1)} %bitcast.114, bf16[1088,256]{1,0:T(8,128)(2,1)S(1)} %fusion.27.rest_0_, bf16[1088,256]{1,0:T(8,128)(2,1)S(1)} %collective-permute-done.33.rest_1_, ...), custom_call_target="tpu_custom_call" | custom-call | flops 402653184 | bytes 3145728 | tf_op jit(solution)/shard_map/backward1/pallas_call | solution.py:89
  153.1 10.2 %collective-permute-done.43 = bf16[2,384,256]{2,1,0:T(8,128)(2,1)S(1)} collective-permute-done((bf16[2,384,256]{2,1,0:T(8,128)(2,1)S(1)}, bf16[2,384,256]{2,1,0:T(8,128)(2,1)S(1)}, u32[]{:S(2)}, u32[]{:S(2)}) %collective-permute-start.43) | collective-permute-done | bytes 393248 | tf_op jit(solution)/shard_map/ppermute | solution.py:24
  163.7 3.0 %collective-permute-start.42 = (bf16[448,256]{1,0:T(8,128)(2,1)S(1)}, bf16[448,256]{1,0:T(8,128)(2,1)S(1)}, u32[]{:S(2)}, u32[]{:S(2)}) collective-permute-start(bf16[448,256]{1,0:T(8,128)(2,1)S(1)} %pad_maximum_fusion.5), channel_id=1, source_target_pairs={{0,192},{32,224},{64,128},{96,160},{128,64},{160,96},{192,0},{224,... | collective-permute-start | bytes 688136 | tf_op jit(solution)/shard_map/ppermute | solution.py:24
  166.7 2.4 %collective-permute-done.44 = bf16[384,256]{1,0:T(8,128)(2,1)S(1)} collective-permute-done((bf16[384,256]{1,0:T(8,128)(2,1)S(1)}, bf16[384,256]{1,0:T(8,128)(2,1)S(1)}, u32[]{:S(2)}, u32[]{:S(2)}) %collective-permute-start.44) | collective-permute-done | bytes 196640 | tf_op jit(solution)/shard_map/ppermute | solution.py:24
  171.0 9.1 %collective-permute-start.45 = (bf16[448,256]{1,0:T(8,128)(2,1)S(1)}, bf16[448,256]{1,0:T(8,128)(2,1)S(1)}, u32[]{:S(2)}, u32[]{:S(2)}) collective-permute-start(bf16[448,256]{1,0:T(8,128)(2,1)S(1)} %pad_maximum_fusion.6), channel_id=1, source_target_pairs={{0,32},{32,0},{64,96},{96,64},{128,160},{160,128},{192,224},{224,1... | collective-permute-start | bytes 688136 | tf_op jit(solution)/shard_map/ppermute | solution.py:24
  180.8 6.7 %collective-permute-done.45 = bf16[448,256]{1,0:T(8,128)(2,1)S(1)} collective-permute-done((bf16[448,256]{1,0:T(8,128)(2,1)S(1)}, bf16[448,256]{1,0:T(8,128)(2,1)S(1)}, u32[]{:S(2)}, u32[]{:S(2)}) %collective-permute-start.45) | collective-permute-done | bytes 229408 | tf_op jit(solution)/shard_map/ppermute | solution.py:24
  187.6 5.1 %collective-permute-start.47 = (bf16[64,256]{1,0:T(8,128)(2,1)S(1)}, bf16[64,256]{1,0:T(8,128)(2,1)S(1)}, u32[]{:S(2)}, u32[]{:S(2)}) collective-permute-start(bf16[64,256]{1,0:T(8,128)(2,1)S(1)} %get-tuple-element.68), channel_id=1, source_target_pairs={{0,16},{1,17},{2,18},{3,19},{4,20},{5,21},{6,22},{7,23},{8,24},{9,... | collective-permute-start | bytes 98312 | tf_op jit(solution)/shard_map/ppermute | solution.py:24
  (184 shorter events, 62.2 us)
Async XLA Ops:
  2.4 12.3 %collective-permute-start.1 = (bf16[384,256]{1,0:T(8,128)(2,1)S(1)}, bf16[384,256]{1,0:T(8,128)(2,1)S(1)}, u32[]{:S(2)}, u32[]{:S(2)}) collective-permute-start(bf16[384,256]{1,0:T(8,128)(2,1)S(1)} %fusion.9.rest_0_), channel_id=1, source_target_pairs={{0,32},{32,0},{64,96},{96,64},{128,160},{160,128},{192,224},{224,1... | collective-permute-start | bytes 589832 | tf_op jit(solution)/shard_map/ppermute | solution.py:24
  9.7 13.7 %collective-permute-start.5 = (bf16[384,256]{1,0:T(8,128)(2,1)S(1)}, bf16[384,256]{1,0:T(8,128)(2,1)S(1)}, u32[]{:S(2)}, u32[]{:S(2)}) collective-permute-start(bf16[384,256]{1,0:T(8,128)(2,1)S(1)} %fusion.9.rest_0_), channel_id=1, source_target_pairs={{0,192},{32,224},{64,128},{96,160},{128,64},{160,96},{192,0},{224,... | collective-permute-start | bytes 589832 | tf_op jit(solution)/shard_map/ppermute | solution.py:24
  12.7 10.7 %collective-permute-start = (bf16[384,256]{1,0:T(8,128)(2,1)S(1)}, bf16[384,256]{1,0:T(8,128)(2,1)S(1)}, u32[]{:S(2)}, u32[]{:S(2)}) collective-permute-start(bf16[384,256]{1,0:T(8,128)(2,1)S(1)} %fusion.9.rest_0_), channel_id=1, source_target_pairs={{0,64},{32,96},{64,0},{96,32},{128,192},{160,224},{192,128},{224,1... | collective-permute-start | bytes 589832 | tf_op jit(solution)/shard_map/ppermute | solution.py:24
  14.7 8.7 %collective-permute-start.3 = (bf16[384,256]{1,0:T(8,128)(2,1)S(1)}, bf16[384,256]{1,0:T(8,128)(2,1)S(1)}, u32[]{:S(2)}, u32[]{:S(2)}) collective-permute-start(bf16[384,256]{1,0:T(8,128)(2,1)S(1)} %collective-permute-done.1.rest_5_), channel_id=1, source_target_pairs={{0,192},{32,224},{64,128},{96,160},{128,64},{160,96},{192,0},{224,... | collective-permute-start | bytes 589832 | tf_op jit(solution)/shard_map/ppermute | solution.py:24
  40.4 16.6 %collective-permute-start.12 = (bf16[32,128,256]{2,1,0:T(8,128)(2,1)S(1)}, bf16[32,128,256]{2,1,0:T(8,128)(2,1)S(1)}, u32[]{:S(2)}, u32[]{:S(2)}) collective-permute-start(bf16[32,128,256]{2,1,0:T(8,128)(2,1)S(1)} %forward2.1), channel_id=1, source_target_pairs={{0,1},{1,0},{2,3},{3,2},{4,5},{5,4},{6,7},{7,6},{8,9},{9,8},{10,11... | collective-permute-start | bytes 6291464 | tf_op jit(solution)/shard_map/ppermute | solution.py:24
  40.5 9.3 %collective-permute-start.9 = (bf16[2,2,128,256]{3,2,1,0:T(8,128)(2,1)S(1)}, bf16[2,2,128,256]{3,2,1,0:T(8,128)(2,1)S(1)}, u32[]{:S(2)}, u32[]{:S(2)}) collective-permute-start(bf16[2,2,128,256]{3,2,1,0:T(8,128)(2,1)S(1)} %get-tuple-element.79), channel_id=1, source_target_pairs={{0,6},{1,7},{2,4},{3,5},{4,2},{5,3},{6,0},{7,1},{8,14},{9,15},{10,... | collective-permute-start | bytes 786440 | tf_op jit(solution)/shard_map/ppermute | solution.py:24
  43.2 8.0 %collective-permute-start.8 = (bf16[2,2,128,256]{3,2,1,0:T(8,128)(2,1)S(1)}, bf16[2,2,128,256]{3,2,1,0:T(8,128)(2,1)S(1)}, u32[]{:S(2)}, u32[]{:S(2)}) collective-permute-start(bf16[2,2,128,256]{3,2,1,0:T(8,128)(2,1)S(1)} %get-tuple-element.80), channel_id=1, source_target_pairs={{0,2},{1,3},{2,0},{3,1},{4,6},{5,7},{6,4},{7,5},{8,10},{9,11},{10,... | collective-permute-start | bytes 786440 | tf_op jit(solution)/shard_map/ppermute | solution.py:24
  57.3 10.7 %collective-permute-start.13 = (bf16[128,256]{1,0:T(8,128)(2,1)S(1)}, bf16[128,256]{1,0:T(8,128)(2,1)S(1)}, u32[]{:S(2)}, u32[]{:S(2)}) collective-permute-start(bf16[128,256]{1,0:T(8,128)(2,1)S(1)} %fusion.26), channel_id=1, source_target_pairs={{0,8},{1,9},{2,10},{3,11},{4,12},{5,13},{6,14},{7,15},{8,0},{9,1},... | collective-permute-start | bytes 196616 | tf_op jit(solution)/shard_map/ppermute | solution.py:24
  65.3 15.1 %collective-permute-start.16 = (bf16[2,2,256,256]{3,2,1,0:T(8,128)(2,1)S(1)}, bf16[2,2,256,256]{3,2,1,0:T(8,128)(2,1)S(1)}, u32[]{:S(2)}, u32[]{:S(2)}) collective-permute-start(bf16[2,2,256,256]{3,2,1,0:T(8,128)(2,1)S(1)} %get-tuple-element.47), channel_id=1, source_target_pairs={{0,2},{1,3},{2,0},{3,1},{4,6},{5,7},{6,4},{7,5},{8,10},{9,11},{10,... | collective-permute-start | bytes 1572872 | tf_op jit(solution)/shard_map/ppermute | solution.py:24
  66.8 13.6 %collective-permute-start.17 = (bf16[2,2,256,256]{3,2,1,0:T(8,128)(2,1)S(1)}, bf16[2,2,256,256]{3,2,1,0:T(8,128)(2,1)S(1)}, u32[]{:S(2)}, u32[]{:S(2)}) collective-permute-start(bf16[2,2,256,256]{3,2,1,0:T(8,128)(2,1)S(1)} %get-tuple-element.48), channel_id=1, source_target_pairs={{0,6},{1,7},{2,4},{3,5},{4,2},{5,3},{6,0},{7,1},{8,14},{9,15},{10,... | collective-permute-start | bytes 1572872 | tf_op jit(solution)/shard_map/ppermute | solution.py:24
  81.5 8.9 %collective-permute-start.31 = (bf16[512,256]{1,0:T(8,128)(2,1)S(1)}, bf16[512,256]{1,0:T(8,128)(2,1)S(1)}, u32[]{:S(2)}, u32[]{:S(2)}) collective-permute-start(bf16[512,256]{1,0:T(8,128)(2,1)S(1)} %pad_maximum_fusion.4.rest_0_), channel_id=1, source_target_pairs={{0,6},{1,7},{2,4},{3,5},{4,2},{5,3},{6,0},{7,1},{8,14},{9,15},{10,... | collective-permute-start | bytes 786440 | tf_op jit(solution)/shard_map/ppermute | solution.py:24
  82.6 11.1 %collective-permute-start.29 = (bf16[512,256]{1,0:T(8,128)(2,1)S(1)}, bf16[512,256]{1,0:T(8,128)(2,1)S(1)}, u32[]{:S(2)}, u32[]{:S(2)}) collective-permute-start(bf16[512,256]{1,0:T(8,128)(2,1)S(1)} %pad_maximum_fusion.4.rest_0_), channel_id=1, source_target_pairs={{0,2},{1,3},{2,0},{3,1},{4,6},{5,7},{6,4},{7,5},{8,10},{9,11},{10,... | collective-permute-start | bytes 786440 | tf_op jit(solution)/shard_map/ppermute | solution.py:24
  85.0 10.1 %collective-permute-start.18 = (bf16[2,256,256]{2,1,0:T(8,128)(2,1)}, bf16[2,256,256]{2,1,0:T(8,128)(2,1)}, u32[]{:S(2)}, u32[]{:S(2)}) collective-permute-start(bf16[2,256,256]{2,1,0:T(8,128)(2,1)} %get-tuple-element.51), channel_id=1, source_target_pairs={{0,6},{1,7},{2,4},{3,5},{4,2},{5,3},{6,0},{7,1},{8,14},{9,15},{10,... | collective-permute-start | bytes 786440 | tf_op jit(solution)/shard_map/ppermute | solution.py:24
  85.9 9.3 %collective-permute-start.19 = (bf16[2,256,256]{2,1,0:T(8,128)(2,1)}, bf16[2,256,256]{2,1,0:T(8,128)(2,1)}, u32[]{:S(2)}, u32[]{:S(2)}) collective-permute-start(bf16[2,256,256]{2,1,0:T(8,128)(2,1)} %get-tuple-element.52), channel_id=1, source_target_pairs={{0,2},{1,3},{2,0},{3,1},{4,6},{5,7},{6,4},{7,5},{8,10},{9,11},{10,... | collective-permute-start | bytes 786440 | tf_op jit(solution)/shard_map/ppermute | solution.py:24
  90.4 25.0 %collective-permute-start.32 = (bf16[256,256]{1,0:T(8,128)(2,1)S(1)}, bf16[256,256]{1,0:T(8,128)(2,1)S(1)}, u32[]{:S(2)}, u32[]{:S(2)}) collective-permute-start(bf16[256,256]{1,0:T(8,128)(2,1)S(1)} %slice.394), channel_id=1, source_target_pairs={{0,2},{1,3},{2,0},{3,1},{4,6},{5,7},{6,4},{7,5},{8,10},{9,11},{10,... | collective-permute-start | bytes 393224 | tf_op jit(solution)/shard_map/ppermute | solution.py:24
  93.8 21.5 %collective-permute-start.30 = (bf16[256,256]{1,0:T(8,128)(2,1)S(1)}, bf16[256,256]{1,0:T(8,128)(2,1)S(1)}, u32[]{:S(2)}, u32[]{:S(2)}) collective-permute-start(bf16[256,256]{1,0:T(8,128)(2,1)S(1)} %slice.393), channel_id=1, source_target_pairs={{0,6},{1,7},{2,4},{3,5},{4,2},{5,3},{6,0},{7,1},{8,14},{9,15},{10,... | collective-permute-start | bytes 393224 | tf_op jit(solution)/shard_map/ppermute | solution.py:24
  98.1 8.5 %collective-permute-start.22 = (bf16[256,256]{1,0:T(8,128)(2,1)S(1)}, bf16[256,256]{1,0:T(8,128)(2,1)S(1)}, u32[]{:S(2)}, u32[]{:S(2)}) collective-permute-start(bf16[256,256]{1,0:T(8,128)(2,1)S(1)} %get-tuple-element.60), channel_id=1, source_target_pairs={{0,24},{1,25},{2,26},{3,27},{4,28},{5,29},{6,30},{7,31},{8,16},{9,... | collective-permute-start | bytes 393224 | tf_op jit(solution)/shard_map/ppermute | solution.py:24
  107.9 14.5 %collective-permute-start.28 = (bf16[320,256]{1,0:T(8,128)(2,1)S(1)}, bf16[320,256]{1,0:T(8,128)(2,1)S(1)}, u32[]{:S(2)}, u32[]{:S(2)}) collective-permute-start(bf16[320,256]{1,0:T(8,128)(2,1)S(1)} %get-tuple-element.94), channel_id=1, source_target_pairs={{0,24},{1,25},{2,26},{3,27},{4,28},{5,29},{6,30},{7,31},{8,16},{9,... | collective-permute-start | bytes 491528 | tf_op jit(solution)/shard_map/ppermute | solution.py:24
  111.0 11.4 %collective-permute-start.27 = (bf16[320,256]{1,0:T(8,128)(2,1)S(1)}, bf16[320,256]{1,0:T(8,128)(2,1)S(1)}, u32[]{:S(2)}, u32[]{:S(2)}) collective-permute-start(bf16[320,256]{1,0:T(8,128)(2,1)S(1)} %get-tuple-element.95), channel_id=1, source_target_pairs={{0,16},{1,17},{2,18},{3,19},{4,20},{5,21},{6,22},{7,23},{8,24},{9,... | collective-permute-start | bytes 491528 | tf_op jit(solution)/shard_map/ppermute | solution.py:24
  115.3 7.1 %collective-permute-start.26 = (bf16[320,256]{1,0:T(8,128)(2,1)S(1)}, bf16[320,256]{1,0:T(8,128)(2,1)S(1)}, u32[]{:S(2)}, u32[]{:S(2)}) collective-permute-start(bf16[320,256]{1,0:T(8,128)(2,1)S(1)} %get-tuple-element.96), channel_id=1, source_target_pairs={{0,8},{1,9},{2,10},{3,11},{4,12},{5,13},{6,14},{7,15},{8,0},{9,1},... | collective-permute-start | bytes 491528 | tf_op jit(solution)/shard_map/ppermute | solution.py:24
  115.4 11.0 %collective-permute-start.35 = (bf16[2048,256]{1,0:T(8,128)(2,1)S(1)}, bf16[2048,256]{1,0:T(8,128)(2,1)S(1)}, u32[]{:S(2)}, u32[]{:S(2)}) collective-permute-start(bf16[2048,256]{1,0:T(8,128)(2,1)S(1)} %constant_dynamic-update-slice_fusion.1), channel_id=1, source_target_pairs={{0,1},{1,0},{2,3},{3,2},{4,5},{5,4},{6,7},{7,6},{8,9},{9,8},{10,11... | collective-permute-start | bytes 3145736 | tf_op jit(solution)/shard_map/ppermute | solution.py:24
  122.5 10.0 %collective-permute-start.34 = (bf16[1088,256]{1,0:T(8,128)(2,1)S(1)}, bf16[1088,256]{1,0:T(8,128)(2,1)S(1)}, u32[]{:S(2)}, u32[]{:S(2)}) collective-permute-start(bf16[1088,256]{1,0:T(8,128)(2,1)S(1)} %fusion.27.rest_0_), channel_id=1, source_target_pairs={{0,6},{1,7},{2,4},{3,5},{4,2},{5,3},{6,0},{7,1},{8,14},{9,15},{10,... | collective-permute-start | bytes 1671176 | tf_op jit(solution)/shard_map/ppermute | solution.py:24
  124.0 9.8 %collective-permute-start.33 = (bf16[1088,256]{1,0:T(8,128)(2,1)S(1)}, bf16[1088,256]{1,0:T(8,128)(2,1)S(1)}, u32[]{:S(2)}, u32[]{:S(2)}) collective-permute-start(bf16[1088,256]{1,0:T(8,128)(2,1)S(1)} %fusion.27.rest_0_), channel_id=1, source_target_pairs={{0,2},{1,3},{2,0},{3,1},{4,6},{5,7},{6,4},{7,5},{8,10},{9,11},{10,... | collective-permute-start | bytes 1671176 | tf_op jit(solution)/shard_map/ppermute | solution.py:24
  134.1 12.3 %collective-permute-start.38 = (bf16[3072,256]{1,0:T(8,128)(2,1)S(1)}, bf16[3072,256]{1,0:T(8,128)(2,1)S(1)}, u32[]{:S(2)}, u32[]{:S(2)}) collective-permute-start(bf16[3072,256]{1,0:T(8,128)(2,1)S(1)} %pad_maximum_fusion), channel_id=1, source_target_pairs={{0,1},{1,0},{2,3},{3,2},{4,5},{5,4},{6,7},{7,6},{8,9},{9,8},{10,11... | collective-permute-start | bytes 4718600 | tf_op jit(solution)/shard_map/ppermute | solution.py:24
  134.2 9.5 %collective-permute-start.36 = (bf16[576,256]{1,0:T(8,128)(2,1)S(1)}, bf16[576,256]{1,0:T(8,128)(2,1)S(1)}, u32[]{:S(2)}, u32[]{:S(2)}) collective-permute-start(bf16[576,256]{1,0:T(8,128)(2,1)S(1)} %pad_maximum_fusion.3), channel_id=1, source_target_pairs={{0,6},{1,7},{2,4},{3,5},{4,2},{5,3},{6,0},{7,1},{8,14},{9,15},{10,... | collective-permute-start | bytes 884744 | tf_op jit(solution)/shard_map/ppermute | solution.py:24
  134.9 9.4 %collective-permute-start.37 = (bf16[512,256]{1,0:T(8,128)(2,1)S(1)}, bf16[512,256]{1,0:T(8,128)(2,1)S(1)}, u32[]{:S(2)}, u32[]{:S(2)}) collective-permute-start(bf16[512,256]{1,0:T(8,128)(2,1)S(1)} %slice.329), channel_id=1, source_target_pairs={{0,2},{1,3},{2,0},{3,1},{4,6},{5,7},{6,4},{7,5},{8,10},{9,11},{10,... | collective-permute-start | bytes 786440 | tf_op jit(solution)/shard_map/ppermute | solution.py:24
  144.5 8.4 %collective-permute-start.40 = (f32[64,256]{1,0:T(8,128)S(1)}, f32[64,256]{1,0:T(8,128)S(1)}, u32[]{:S(2)}, u32[]{:S(2)}) collective-permute-start(f32[64,256]{1,0:T(8,128)S(1)} %add_add_fusion), channel_id=1, source_target_pairs={{0,1},{1,0},{2,3},{3,2},{4,5},{5,4},{6,7},{7,6},{8,9},{9,8},{10,11... | collective-permute-start | bytes 196616 | tf_op jit(solution)/shard_map/ppermute | solution.py:24
  151.5 11.8 %collective-permute-start.43 = (bf16[2,384,256]{2,1,0:T(8,128)(2,1)S(1)}, bf16[2,384,256]{2,1,0:T(8,128)(2,1)S(1)}, u32[]{:S(2)}, u32[]{:S(2)}) collective-permute-start(bf16[2,384,256]{2,1,0:T(8,128)(2,1)S(1)} %bitcast.129), channel_id=1, source_target_pairs={{0,192},{32,224},{64,128},{96,160},{128,64},{160,96},{192,0},{224,... | collective-permute-start | bytes 1179656 | tf_op jit(solution)/shard_map/ppermute | solution.py:24
  152.9 10.6 %collective-permute-start.41 = (bf16[832,256]{1,0:T(8,128)(2,1)S(1)}, bf16[832,256]{1,0:T(8,128)(2,1)S(1)}, u32[]{:S(2)}, u32[]{:S(2)}) collective-permute-start(bf16[832,256]{1,0:T(8,128)(2,1)S(1)} %pad_maximum_fusion.2), channel_id=1, source_target_pairs={{0,64},{32,96},{64,0},{96,32},{128,192},{160,224},{192,128},{224,1... | collective-permute-start | bytes 1277960 | tf_op jit(solution)/shard_map/ppermute | solution.py:24
  163.7 7.3 %collective-permute-start.42 = (bf16[448,256]{1,0:T(8,128)(2,1)S(1)}, bf16[448,256]{1,0:T(8,128)(2,1)S(1)}, u32[]{:S(2)}, u32[]{:S(2)}) collective-permute-start(bf16[448,256]{1,0:T(8,128)(2,1)S(1)} %pad_maximum_fusion.5), channel_id=1, source_target_pairs={{0,192},{32,224},{64,128},{96,160},{128,64},{160,96},{192,0},{224,... | collective-permute-start | bytes 688136 | tf_op jit(solution)/shard_map/ppermute | solution.py:24
  171.0 16.5 %collective-permute-start.45 = (bf16[448,256]{1,0:T(8,128)(2,1)S(1)}, bf16[448,256]{1,0:T(8,128)(2,1)S(1)}, u32[]{:S(2)}, u32[]{:S(2)}) collective-permute-start(bf16[448,256]{1,0:T(8,128)(2,1)S(1)} %pad_maximum_fusion.6), channel_id=1, source_target_pairs={{0,32},{32,0},{64,96},{96,64},{128,160},{160,128},{192,224},{224,1... | collective-permute-start | bytes 688136 | tf_op jit(solution)/shard_map/ppermute | solution.py:24
  187.6 9.0 %collective-permute-start.47 = (bf16[64,256]{1,0:T(8,128)(2,1)S(1)}, bf16[64,256]{1,0:T(8,128)(2,1)S(1)}, u32[]{:S(2)}, u32[]{:S(2)}) collective-permute-start(bf16[64,256]{1,0:T(8,128)(2,1)S(1)} %get-tuple-element.68), channel_id=1, source_target_pairs={{0,16},{1,17},{2,18},{3,19},{4,20},{5,21},{6,22},{7,23},{8,24},{9,... | collective-permute-start | bytes 98312 | tf_op jit(solution)/shard_map/ppermute | solution.py:24
  (34 other events, 403.1 us)

commit v2 on v1

--- a/solution.py
+++ b/solution.py
@@ -185,17 +185,19 @@
     )(coords, place_info, tiles)
 
 
-def gather_row(block, table):
+def gather_row(block):
     near, far = 1 << y_bit, 3 << y_bit
     rows = block.shape[0]
     half = rows // 2
     across = exchange(block, "row", 1)
     first, third = exchange(block, "row", near), exchange(block, "row", far)
     first_across, third_across = exchange(across, "row", near), exchange(across, "row", far)
-    first_across, third_across = after((first_across, third_across), table)
-    low = exchange(jnp.concatenate([first[:half], first_across[:half]], axis=0), "row", far)
-    high = exchange(jnp.concatenate([third[half:], third_across[half:]], axis=0), "row", near)
-    return [
+    low = jnp.concatenate([first[:half], first_across[:half]], axis=0)
+    high = jnp.concatenate([third[half:], third_across[half:]], axis=0)
+    messages = lax.optimization_barrier((low, high))
+    low = exchange(messages[0], "row", far)
+    high = exchange(messages[1], "row", near)
+    return messages, [
         (block, 0, rows),
         (first, 0, rows),
         (low, 0, half),
@@ -250,10 +252,11 @@
     scale_out = lax.rsqrt(out_degree.astype(f32))
     scale_in = lax.rsqrt(in_degree.astype(f32))
     scaled = (scale_out[:, None] * wide(embedding)).astype(bf16)
+    messages, source = gather_row(scaled)
+    coords = after(tile_coords[0, 0], messages)
     forward_table, backward_table = slot_tables(
-        tile_coords[0, 0], tile_count[0, 0], own_col, own_row, per_owner, tiles
+        coords, tile_count[0, 0], own_col, own_row, per_owner, tiles
     )
-    source = gather_row(scaled, forward_table)
 
     near, far = 1 << x_bit, 3 << x_bit
     z = (own_col >> z_bit) & 3
@@ -337,12 +340,16 @@
             )
 
         stack = [upstream]
+        messages = (upstream,) * 3
         if last:
             share = weight_share(0)
-        for distance in (1, 2, 3):
-            message = upstream
-            if last:
-                message = jnp.concatenate([upstream, weight_share(distance).astype(bf16)], axis=0)
+            messages = lax.optimization_barrier(
+                tuple(
+                    jnp.concatenate([upstream, weight_share(d).astype(bf16)], axis=0)
+                    for d in (1, 2, 3)
+                )
+            )
+        for distance, message in zip((1, 2, 3), messages):
             message = exchange(message, "col", distance << z_bit)
             stack.append(message[:rows])
             if last:
@@ -360,6 +367,8 @@
             stack = after(stack, (second_low, second_high))
         first = exchange(stack, "col", near)
         third = exchange(stack, "col", far)
+        if not last:
+            first, third = after((first, third), messages)
         if k:
             terms = products(k - 1)
             first, third = after((first, third), terms)

time: 200 us -> 201 us (level)
  waiting for transfers between devices: 73.5 us -> 68.1 us
  Pallas kernels: 18.9 us -> 23.1 us
  local copies, waits for them, and re-layouts: 7.68 us -> 9.92 us
  starting transfers between devices: 85.7 us -> 87.9 us
    ppermute x49, waiting for transfers between devices: 73.5 us -> 68.1 us  [exchange(): return lax.ppermute(value, axis, [(i, i ^ mask) for i in range(size)])]
    pallas_call x6, Pallas kernels: 17.7 us -> 21.9 us  [group_products(): pl.pallas_call(functools.partial(group_kernel, spans=spans, group=group,...]
    ppermute x49, starting transfers between devices: 85.7 us -> 87.9 us  [exchange(): return lax.ppermute(value, axis, [(i, i ^ mask) for i in range(size)])]
    unnamed x42 -> x36, local copies, waits for them, and re-layouts: 6.54 us -> 8.31 us
  transfers between devices with their start and end apart: 49 -> 49, of which waited for: 27 -> 25; matrix products, arithmetic and copies ran while one was open for 5% -> 4% of each run, Pallas kernels for 7% -> 9%
where the time goes in v2:
time: 201 us; the launch traced here: 202 us
  starting transfers between devices  87.9 us (44%)
  waiting for transfers between devices  68.1 us (34%)
  Pallas kernels  23.1 us (11%)
  local copies, waits for them, and re-layouts  9.92 us (5%)
  other arithmetic  9.5 us (5%)
  between operations  2.02 us (1%)
    ppermute x49, starting transfers between devices, exchange(): return lax.ppermute(value, axis, [(i, i ^ mask) for i in range(size)])  87.9 us
    ppermute x49, waiting for transfers between devices, exchange(): return lax.ppermute(value, axis, [(i, i ^ mask) for i in range(size)])  68.1 us
    pallas_call x6, Pallas kernels, group_products(): pl.pallas_call(functools.partial(group_kernel, spans=spans, group=group,...  21.9 us
    unnamed x36, local copies, waits for them, and re-layouts  8.31 us
  transfers between devices with their start and end apart: 49, of which 25 were waited for; matrix products, arithmetic and copies ran while one was open for 4% of the time, Pallas kernels for 9%

profile of v2, /device:TPU:2, one launch (start us, length us, event | category | flops | bytes accessed | tf_op | source)
XLA Modules:
  0.0 202.0 jit_solution(18369951588259918992)
XLA Ops:
  2.4 7.3 %collective-permute-start.1 = (bf16[384,256]{1,0:T(8,128)(2,1)S(1)}, bf16[384,256]{1,0:T(8,128)(2,1)S(1)}, u32[]{:S(2)}, u32[]{:S(2)}) collective-permute-start(bf16[384,256]{1,0:T(8,128)(2,1)S(1)} %fusion.9.rest_0_), channel_id=1, source_target_pairs={{0,32},{32,0},{64,96},{96,64},{128,160},{160,128},{192,224},{224,1... | collective-permute-start | bytes 589832 | tf_op jit(solution)/shard_map/ppermute | solution.py:24
  9.7 3.0 %collective-permute-start.3 = (bf16[384,256]{1,0:T(8,128)(2,1)S(1)}, bf16[384,256]{1,0:T(8,128)(2,1)S(1)}, u32[]{:S(2)}, u32[]{:S(2)}) collective-permute-start(bf16[384,256]{1,0:T(8,128)(2,1)S(1)} %fusion.9.rest_0_), channel_id=1, source_target_pairs={{0,192},{32,224},{64,128},{96,160},{128,64},{160,96},{192,0},{224,... | collective-permute-start | bytes 589832 | tf_op jit(solution)/shard_map/ppermute | solution.py:24
  14.7 3.0 %collective-permute-start.4 = (bf16[384,256]{1,0:T(8,128)(2,1)S(1)}, bf16[384,256]{1,0:T(8,128)(2,1)S(1)}, u32[]{:S(2)}, u32[]{:S(2)}) collective-permute-start(bf16[384,256]{1,0:T(8,128)(2,1)S(1)} %collective-permute-done.1.rest_5_), channel_id=1, source_target_pairs={{0,192},{32,224},{64,128},{96,160},{128,64},{160,96},{192,0},{224,... | collective-permute-start | bytes 589832 | tf_op jit(solution)/shard_map/ppermute | solution.py:24
  18.8 3.2 %collective-permute-done.4.rest_9_ = bf16[384,256]{1,0:T(8,128)(2,1)S(1)} collective-permute-done((bf16[384,256]{1,0:T(8,128)(2,1)S(1)}, bf16[384,256]{1,0:T(8,128)(2,1)S(1)}, u32[]{:S(2)}, u32[]{:S(2)}) %collective-permute-start.4) | collective-permute-done | bytes 196640 | tf_op jit(solution)/shard_map/ppermute | solution.py:24
  26.6 2.8 %copy-done.1 = bf16[1,1,192,128,128]{4,3,2,1,0:T(8,128)(2,1)S(1)} copy-done((bf16[1,1,192,128,128]{4,3,2,1,0:T(8,128)(2,1)S(1)}, bf16[1,1,192,128,128]{4,3,2,1,0:T(8,128)(2,1)}, u32[]{:S(2)}) %copy-start.1) | copy-done | bytes 6291480
  34.5 2.5 %forward1.1 = bf16[16,128,256]{2,1,0:T(8,128)(2,1)S(1)} custom-call(s32[1,256]{1,0:T(1,128)S(1)} %get-tuple-element.49.table, bf16[192,128,128]{2,1,0:T(8,128)(2,1)S(1)} %bitcast.108, bf16[384,256]{1,0:T(8,128)(2,1)S(1)} %fusion.9.rest_0_, bf16[384,256]{1,0:T(8,128)(2,1)S(1)} %collective-permute-done.rest_1_, ...), custom_call_target="tpu_custom_call" | custom-call | flops 402653184 | bytes 2097152 | tf_op jit(solution)/shard_map/forward1/pallas_call | solution.py:89
  37.3 3.4 %forward2.1 = bf16[32,128,256]{2,1,0:T(8,128)(2,1)S(1)} custom-call(s32[1,256]{1,0:T(1,128)S(1)} %get-tuple-element.49.table, bf16[192,128,128]{2,1,0:T(8,128)(2,1)S(1)} %bitcast.109, bf16[384,256]{1,0:T(8,128)(2,1)S(1)} %fusion.9.rest_0_, bf16[384,256]{1,0:T(8,128)(2,1)S(1)} %collective-permute-done.rest_1_, ...), custom_call_target="tpu_custom_call" | custom-call | flops 402653184 | bytes 4194304 | tf_op jit(solution)/shard_map/forward2/pallas_call | solution.py:89
  43.3 6.2 %collective-permute-done.8 = bf16[2,2,128,256]{3,2,1,0:T(8,128)(2,1)S(1)} collective-permute-done((bf16[2,2,128,256]{3,2,1,0:T(8,128)(2,1)S(1)}, bf16[2,2,128,256]{3,2,1,0:T(8,128)(2,1)S(1)}, u32[]{:S(2)}, u32[]{:S(2)}) %collective-permute-start.8) | collective-permute-done | bytes 262176 | tf_op jit(solution)/shard_map/ppermute | solution.py:24
  51.8 3.2 %collective-permute-start.11 = (bf16[2,128,256]{2,1,0:T(8,128)(2,1)S(1)}, bf16[2,128,256]{2,1,0:T(8,128)(2,1)S(1)}, u32[]{:S(2)}, u32[]{:S(2)}) collective-permute-start(bf16[2,128,256]{2,1,0:T(8,128)(2,1)S(1)} %get-tuple-element.48), channel_id=1, source_target_pairs={{0,2},{1,3},{2,0},{3,1},{4,6},{5,7},{6,4},{7,5},{8,10},{9,11},{10,... | collective-permute-start | bytes 393224 | tf_op jit(solution)/shard_map/ppermute | solution.py:24
  56.9 3.1 %forward3.1 = bf16[32,128,256]{2,1,0:T(8,128)(2,1)S(1)} custom-call(s32[1,256]{1,0:T(1,128)S(1)} %get-tuple-element.49.table, bf16[192,128,128]{2,1,0:T(8,128)(2,1)S(1)} %bitcast.110, bf16[384,256]{1,0:T(8,128)(2,1)S(1)} %fusion.9.rest_0_, bf16[384,256]{1,0:T(8,128)(2,1)S(1)} %collective-permute-done.rest_1_, ...), custom_call_target="tpu_custom_call" | custom-call | flops 402653184 | bytes 4194304 | tf_op jit(solution)/shard_map/forward3/pallas_call | solution.py:89
  63.2 4.2 %collective-permute-start.13 = (bf16[128,256]{1,0:T(8,128)(2,1)S(1)}, bf16[128,256]{1,0:T(8,128)(2,1)}, u32[]{:S(2)}, u32[]{:S(2)}) collective-permute-start(bf16[128,256]{1,0:T(8,128)(2,1)S(1)} %fusion.26), channel_id=1, source_target_pairs={{0,8},{1,9},{2,10},{3,11},{4,12},{5,13},{6,14},{7,15},{8,0},{9,1},... | collective-permute-start | bytes 196616 | tf_op jit(solution)/shard_map/ppermute | solution.py:24
  70.6 3.5 %collective-permute-done.14 = bf16[128,256]{1,0:T(8,128)(2,1)} collective-permute-done((bf16[128,256]{1,0:T(8,128)(2,1)}, bf16[128,256]{1,0:T(8,128)(2,1)}, u32[]{:S(2)}, u32[]{:S(2)}) %collective-permute-start.14) | collective-permute-done | bytes 65568 | tf_op jit(solution)/shard_map/ppermute | solution.py:24
  78.4 2.8 %collective-permute-start.19 = (bf16[2,256,256]{2,1,0:T(8,128)(2,1)S(1)}, bf16[2,256,256]{2,1,0:T(8,128)(2,1)S(1)}, u32[]{:S(2)}, u32[]{:S(2)}) collective-permute-start(bf16[2,256,256]{2,1,0:T(8,128)(2,1)S(1)} %get-tuple-element.59), channel_id=1, source_target_pairs={{0,2},{1,3},{2,0},{3,1},{4,6},{5,7},{6,4},{7,5},{8,10},{9,11},{10,... | collective-permute-start | bytes 786440 | tf_op jit(solution)/shard_map/ppermute | solution.py:24
  81.6 2.8 %collective-permute-start.23 = (bf16[128,256]{1,0:T(8,128)(2,1)S(1)}, bf16[128,256]{1,0:T(8,128)(2,1)S(1)}, u32[]{:S(2)}, u32[]{:S(2)}) collective-permute-start(bf16[128,256]{1,0:T(8,128)(2,1)S(1)} %fusion.1), channel_id=1, source_target_pairs={{0,8},{1,9},{2,10},{3,11},{4,12},{5,13},{6,14},{7,15},{8,0},{9,1},... | collective-permute-start | bytes 196616 | tf_op jit(solution)/shard_map/ppermute | solution.py:24
  84.4 2.2 %collective-permute-start.24 = (bf16[128,256]{1,0:T(8,128)(2,1)S(1)}, bf16[128,256]{1,0:T(8,128)(2,1)S(1)}, u32[]{:S(2)}, u32[]{:S(2)}) collective-permute-start(bf16[128,256]{1,0:T(8,128)(2,1)S(1)} %fusion.1), channel_id=1, source_target_pairs={{0,16},{1,17},{2,18},{3,19},{4,20},{5,21},{6,22},{7,23},{8,24},{9,... | collective-permute-start | bytes 196616 | tf_op jit(solution)/shard_map/ppermute | solution.py:24
  90.9 2.2 %collective-permute-start.21 = (bf16[256,256]{1,0:T(8,128)(2,1)S(1)}, bf16[256,256]{1,0:T(8,128)(2,1)S(1)}, u32[]{:S(2)}, u32[]{:S(2)}) collective-permute-start(bf16[256,256]{1,0:T(8,128)(2,1)S(1)} %get-tuple-element.66), channel_id=1, source_target_pairs={{0,16},{1,17},{2,18},{3,19},{4,20},{5,21},{6,22},{7,23},{8,24},{9,... | collective-permute-start | bytes 393224 | tf_op jit(solution)/shard_map/ppermute | solution.py:24
  97.5 5.6 %collective-permute-done.21 = bf16[256,256]{1,0:T(8,128)(2,1)S(1)} collective-permute-done((bf16[256,256]{1,0:T(8,128)(2,1)S(1)}, bf16[256,256]{1,0:T(8,128)(2,1)S(1)}, u32[]{:S(2)}, u32[]{:S(2)}) %collective-permute-start.21) | collective-permute-done | bytes 131104 | tf_op jit(solution)/shard_map/ppermute | solution.py:24
  110.2 2.3 %collective-permute-start.32 = (bf16[256,256]{1,0:T(8,128)(2,1)S(1)}, bf16[256,256]{1,0:T(8,128)(2,1)S(1)}, u32[]{:S(2)}, u32[]{:S(2)}) collective-permute-start(bf16[256,256]{1,0:T(8,128)(2,1)S(1)} %slice.326), channel_id=1, source_target_pairs={{0,2},{1,3},{2,0},{3,1},{4,6},{5,7},{6,4},{7,5},{8,10},{9,11},{10,... | collective-permute-start | bytes 393224 | tf_op jit(solution)/shard_map/ppermute | solution.py:24
  115.6 5.0 %collective-permute-done.27 = bf16[320,256]{1,0:T(8,128)(2,1)S(1)} collective-permute-done((bf16[320,256]{1,0:T(8,128)(2,1)S(1)}, bf16[320,256]{1,0:T(8,128)(2,1)S(1)}, u32[]{:S(2)}, u32[]{:S(2)}) %collective-permute-start.27) | collective-permute-done | bytes 163872 | tf_op jit(solution)/shard_map/ppermute | solution.py:24
  123.9 4.0 %backward0.1.rest_10_ = f32[24,128,256]{2,1,0:T(8,128)S(1)} custom-call(s32[1,256]{1,0:T(1,128)S(1)} %get-tuple-element.70.table, bf16[192,128,128]{2,1,0:T(8,128)(2,1)S(1)} %bitcast.113, bf16[512,256]{1,0:T(8,128)(2,1)S(1)} %pad_maximum_fusion.4.rest_0_, bf16[512,256]{1,0:T(8,128)(2,1)S(1)} %collective-permute-done.29.rest_1_, ...), custom_call_target="tpu_custom_call" | custom-call | flops 402653184 | bytes 3145728 | tf_op jit(solution)/shard_map/backward0/pallas_call | solution.py:89
  127.9 3.5 %collective-permute-done.33.rest_1_ = bf16[1088,256]{1,0:T(8,128)(2,1)S(1)} collective-permute-done((bf16[1088,256]{1,0:T(8,128)(2,1)S(1)}, bf16[1088,256]{1,0:T(8,128)(2,1)S(1)}, u32[]{:S(2)}, u32[]{:S(2)}) %collective-permute-start.33) | collective-permute-done | bytes 557088 | tf_op jit(solution)/shard_map/ppermute | solution.py:24
  135.6 2.8 %collective-permute-start.37 = (bf16[512,256]{1,0:T(8,128)(2,1)S(1)}, bf16[512,256]{1,0:T(8,128)(2,1)S(1)}, u32[]{:S(2)}, u32[]{:S(2)}) collective-permute-start(bf16[512,256]{1,0:T(8,128)(2,1)S(1)} %slice.329), channel_id=1, source_target_pairs={{0,2},{1,3},{2,0},{3,1},{4,6},{5,7},{6,4},{7,5},{8,10},{9,11},{10,... | collective-permute-start | bytes 786440 | tf_op jit(solution)/shard_map/ppermute | solution.py:24
  138.3 4.9 %collective-permute-done.36.rest_2_ = bf16[576,256]{1,0:T(8,128)(2,1)S(1)} collective-permute-done((bf16[576,256]{1,0:T(8,128)(2,1)S(1)}, bf16[576,256]{1,0:T(8,128)(2,1)S(1)}, u32[]{:S(2)}, u32[]{:S(2)}) %collective-permute-start.36) | collective-permute-done | bytes 294944 | tf_op jit(solution)/shard_map/ppermute | solution.py:24
  147.1 6.7 %backward1.1 = bf16[24,128,256]{2,1,0:T(8,128)(2,1)S(1)} custom-call(s32[1,256]{1,0:T(1,128)S(1)} %get-tuple-element.70.table, bf16[192,128,128]{2,1,0:T(8,128)(2,1)S(1)} %bitcast.114, bf16[1088,256]{1,0:T(8,128)(2,1)S(1)} %fusion.27.rest_0_, bf16[1088,256]{1,0:T(8,128)(2,1)S(1)} %collective-permute-done.33.rest_1_, ...), custom_call_target="tpu_custom_call" | custom-call | flops 402653184 | bytes 3145728 | tf_op jit(solution)/shard_map/backward1/pallas_call | solution.py:89
  154.4 10.6 %collective-permute-done.43 = bf16[2,384,256]{2,1,0:T(8,128)(2,1)S(1)} collective-permute-done((bf16[2,384,256]{2,1,0:T(8,128)(2,1)S(1)}, bf16[2,384,256]{2,1,0:T(8,128)(2,1)S(1)}, u32[]{:S(2)}, u32[]{:S(2)}) %collective-permute-start.43) | collective-permute-done | bytes 393248 | tf_op jit(solution)/shard_map/ppermute | solution.py:24
  165.2 4.0 %collective-permute-start.42 = (bf16[448,256]{1,0:T(8,128)(2,1)S(1)}, bf16[448,256]{1,0:T(8,128)(2,1)S(1)}, u32[]{:S(2)}, u32[]{:S(2)}) collective-permute-start(bf16[448,256]{1,0:T(8,128)(2,1)S(1)} %pad_maximum_fusion.5), channel_id=1, source_target_pairs={{0,192},{32,224},{64,128},{96,160},{128,64},{160,96},{192,0},{224,... | collective-permute-start | bytes 688136 | tf_op jit(solution)/shard_map/ppermute | solution.py:24
  170.9 2.4 %collective-permute-done.42 = bf16[448,256]{1,0:T(8,128)(2,1)S(1)} collective-permute-done((bf16[448,256]{1,0:T(8,128)(2,1)S(1)}, bf16[448,256]{1,0:T(8,128)(2,1)S(1)}, u32[]{:S(2)}, u32[]{:S(2)}) %collective-permute-start.42) | collective-permute-done | bytes 229408 | tf_op jit(solution)/shard_map/ppermute | solution.py:24
  173.3 6.9 %collective-permute-start.45 = (bf16[448,256]{1,0:T(8,128)(2,1)S(1)}, bf16[448,256]{1,0:T(8,128)(2,1)S(1)}, u32[]{:S(2)}, u32[]{:S(2)}) collective-permute-start(bf16[448,256]{1,0:T(8,128)(2,1)S(1)} %pad_maximum_fusion.6), channel_id=1, source_target_pairs={{0,32},{32,0},{64,96},{96,64},{128,160},{160,128},{192,224},{224,1... | collective-permute-start | bytes 688136 | tf_op jit(solution)/shard_map/ppermute | solution.py:24
  180.9 3.3 %collective-permute-done.45 = bf16[448,256]{1,0:T(8,128)(2,1)S(1)} collective-permute-done((bf16[448,256]{1,0:T(8,128)(2,1)S(1)}, bf16[448,256]{1,0:T(8,128)(2,1)S(1)}, u32[]{:S(2)}, u32[]{:S(2)}) %collective-permute-start.45) | collective-permute-done | bytes 229408 | tf_op jit(solution)/shard_map/ppermute | solution.py:24
  184.2 8.6 %collective-permute-start.46 = (bf16[64,256]{1,0:T(8,128)(2,1)S(1)}, bf16[64,256]{1,0:T(8,128)(2,1)S(1)}, u32[]{:S(2)}, u32[]{:S(2)}) collective-permute-start(bf16[64,256]{1,0:T(8,128)(2,1)S(1)} %get-tuple-element.80), channel_id=1, source_target_pairs={{0,8},{1,9},{2,10},{3,11},{4,12},{5,13},{6,14},{7,15},{8,0},{9,1},... | collective-permute-start | bytes 98312 | tf_op jit(solution)/shard_map/ppermute | solution.py:24
  192.9 2.7 %collective-permute-start.47 = (bf16[64,256]{1,0:T(8,128)(2,1)S(1)}, bf16[64,256]{1,0:T(8,128)(2,1)S(1)}, u32[]{:S(2)}, u32[]{:S(2)}) collective-permute-start(bf16[64,256]{1,0:T(8,128)(2,1)S(1)} %get-tuple-element.80), channel_id=1, source_target_pairs={{0,16},{1,17},{2,18},{3,19},{4,20},{5,21},{6,22},{7,23},{8,24},{9,... | collective-permute-start | bytes 98312 | tf_op jit(solution)/shard_map/ppermute | solution.py:24
  197.7 3.5 %collective-permute-done.48 = bf16[64,256]{1,0:T(8,128)(2,1)S(1)} collective-permute-done((bf16[64,256]{1,0:T(8,128)(2,1)S(1)}, bf16[64,256]{1,0:T(8,128)(2,1)S(1)}, u32[]{:S(2)}, u32[]{:S(2)}) %collective-permute-start.48) | collective-permute-done | bytes 32800 | tf_op jit(solution)/shard_map/ppermute | solution.py:24
  (178 shorter events, 67.8 us)
Async XLA Ops:
  2.4 12.3 %collective-permute-start.1 = (bf16[384,256]{1,0:T(8,128)(2,1)S(1)}, bf16[384,256]{1,0:T(8,128)(2,1)S(1)}, u32[]{:S(2)}, u32[]{:S(2)}) collective-permute-start(bf16[384,256]{1,0:T(8,128)(2,1)S(1)} %fusion.9.rest_0_), channel_id=1, source_target_pairs={{0,32},{32,0},{64,96},{96,64},{128,160},{160,128},{192,224},{224,1... | collective-permute-start | bytes 589832 | tf_op jit(solution)/shard_map/ppermute | solution.py:24
  9.7 8.2 %collective-permute-start.3 = (bf16[384,256]{1,0:T(8,128)(2,1)S(1)}, bf16[384,256]{1,0:T(8,128)(2,1)S(1)}, u32[]{:S(2)}, u32[]{:S(2)}) collective-permute-start(bf16[384,256]{1,0:T(8,128)(2,1)S(1)} %fusion.9.rest_0_), channel_id=1, source_target_pairs={{0,192},{32,224},{64,128},{96,160},{128,64},{160,96},{192,0},{224,... | collective-permute-start | bytes 589832 | tf_op jit(solution)/shard_map/ppermute | solution.py:24
  40.7 19.6 %collective-permute-start.12 = (bf16[32,128,256]{2,1,0:T(8,128)(2,1)S(1)}, bf16[32,128,256]{2,1,0:T(8,128)(2,1)S(1)}, u32[]{:S(2)}, u32[]{:S(2)}) collective-permute-start(bf16[32,128,256]{2,1,0:T(8,128)(2,1)S(1)} %forward2.1), channel_id=1, source_target_pairs={{0,1},{1,0},{2,3},{3,2},{4,5},{5,4},{6,7},{7,6},{8,9},{9,8},{10,11... | collective-permute-start | bytes 6291464 | tf_op jit(solution)/shard_map/ppermute | solution.py:24
  40.8 8.7 %collective-permute-start.8 = (bf16[2,2,128,256]{3,2,1,0:T(8,128)(2,1)S(1)}, bf16[2,2,128,256]{3,2,1,0:T(8,128)(2,1)S(1)}, u32[]{:S(2)}, u32[]{:S(2)}) collective-permute-start(bf16[2,2,128,256]{3,2,1,0:T(8,128)(2,1)S(1)} %get-tuple-element.92), channel_id=1, source_target_pairs={{0,2},{1,3},{2,0},{3,1},{4,6},{5,7},{6,4},{7,5},{8,10},{9,11},{10,... | collective-permute-start | bytes 786440 | tf_op jit(solution)/shard_map/ppermute | solution.py:24
  41.4 8.5 %collective-permute-start.9 = (bf16[2,2,128,256]{3,2,1,0:T(8,128)(2,1)S(1)}, bf16[2,2,128,256]{3,2,1,0:T(8,128)(2,1)S(1)}, u32[]{:S(2)}, u32[]{:S(2)}) collective-permute-start(bf16[2,2,128,256]{3,2,1,0:T(8,128)(2,1)S(1)} %get-tuple-element.91), channel_id=1, source_target_pairs={{0,6},{1,7},{2,4},{3,5},{4,2},{5,3},{6,0},{7,1},{8,14},{9,15},{10,... | collective-permute-start | bytes 786440 | tf_op jit(solution)/shard_map/ppermute | solution.py:24
  50.0 10.1 %collective-permute-start.10 = (bf16[2,128,256]{2,1,0:T(8,128)(2,1)S(1)}, bf16[2,128,256]{2,1,0:T(8,128)(2,1)S(1)}, u32[]{:S(2)}, u32[]{:S(2)}) collective-permute-start(bf16[2,128,256]{2,1,0:T(8,128)(2,1)S(1)} %get-tuple-element.47), channel_id=1, source_target_pairs={{0,6},{1,7},{2,4},{3,5},{4,2},{5,3},{6,0},{7,1},{8,14},{9,15},{10,... | collective-permute-start | bytes 393224 | tf_op jit(solution)/shard_map/ppermute | solution.py:24
  51.8 8.3 %collective-permute-start.11 = (bf16[2,128,256]{2,1,0:T(8,128)(2,1)S(1)}, bf16[2,128,256]{2,1,0:T(8,128)(2,1)S(1)}, u32[]{:S(2)}, u32[]{:S(2)}) collective-permute-start(bf16[2,128,256]{2,1,0:T(8,128)(2,1)S(1)} %get-tuple-element.48), channel_id=1, source_target_pairs={{0,2},{1,3},{2,0},{3,1},{4,6},{5,7},{6,4},{7,5},{8,10},{9,11},{10,... | collective-permute-start | bytes 393224 | tf_op jit(solution)/shard_map/ppermute | solution.py:24
  61.9 13.9 %collective-permute-start.16 = (bf16[2,2,256,256]{3,2,1,0:T(8,128)(2,1)S(1)}, bf16[2,2,256,256]{3,2,1,0:T(8,128)(2,1)}, u32[]{:S(2)}, u32[]{:S(2)}) collective-permute-start(bf16[2,2,256,256]{3,2,1,0:T(8,128)(2,1)S(1)} %get-tuple-element.54), channel_id=1, source_target_pairs={{0,2},{1,3},{2,0},{3,1},{4,6},{5,7},{6,4},{7,5},{8,10},{9,11},{10,... | collective-permute-start | bytes 1572872 | tf_op jit(solution)/shard_map/ppermute | solution.py:24
  62.0 13.8 %collective-permute-start.17 = (bf16[2,2,256,256]{3,2,1,0:T(8,128)(2,1)S(1)}, bf16[2,2,256,256]{3,2,1,0:T(8,128)(2,1)}, u32[]{:S(2)}, u32[]{:S(2)}) collective-permute-start(bf16[2,2,256,256]{3,2,1,0:T(8,128)(2,1)S(1)} %get-tuple-element.55), channel_id=1, source_target_pairs={{0,6},{1,7},{2,4},{3,5},{4,2},{5,3},{6,0},{7,1},{8,14},{9,15},{10,... | collective-permute-start | bytes 1572872 | tf_op jit(solution)/shard_map/ppermute | solution.py:24
  77.2 10.7 %collective-permute-start.18 = (bf16[2,256,256]{2,1,0:T(8,128)(2,1)S(1)}, bf16[2,256,256]{2,1,0:T(8,128)(2,1)S(1)}, u32[]{:S(2)}, u32[]{:S(2)}) collective-permute-start(bf16[2,256,256]{2,1,0:T(8,128)(2,1)S(1)} %get-tuple-element.58), channel_id=1, source_target_pairs={{0,6},{1,7},{2,4},{3,5},{4,2},{5,3},{6,0},{7,1},{8,14},{9,15},{10,... | collective-permute-start | bytes 786440 | tf_op jit(solution)/shard_map/ppermute | solution.py:24
  78.4 9.6 %collective-permute-start.19 = (bf16[2,256,256]{2,1,0:T(8,128)(2,1)S(1)}, bf16[2,256,256]{2,1,0:T(8,128)(2,1)S(1)}, u32[]{:S(2)}, u32[]{:S(2)}) collective-permute-start(bf16[2,256,256]{2,1,0:T(8,128)(2,1)S(1)} %get-tuple-element.59), channel_id=1, source_target_pairs={{0,2},{1,3},{2,0},{3,1},{4,6},{5,7},{6,4},{7,5},{8,10},{9,11},{10,... | collective-permute-start | bytes 786440 | tf_op jit(solution)/shard_map/ppermute | solution.py:24
  81.6 11.5 %collective-permute-start.23 = (bf16[128,256]{1,0:T(8,128)(2,1)S(1)}, bf16[128,256]{1,0:T(8,128)(2,1)S(1)}, u32[]{:S(2)}, u32[]{:S(2)}) collective-permute-start(bf16[128,256]{1,0:T(8,128)(2,1)S(1)} %fusion.1), channel_id=1, source_target_pairs={{0,8},{1,9},{2,10},{3,11},{4,12},{5,13},{6,14},{7,15},{8,0},{9,1},... | collective-permute-start | bytes 196616 | tf_op jit(solution)/shard_map/ppermute | solution.py:24
  84.4 10.1 %collective-permute-start.24 = (bf16[128,256]{1,0:T(8,128)(2,1)S(1)}, bf16[128,256]{1,0:T(8,128)(2,1)S(1)}, u32[]{:S(2)}, u32[]{:S(2)}) collective-permute-start(bf16[128,256]{1,0:T(8,128)(2,1)S(1)} %fusion.1), channel_id=1, source_target_pairs={{0,16},{1,17},{2,18},{3,19},{4,20},{5,21},{6,22},{7,23},{8,24},{9,... | collective-permute-start | bytes 196616 | tf_op jit(solution)/shard_map/ppermute | solution.py:24
  90.9 12.2 %collective-permute-start.21 = (bf16[256,256]{1,0:T(8,128)(2,1)S(1)}, bf16[256,256]{1,0:T(8,128)(2,1)S(1)}, u32[]{:S(2)}, u32[]{:S(2)}) collective-permute-start(bf16[256,256]{1,0:T(8,128)(2,1)S(1)} %get-tuple-element.66), channel_id=1, source_target_pairs={{0,16},{1,17},{2,18},{3,19},{4,20},{5,21},{6,22},{7,23},{8,24},{9,... | collective-permute-start | bytes 393224 | tf_op jit(solution)/shard_map/ppermute | solution.py:24
  93.1 10.0 %collective-permute-start.22 = (bf16[256,256]{1,0:T(8,128)(2,1)S(1)}, bf16[256,256]{1,0:T(8,128)(2,1)S(1)}, u32[]{:S(2)}, u32[]{:S(2)}) collective-permute-start(bf16[256,256]{1,0:T(8,128)(2,1)S(1)} %get-tuple-element.67), channel_id=1, source_target_pairs={{0,24},{1,25},{2,26},{3,27},{4,28},{5,29},{6,30},{7,31},{8,16},{9,... | collective-permute-start | bytes 393224 | tf_op jit(solution)/shard_map/ppermute | solution.py:24
  94.5 14.3 %collective-permute-start.29 = (bf16[512,256]{1,0:T(8,128)(2,1)S(1)}, bf16[512,256]{1,0:T(8,128)(2,1)S(1)}, u32[]{:S(2)}, u32[]{:S(2)}) collective-permute-start(bf16[512,256]{1,0:T(8,128)(2,1)S(1)} %pad_maximum_fusion.4.rest_0_), channel_id=1, source_target_pairs={{0,2},{1,3},{2,0},{3,1},{4,6},{5,7},{6,4},{7,5},{8,10},{9,11},{10,... | collective-permute-start | bytes 786440 | tf_op jit(solution)/shard_map/ppermute | solution.py:24
  96.4 12.5 %collective-permute-start.30 = (bf16[512,256]{1,0:T(8,128)(2,1)S(1)}, bf16[512,256]{1,0:T(8,128)(2,1)S(1)}, u32[]{:S(2)}, u32[]{:S(2)}) collective-permute-start(bf16[512,256]{1,0:T(8,128)(2,1)S(1)} %pad_maximum_fusion.4.rest_0_), channel_id=1, source_target_pairs={{0,6},{1,7},{2,4},{3,5},{4,2},{5,3},{6,0},{7,1},{8,14},{9,15},{10,... | collective-permute-start | bytes 786440 | tf_op jit(solution)/shard_map/ppermute | solution.py:24
  104.3 11.2 %collective-permute-start.26 = (bf16[320,256]{1,0:T(8,128)(2,1)S(1)}, bf16[320,256]{1,0:T(8,128)(2,1)S(1)}, u32[]{:S(2)}, u32[]{:S(2)}) collective-permute-start(bf16[320,256]{1,0:T(8,128)(2,1)S(1)} %get-tuple-element.71), channel_id=1, source_target_pairs={{0,8},{1,9},{2,10},{3,11},{4,12},{5,13},{6,14},{7,15},{8,0},{9,1},... | collective-permute-start | bytes 491528 | tf_op jit(solution)/shard_map/ppermute | solution.py:24
  106.4 14.2 %collective-permute-start.27 = (bf16[320,256]{1,0:T(8,128)(2,1)S(1)}, bf16[320,256]{1,0:T(8,128)(2,1)S(1)}, u32[]{:S(2)}, u32[]{:S(2)}) collective-permute-start(bf16[320,256]{1,0:T(8,128)(2,1)S(1)} %get-tuple-element.72), channel_id=1, source_target_pairs={{0,16},{1,17},{2,18},{3,19},{4,20},{5,21},{6,22},{7,23},{8,24},{9,... | collective-permute-start | bytes 491528 | tf_op jit(solution)/shard_map/ppermute | solution.py:24
  107.5 13.1 %collective-permute-start.28 = (bf16[320,256]{1,0:T(8,128)(2,1)S(1)}, bf16[320,256]{1,0:T(8,128)(2,1)S(1)}, u32[]{:S(2)}, u32[]{:S(2)}) collective-permute-start(bf16[320,256]{1,0:T(8,128)(2,1)S(1)} %get-tuple-element.73), channel_id=1, source_target_pairs={{0,24},{1,25},{2,26},{3,27},{4,28},{5,29},{6,30},{7,31},{8,16},{9,... | collective-permute-start | bytes 491528 | tf_op jit(solution)/shard_map/ppermute | solution.py:24
  115.5 8.4 %collective-permute-start.35 = (bf16[2048,256]{1,0:T(8,128)(2,1)S(1)}, bf16[2048,256]{1,0:T(8,128)(2,1)S(1)}, u32[]{:S(2)}, u32[]{:S(2)}) collective-permute-start(bf16[2048,256]{1,0:T(8,128)(2,1)S(1)} %constant_dynamic-update-slice_fusion.1), channel_id=1, source_target_pairs={{0,1},{1,0},{2,3},{3,2},{4,5},{5,4},{6,7},{7,6},{8,9},{9,8},{10,11... | collective-permute-start | bytes 3145736 | tf_op jit(solution)/shard_map/ppermute | solution.py:24
  120.7 10.7 %collective-permute-start.33 = (bf16[1088,256]{1,0:T(8,128)(2,1)S(1)}, bf16[1088,256]{1,0:T(8,128)(2,1)S(1)}, u32[]{:S(2)}, u32[]{:S(2)}) collective-permute-start(bf16[1088,256]{1,0:T(8,128)(2,1)S(1)} %fusion.27.rest_0_), channel_id=1, source_target_pairs={{0,2},{1,3},{2,0},{3,1},{4,6},{5,7},{6,4},{7,5},{8,10},{9,11},{10,... | collective-permute-start | bytes 1671176 | tf_op jit(solution)/shard_map/ppermute | solution.py:24
  122.6 10.8 %collective-permute-start.34 = (bf16[1088,256]{1,0:T(8,128)(2,1)S(1)}, bf16[1088,256]{1,0:T(8,128)(2,1)S(1)}, u32[]{:S(2)}, u32[]{:S(2)}) collective-permute-start(bf16[1088,256]{1,0:T(8,128)(2,1)S(1)} %fusion.27.rest_0_), channel_id=1, source_target_pairs={{0,6},{1,7},{2,4},{3,5},{4,2},{5,3},{6,0},{7,1},{8,14},{9,15},{10,... | collective-permute-start | bytes 1671176 | tf_op jit(solution)/shard_map/ppermute | solution.py:24
  133.6 13.5 %collective-permute-start.38 = (bf16[3072,256]{1,0:T(8,128)(2,1)S(1)}, bf16[3072,256]{1,0:T(8,128)(2,1)S(1)}, u32[]{:S(2)}, u32[]{:S(2)}) collective-permute-start(bf16[3072,256]{1,0:T(8,128)(2,1)S(1)} %pad_maximum_fusion), channel_id=1, source_target_pairs={{0,1},{1,0},{2,3},{3,2},{4,5},{5,4},{6,7},{7,6},{8,9},{9,8},{10,11... | collective-permute-start | bytes 4718600 | tf_op jit(solution)/shard_map/ppermute | solution.py:24
  133.7 9.5 %collective-permute-start.36 = (bf16[576,256]{1,0:T(8,128)(2,1)S(1)}, bf16[576,256]{1,0:T(8,128)(2,1)S(1)}, u32[]{:S(2)}, u32[]{:S(2)}) collective-permute-start(bf16[576,256]{1,0:T(8,128)(2,1)S(1)} %pad_maximum_fusion.3), channel_id=1, source_target_pairs={{0,6},{1,7},{2,4},{3,5},{4,2},{5,3},{6,0},{7,1},{8,14},{9,15},{10,... | collective-permute-start | bytes 884744 | tf_op jit(solution)/shard_map/ppermute | solution.py:24
  135.6 9.4 %collective-permute-start.37 = (bf16[512,256]{1,0:T(8,128)(2,1)S(1)}, bf16[512,256]{1,0:T(8,128)(2,1)S(1)}, u32[]{:S(2)}, u32[]{:S(2)}) collective-permute-start(bf16[512,256]{1,0:T(8,128)(2,1)S(1)} %slice.329), channel_id=1, source_target_pairs={{0,2},{1,3},{2,0},{3,1},{4,6},{5,7},{6,4},{7,5},{8,10},{9,11},{10,... | collective-permute-start | bytes 786440 | tf_op jit(solution)/shard_map/ppermute | solution.py:24
  145.2 8.9 %collective-permute-start.40 = (f32[64,256]{1,0:T(8,128)S(1)}, f32[64,256]{1,0:T(8,128)S(1)}, u32[]{:S(2)}, u32[]{:S(2)}) collective-permute-start(f32[64,256]{1,0:T(8,128)S(1)} %add_add_fusion), channel_id=1, source_target_pairs={{0,1},{1,0},{2,3},{3,2},{4,5},{5,4},{6,7},{7,6},{8,9},{9,8},{10,11... | collective-permute-start | bytes 196616 | tf_op jit(solution)/shard_map/ppermute | solution.py:24
  153.9 11.1 %collective-permute-start.43 = (bf16[2,384,256]{2,1,0:T(8,128)(2,1)S(1)}, bf16[2,384,256]{2,1,0:T(8,128)(2,1)S(1)}, u32[]{:S(2)}, u32[]{:S(2)}) collective-permute-start(bf16[2,384,256]{2,1,0:T(8,128)(2,1)S(1)} %bitcast.129), channel_id=1, source_target_pairs={{0,192},{32,224},{64,128},{96,160},{128,64},{160,96},{192,0},{224,... | collective-permute-start | bytes 1179656 | tf_op jit(solution)/shard_map/ppermute | solution.py:24
  154.2 10.9 %collective-permute-start.41 = (bf16[832,256]{1,0:T(8,128)(2,1)S(1)}, bf16[832,256]{1,0:T(8,128)(2,1)S(1)}, u32[]{:S(2)}, u32[]{:S(2)}) collective-permute-start(bf16[832,256]{1,0:T(8,128)(2,1)S(1)} %pad_maximum_fusion.2), channel_id=1, source_target_pairs={{0,64},{32,96},{64,0},{96,32},{128,192},{160,224},{192,128},{224,1... | collective-permute-start | bytes 1277960 | tf_op jit(solution)/shard_map/ppermute | solution.py:24
  165.2 8.0 %collective-permute-start.42 = (bf16[448,256]{1,0:T(8,128)(2,1)S(1)}, bf16[448,256]{1,0:T(8,128)(2,1)S(1)}, u32[]{:S(2)}, u32[]{:S(2)}) collective-permute-start(bf16[448,256]{1,0:T(8,128)(2,1)S(1)} %pad_maximum_fusion.5), channel_id=1, source_target_pairs={{0,192},{32,224},{64,128},{96,160},{128,64},{160,96},{192,0},{224,... | collective-permute-start | bytes 688136 | tf_op jit(solution)/shard_map/ppermute | solution.py:24
  173.3 10.9 %collective-permute-start.45 = (bf16[448,256]{1,0:T(8,128)(2,1)S(1)}, bf16[448,256]{1,0:T(8,128)(2,1)S(1)}, u32[]{:S(2)}, u32[]{:S(2)}) collective-permute-start(bf16[448,256]{1,0:T(8,128)(2,1)S(1)} %pad_maximum_fusion.6), channel_id=1, source_target_pairs={{0,32},{32,0},{64,96},{96,64},{128,160},{160,128},{192,224},{224,1... | collective-permute-start | bytes 688136 | tf_op jit(solution)/shard_map/ppermute | solution.py:24
  184.2 12.2 %collective-permute-start.46 = (bf16[64,256]{1,0:T(8,128)(2,1)S(1)}, bf16[64,256]{1,0:T(8,128)(2,1)S(1)}, u32[]{:S(2)}, u32[]{:S(2)}) collective-permute-start(bf16[64,256]{1,0:T(8,128)(2,1)S(1)} %get-tuple-element.80), channel_id=1, source_target_pairs={{0,8},{1,9},{2,10},{3,11},{4,12},{5,13},{6,14},{7,15},{8,0},{9,1},... | collective-permute-start | bytes 98312 | tf_op jit(solution)/shard_map/ppermute | solution.py:24
  (31 other events, 354.1 us)

commit v3 on v2

--- a/solution.py
+++ b/solution.py
@@ -13,7 +13,8 @@
 bf16 = jnp.bfloat16
 
 chunks = ((0,), (1, 2))
-unroll = 8
+forward_unroll = 8
+backward_unroll = 16
 padded = 256
 
 x_bit, z_bit, y_bit = 1, 3, 1
@@ -28,7 +29,8 @@
     return lax.optimization_barrier((value, earlier))[0]
 
 
-def group_kernel(table, tiles, *rest, spans, group, flipped, carried):
+def group_kernel(table, tiles, *rest, spans, group, flipped, carried, base):
+    unroll = backward_unroll if flipped else forward_unroll
     pieces = rest[: len(spans)]
     previous = rest[len(spans)] if carried else None
     out, source = rest[-2:]
@@ -45,7 +47,7 @@
 
     def clear(i, _):
         if carried:
-            out[i] = previous[i].astype(out.dtype)
+            out[i] = previous[base + i].astype(out.dtype)
         else:
             out[i] = jnp.zeros(out.shape[1:], out.dtype)
         return 0
@@ -72,14 +74,16 @@
                 total = jnp.where(fresh, previous[place], total) + product
             else:
                 total = total * (1.0 - fresh.astype(f32)) + product
-            out[place] = total.astype(out.dtype)
+            out[place - base] = total.astype(out.dtype)
         return total
 
     steps = (stop - start + unroll - 1) // unroll
     lax.fori_loop(0, steps, advance, jnp.zeros(out.shape[1:], f32))
 
 
-def group_products(table, tiles, pieces, count, group, flipped, previous=None, dtype=bf16):
+def group_products(
+    table, tiles, pieces, count, group, flipped, previous=None, dtype=bf16, base=0
+):
     slots, edge, _ = tiles.shape
     arrays = [array for array, _, _ in pieces]
     spans = [(first, span) for _, first, span in pieces]
@@ -93,6 +97,7 @@
             group=group,
             flipped=flipped,
             carried=previous is not None,
+            base=base,
         ),
         out_shape=jax.ShapeDtypeStruct((count, edge, width), dtype),
         in_specs=[pl.BlockSpec(memory_space=pltpu.SMEM)] + [whole] * (len(operands) - 1),
@@ -141,7 +146,8 @@
     forward_place = block * breadth + inner
     forward_key = (chunk * 2 + 1 - core) * 128 + forward_place
     backward_origin = (core * 16 + x * 4 + z) * breadth + inner
-    backward_key = chunk * 128 + source_place
+    kept = jnp.logical_and(chunk == len(chunks) - 1, (row_apart & 1) == 0)
+    backward_key = (chunk + kept.astype(jnp.int32)) * 128 + source_place
 
     lane = lax.broadcasted_iota(jnp.int32, shape, 1)
     sub = lax.broadcasted_iota(jnp.int32, shape, 0)
@@ -168,7 +174,7 @@
         out[...] = jnp.where(lane[0:1] < slots, low | (high << 16), bounds.astype(jnp.int32))
 
     table(forward_key, forward_place, source_place, 2 * len(chunks), forward)
-    table(backward_key, source_place, backward_origin, len(chunks), backward)
+    table(backward_key, source_place, backward_origin, len(chunks) + 1, backward)
 
 
 def slot_tables(coords, live_count, own_col, own_row, per_owner, tiles):
@@ -215,10 +221,9 @@
     return value.astype(f32)
 
 
-def reduce_row(terms, share):
+def reduce_row(low, high, share):
     near, far = 1 << y_bit, 3 << y_bit
-    rows, width = terms.shape[2:]
-    low, high = terms[0], terms[1]
+    width = low.shape[2]
 
     def send(value, mask):
         rounded = share.astype(bf16)
@@ -229,11 +234,14 @@
 
     high_in = exchange(high[2:4], "row", far)
     low_in, share = send(low[1:3], near)
-    high_next = exchange((wide(high[1]) + wide(high_in[0])).astype(bf16), "row", near)
-    low_next, share = send((wide(low[3]) + wide(low_in[1])).astype(bf16), far)
+    high_second = (wide(high[1]) + wide(high_in[0])).astype(bf16)
+    high_next = exchange(high_second, "row", near)
+    low_second = (wide(low[3]) + wide(low_in[1])).astype(bf16)
+    low_next, share = send(after(low_second, high_second), far)
     leaving = (wide(high[0]) + wide(high_in[1]) + wide(high_next)).astype(bf16)
-    arrived, share = send(leaving, 1)
-    return wide(low[0]) + wide(low_in[0]) + wide(low_next) + wide(arrived), share
+    arrived = exchange(leaving, "row", 1)
+    total = wide(low[0]) + wide(low_in[0]) + wide(low_next) + wide(arrived)
+    return total, after(share, leaving)
 
 
 def per_device(
@@ -370,7 +378,16 @@
         if not last:
             first, third = after((first, third), messages)
         if k:
-            terms = products(k - 1)
+            terms = group_products(
+                backward_table,
+                tiles,
+                arrivals(k - 1),
+                n_row * per_owner,
+                k - 1,
+                True,
+                terms,
+                f32,
+            )
             first, third = after((first, third), terms)
         low = first[: 2 * rows]
         if last:
@@ -391,9 +408,7 @@
             (third, 0, 4 * rows),
         ]
 
-        def products(
-            k, last=last, rows=rows, pieces=pieces, blocks=blocks, seconds=seconds, terms=terms
-        ):
+        def arrivals(k, last=last, rows=rows, pieces=pieces, blocks=blocks, seconds=seconds):
             if last:
                 main = exchange(jnp.concatenate(blocks, axis=0), "col", 1)
                 second, base = exchange(jnp.concatenate(seconds, axis=0), "col", 1), 0
@@ -407,20 +422,22 @@
                 (second, base + 2 * rows, 2 * rows),
                 (main, 8 * rows, 4 * rows),
             ]
-            return group_products(
-                backward_table,
-                tiles,
-                pieces + arrived,
-                n_row * per_owner,
-                k,
-                True,
-                terms,
-                bf16 if last else f32,
-            )
-
+            return pieces + arrived
+
+    half = n_row * per_owner // 2
+    last = len(chunks) - 1
+    pieces = arrivals(last)
     share = share + exchange(share, "col", 1)
-    terms = products(len(chunks) - 1)
-    source_total, share = reduce_row(terms.reshape(2, 4, own_rows, width), share)
+    share = share + exchange(after(share, pieces[-1][0]), "row", 1)
+
+    def final_terms(table, group, base):
+        return group_products(
+            table, tiles, pieces, half, group, True, terms, bf16, base
+        ).reshape(4, own_rows, width)
+
+    high = final_terms(backward_table, last, half)
+    low = final_terms(after(backward_table, high[2:4]), last + 1, 0)
+    source_total, share = reduce_row(low, high, share)
     share = share.astype(bf16)
     grad_weight = jnp.zeros((width, width), f32)
     for distance in (0, 1, 2, 3):

time: 201 us -> 196 us (0.975); the launches traced: 202 us -> 194 us
  waiting for transfers between devices: 68.1 us -> 59.6 us
  Pallas kernels: 23.1 us -> 16.6 us
  starting transfers between devices: 87.9 us -> 93.5 us
    ppermute x49 -> x50, waiting for transfers between devices: 68.1 us -> 59.6 us  [exchange(): return lax.ppermute(value, axis, [(i, i ^ mask) for i in range(size)])]
    pallas_call x6 -> x7, Pallas kernels: 21.9 us -> 15.4 us  [group_products(): pl.pallas_call(functools.partial(group_kernel, spans=spans, group=group,...]
    ppermute x49 -> x50, starting transfers between devices: 87.9 us -> 93.5 us  [exchange(): return lax.ppermute(value, axis, [(i, i ^ mask) for i in range(size)])]
    unnamed x36 -> x38, local copies, waits for them, and re-layouts: 8.31 us -> 8.87 us
  transfers between devices with their start and end apart: 49 -> 50, of which waited for: 25 -> 22; matrix products, arithmetic and copies ran while one was open for 4% -> 5% of each run, Pallas kernels for 9% -> 7%
where the time goes in v3:
time: 196 us; the launch traced here: 194 us
  starting transfers between devices  93.5 us (48%)
  waiting for transfers between devices  59.6 us (30%)
  Pallas kernels  16.6 us (8%)
  local copies, waits for them, and re-layouts  11.2 us (6%)
  other arithmetic  9.52 us (5%)
  between operations  2.07 us (1%)
    ppermute x50, starting transfers between devices, exchange(): return lax.ppermute(value, axis, [(i, i ^ mask) for i in range(size)])  93.5 us
    ppermute x50, waiting for transfers between devices, exchange(): return lax.ppermute(value, axis, [(i, i ^ mask) for i in range(size)])  59.6 us
    pallas_call x7, Pallas kernels, group_products(): pl.pallas_call(functools.partial(group_kernel, spans=spans, group=group,...  15.4 us
    unnamed x38, local copies, waits for them, and re-layouts  8.87 us
  transfers between devices with their start and end apart: 50, of which 22 were waited for; matrix products, arithmetic and copies ran while one was open for 5% of the time, Pallas kernels for 7%

profile of v3, /device:TPU:2, one launch (start us, length us, event | category | flops | bytes accessed | tf_op | source)
XLA Modules:
  0.0 193.9 jit_solution(15053879304122025543)
XLA Ops:
  2.4 7.3 %collective-permute-start.1 = (bf16[384,256]{1,0:T(8,128)(2,1)S(1)}, bf16[384,256]{1,0:T(8,128)(2,1)S(1)}, u32[]{:S(2)}, u32[]{:S(2)}) collective-permute-start(bf16[384,256]{1,0:T(8,128)(2,1)S(1)} %fusion.9.rest_0_), channel_id=1, source_target_pairs={{0,32},{32,0},{64,96},{96,64},{128,160},{160,128},{192,224},{224,1... | collective-permute-start | bytes 589832 | tf_op jit(solution)/shard_map/ppermute | solution.py:25
  9.7 3.0 %collective-permute-start.3 = (bf16[384,256]{1,0:T(8,128)(2,1)S(1)}, bf16[384,256]{1,0:T(8,128)(2,1)S(1)}, u32[]{:S(2)}, u32[]{:S(2)}) collective-permute-start(bf16[384,256]{1,0:T(8,128)(2,1)S(1)} %fusion.9.rest_0_), channel_id=1, source_target_pairs={{0,192},{32,224},{64,128},{96,160},{128,64},{160,96},{192,0},{224,... | collective-permute-start | bytes 589832 | tf_op jit(solution)/shard_map/ppermute | solution.py:25
  14.7 3.0 %collective-permute-start.4 = (bf16[384,256]{1,0:T(8,128)(2,1)S(1)}, bf16[384,256]{1,0:T(8,128)(2,1)S(1)}, u32[]{:S(2)}, u32[]{:S(2)}) collective-permute-start(bf16[384,256]{1,0:T(8,128)(2,1)S(1)} %collective-permute-done.1.rest_5_), channel_id=1, source_target_pairs={{0,192},{32,224},{64,128},{96,160},{128,64},{160,96},{192,0},{224,... | collective-permute-start | bytes 589832 | tf_op jit(solution)/shard_map/ppermute | solution.py:25
  18.8 3.2 %collective-permute-done.4.rest_9_ = bf16[384,256]{1,0:T(8,128)(2,1)S(1)} collective-permute-done((bf16[384,256]{1,0:T(8,128)(2,1)S(1)}, bf16[384,256]{1,0:T(8,128)(2,1)S(1)}, u32[]{:S(2)}, u32[]{:S(2)}) %collective-permute-start.4) | collective-permute-done | bytes 196640 | tf_op jit(solution)/shard_map/ppermute | solution.py:25
  26.6 2.8 %copy-done.1 = bf16[1,1,192,128,128]{4,3,2,1,0:T(8,128)(2,1)S(1)} copy-done((bf16[1,1,192,128,128]{4,3,2,1,0:T(8,128)(2,1)S(1)}, bf16[1,1,192,128,128]{4,3,2,1,0:T(8,128)(2,1)}, u32[]{:S(2)}) %copy-start.1) | copy-done | bytes 6291480
  36.7 2.2 %forward2.1 = bf16[32,128,256]{2,1,0:T(8,128)(2,1)S(1)} custom-call(s32[1,256]{1,0:T(1,128)S(1)} %get-tuple-element.53.table, bf16[192,128,128]{2,1,0:T(8,128)(2,1)S(1)} %bitcast.109, bf16[384,256]{1,0:T(8,128)(2,1)S(1)} %fusion.9.rest_0_, bf16[384,256]{1,0:T(8,128)(2,1)S(1)} %collective-permute-done.rest_1_, ...), custom_call_target="tpu_custom_call" | custom-call | flops 402653184 | bytes 4194304 | tf_op jit(solution)/shard_map/forward2/pallas_call | solution.py:93
  43.0 5.6 %collective-permute-done.9 = bf16[2,2,128,256]{3,2,1,0:T(8,128)(2,1)S(1)} collective-permute-done((bf16[2,2,128,256]{3,2,1,0:T(8,128)(2,1)S(1)}, bf16[2,2,128,256]{3,2,1,0:T(8,128)(2,1)S(1)}, u32[]{:S(2)}, u32[]{:S(2)}) %collective-permute-start.9) | collective-permute-done | bytes 262176 | tf_op jit(solution)/shard_map/ppermute | solution.py:25
  61.4 7.0 %collective-permute-start.13 = (bf16[128,256]{1,0:T(8,128)(2,1)S(1)}, bf16[128,256]{1,0:T(8,128)(2,1)}, u32[]{:S(2)}, u32[]{:S(2)}) collective-permute-start(bf16[128,256]{1,0:T(8,128)(2,1)S(1)} %fusion.26), channel_id=1, source_target_pairs={{0,8},{1,9},{2,10},{3,11},{4,12},{5,13},{6,14},{7,15},{8,0},{9,1},... | collective-permute-start | bytes 196616 | tf_op jit(solution)/shard_map/ppermute | solution.py:25
  68.4 2.4 %collective-permute-start.15 = (bf16[128,256]{1,0:T(8,128)(2,1)S(1)}, bf16[128,256]{1,0:T(8,128)(2,1)}, u32[]{:S(2)}, u32[]{:S(2)}) collective-permute-start(bf16[128,256]{1,0:T(8,128)(2,1)S(1)} %get-tuple-element.57), channel_id=1, source_target_pairs={{0,24},{1,25},{2,26},{3,27},{4,28},{5,29},{6,30},{7,31},{8,16},{9,... | collective-permute-start | bytes 196616 | tf_op jit(solution)/shard_map/ppermute | solution.py:25
  72.5 2.5 %collective-permute-done.14 = bf16[128,256]{1,0:T(8,128)(2,1)} collective-permute-done((bf16[128,256]{1,0:T(8,128)(2,1)}, bf16[128,256]{1,0:T(8,128)(2,1)}, u32[]{:S(2)}, u32[]{:S(2)}) %collective-permute-start.14) | collective-permute-done | bytes 65568 | tf_op jit(solution)/shard_map/ppermute | solution.py:25
  78.4 2.4 %collective-permute-start.19 = (bf16[2,256,256]{2,1,0:T(8,128)(2,1)S(1)}, bf16[2,256,256]{2,1,0:T(8,128)(2,1)S(1)}, u32[]{:S(2)}, u32[]{:S(2)}) collective-permute-start(bf16[2,256,256]{2,1,0:T(8,128)(2,1)S(1)} %get-tuple-element.63), channel_id=1, source_target_pairs={{0,2},{1,3},{2,0},{3,1},{4,6},{5,7},{6,4},{7,5},{8,10},{9,11},{10,... | collective-permute-start | bytes 786440 | tf_op jit(solution)/shard_map/ppermute | solution.py:25
  81.3 3.6 %collective-permute-start.25 = (bf16[128,256]{1,0:T(8,128)(2,1)S(1)}, bf16[128,256]{1,0:T(8,128)(2,1)S(1)}, u32[]{:S(2)}, u32[]{:S(2)}) collective-permute-start(bf16[128,256]{1,0:T(8,128)(2,1)S(1)} %fusion.1), channel_id=1, source_target_pairs={{0,24},{1,25},{2,26},{3,27},{4,28},{5,29},{6,30},{7,31},{8,16},{9,... | collective-permute-start | bytes 196616 | tf_op jit(solution)/shard_map/ppermute | solution.py:25
  88.6 2.4 %collective-permute-start.20 = (bf16[256,256]{1,0:T(8,128)(2,1)S(1)}, bf16[256,256]{1,0:T(8,128)(2,1)S(1)}, u32[]{:S(2)}, u32[]{:S(2)}) collective-permute-start(bf16[256,256]{1,0:T(8,128)(2,1)S(1)} %get-tuple-element.69), channel_id=1, source_target_pairs={{0,8},{1,9},{2,10},{3,11},{4,12},{5,13},{6,14},{7,15},{8,0},{9,1},... | collective-permute-start | bytes 393224 | tf_op jit(solution)/shard_map/ppermute | solution.py:25
  94.2 2.6 %collective-permute-start.29 = (bf16[512,256]{1,0:T(8,128)(2,1)S(1)}, bf16[512,256]{1,0:T(8,128)(2,1)S(1)}, u32[]{:S(2)}, u32[]{:S(2)}) collective-permute-start(bf16[512,256]{1,0:T(8,128)(2,1)S(1)} %pad_maximum_fusion.4.rest_0_), channel_id=1, source_target_pairs={{0,2},{1,3},{2,0},{3,1},{4,6},{5,7},{6,4},{7,5},{8,10},{9,11},{10,... | collective-permute-start | bytes 786440 | tf_op jit(solution)/shard_map/ppermute | solution.py:25
  96.8 3.8 %collective-permute-done.21 = bf16[256,256]{1,0:T(8,128)(2,1)S(1)} collective-permute-done((bf16[256,256]{1,0:T(8,128)(2,1)S(1)}, bf16[256,256]{1,0:T(8,128)(2,1)S(1)}, u32[]{:S(2)}, u32[]{:S(2)}) %collective-permute-start.21) | collective-permute-done | bytes 131104 | tf_op jit(solution)/shard_map/ppermute | solution.py:25
  106.4 2.7 %collective-permute-start.32 = (bf16[256,256]{1,0:T(8,128)(2,1)S(1)}, bf16[256,256]{1,0:T(8,128)(2,1)S(1)}, u32[]{:S(2)}, u32[]{:S(2)}) collective-permute-start(bf16[256,256]{1,0:T(8,128)(2,1)S(1)} %slice.311), channel_id=1, source_target_pairs={{0,2},{1,3},{2,0},{3,1},{4,6},{5,7},{6,4},{7,5},{8,10},{9,11},{10,... | collective-permute-start | bytes 393224 | tf_op jit(solution)/shard_map/ppermute | solution.py:25
  110.0 4.1 %collective-permute-done.31.rest_2_ = bf16[256,256]{1,0:T(8,128)(2,1)S(1)} collective-permute-done((bf16[256,256]{1,0:T(8,128)(2,1)S(1)}, bf16[256,256]{1,0:T(8,128)(2,1)S(1)}, u32[]{:S(2)}, u32[]{:S(2)}) %collective-permute-start.31) | collective-permute-done | bytes 131104 | tf_op jit(solution)/shard_map/ppermute | solution.py:25
  114.3 3.1 %collective-permute-done.27 = bf16[320,256]{1,0:T(8,128)(2,1)S(1)} collective-permute-done((bf16[320,256]{1,0:T(8,128)(2,1)S(1)}, bf16[320,256]{1,0:T(8,128)(2,1)S(1)}, u32[]{:S(2)}, u32[]{:S(2)}) %collective-permute-start.27) | collective-permute-done | bytes 163872 | tf_op jit(solution)/shard_map/ppermute | solution.py:25
  121.6 2.7 %backward0.1.rest_10_ = f32[24,128,256]{2,1,0:T(8,128)S(1)} custom-call(s32[1,256]{1,0:T(1,128)S(1)} %get-tuple-element.83.table, bf16[192,128,128]{2,1,0:T(8,128)(2,1)S(1)} %bitcast.113, bf16[512,256]{1,0:T(8,128)(2,1)S(1)} %pad_maximum_fusion.4.rest_0_, bf16[512,256]{1,0:T(8,128)(2,1)S(1)} %collective-permute-done.29.rest_1_, ...), custom_call_target="tpu_custom_call" | custom-call | flops 402653184 | bytes 3145728 | tf_op jit(solution)/shard_map/backward0/pallas_call | solution.py:93
  124.3 5.2 %collective-permute-done.34.rest_4_ = bf16[1088,256]{1,0:T(8,128)(2,1)S(1)} collective-permute-done((bf16[1088,256]{1,0:T(8,128)(2,1)S(1)}, bf16[1088,256]{1,0:T(8,128)(2,1)S(1)}, u32[]{:S(2)}, u32[]{:S(2)}) %collective-permute-start.34) | collective-permute-done | bytes 557088 | tf_op jit(solution)/shard_map/ppermute | solution.py:25
  132.1 2.4 %collective-permute-start.37 = (bf16[512,256]{1,0:T(8,128)(2,1)S(1)}, bf16[512,256]{1,0:T(8,128)(2,1)S(1)}, u32[]{:S(2)}, u32[]{:S(2)}) collective-permute-start(bf16[512,256]{1,0:T(8,128)(2,1)S(1)} %slice.314), channel_id=1, source_target_pairs={{0,2},{1,3},{2,0},{3,1},{4,6},{5,7},{6,4},{7,5},{8,10},{9,11},{10,... | collective-permute-start | bytes 786440 | tf_op jit(solution)/shard_map/ppermute | solution.py:25
  134.6 5.9 %collective-permute-done.36.rest_2_ = bf16[576,256]{1,0:T(8,128)(2,1)S(1)} collective-permute-done((bf16[576,256]{1,0:T(8,128)(2,1)S(1)}, bf16[576,256]{1,0:T(8,128)(2,1)S(1)}, u32[]{:S(2)}, u32[]{:S(2)}) %collective-permute-start.36) | collective-permute-done | bytes 294944 | tf_op jit(solution)/shard_map/ppermute | solution.py:25
  143.4 7.7 %collective-permute-start.41 = (f32[64,256]{1,0:T(8,128)S(1)}, f32[64,256]{1,0:T(8,128)S(1)}, u32[]{:S(2)}, u32[]{:S(2)}) collective-permute-start(f32[64,256]{1,0:T(8,128)S(1)} %add.280), channel_id=1, source_target_pairs={{0,32},{32,0},{64,96},{96,64},{128,160},{160,128},{192,224},{224,1... | collective-permute-start | bytes 196616 | tf_op jit(solution)/shard_map/ppermute | solution.py:25
  151.1 2.6 %backward1.1 = bf16[12,128,256]{2,1,0:T(8,128)(2,1)S(1)} custom-call(s32[1,256]{1,0:T(1,128)S(1)} %get-tuple-element.83.table, bf16[192,128,128]{2,1,0:T(8,128)(2,1)S(1)} %bitcast.114, bf16[1088,256]{1,0:T(8,128)(2,1)S(1)} %fusion.27.rest_0_, bf16[1088,256]{1,0:T(8,128)(2,1)S(1)} %collective-permute-done.33.rest_1_, ...), custom_call_target="tpu_custom_call" | custom-call | flops 402653184 | bytes 1572864 | tf_op jit(solution)/shard_map/backward1/pallas_call | solution.py:93
  154.2 2.6 %backward2.1 = bf16[12,128,256]{2,1,0:T(8,128)(2,1)S(1)} custom-call(s32[1,256]{1,0:T(1,128)S(1)} %get-tuple-element.83.table, bf16[192,128,128]{2,1,0:T(8,128)(2,1)S(1)} %bitcast.115, bf16[1088,256]{1,0:T(8,128)(2,1)S(1)} %fusion.27.rest_0_, bf16[1088,256]{1,0:T(8,128)(2,1)S(1)} %collective-permute-done.33.rest_1_, ...), custom_call_target="tpu_custom_call" | custom-call | flops 402653184 | bytes 1572864 | tf_op jit(solution)/shard_map/backward2/pallas_call | solution.py:93
  156.9 3.8 %collective-permute-start.42 = (bf16[832,256]{1,0:T(8,128)(2,1)S(1)}, bf16[832,256]{1,0:T(8,128)(2,1)S(1)}, u32[]{:S(2)}, u32[]{:S(2)}) collective-permute-start(bf16[832,256]{1,0:T(8,128)(2,1)S(1)} %pad_maximum_fusion.2), channel_id=1, source_target_pairs={{0,64},{32,96},{64,0},{96,32},{128,192},{160,224},{192,128},{224,1... | collective-permute-start | bytes 1277960 | tf_op jit(solution)/shard_map/ppermute | solution.py:25
  160.7 6.2 %collective-permute-done.43 = bf16[2,384,256]{2,1,0:T(8,128)(2,1)S(1)} collective-permute-done((bf16[2,384,256]{2,1,0:T(8,128)(2,1)S(1)}, bf16[2,384,256]{2,1,0:T(8,128)(2,1)S(1)}, u32[]{:S(2)}, u32[]{:S(2)}) %collective-permute-start.43) | collective-permute-done | bytes 393248 | tf_op jit(solution)/shard_map/ppermute | solution.py:25
  168.4 2.9 %collective-permute-done.42 = bf16[832,256]{1,0:T(8,128)(2,1)S(1)} collective-permute-done((bf16[832,256]{1,0:T(8,128)(2,1)S(1)}, bf16[832,256]{1,0:T(8,128)(2,1)S(1)}, u32[]{:S(2)}, u32[]{:S(2)}) %collective-permute-start.42) | collective-permute-done | bytes 426016 | tf_op jit(solution)/shard_map/ppermute | solution.py:25
  171.4 3.8 %collective-permute-start.44 = (bf16[448,256]{1,0:T(8,128)(2,1)S(1)}, bf16[448,256]{1,0:T(8,128)(2,1)S(1)}, u32[]{:S(2)}, u32[]{:S(2)}) collective-permute-start(bf16[448,256]{1,0:T(8,128)(2,1)S(1)} %pad_maximum_fusion.5), channel_id=1, source_target_pairs={{0,192},{32,224},{64,128},{96,160},{128,64},{160,96},{192,0},{224,... | collective-permute-start | bytes 688136 | tf_op jit(solution)/shard_map/ppermute | solution.py:25
  179.2 5.3 %collective-permute-start.48 = (bf16[64,256]{1,0:T(8,128)(2,1)S(1)}, bf16[64,256]{1,0:T(8,128)(2,1)S(1)}, u32[]{:S(2)}, u32[]{:S(2)}) collective-permute-start(bf16[64,256]{1,0:T(8,128)(2,1)S(1)} %convert_add_fusion.13), channel_id=1, source_target_pairs={{0,16},{1,17},{2,18},{3,19},{4,20},{5,21},{6,22},{7,23},{8,24},{9,... | collective-permute-start | bytes 98312 | tf_op jit(solution)/shard_map/ppermute | solution.py:25
  186.1 2.3 %collective-permute-done.47 = bf16[64,256]{1,0:T(8,128)(2,1)S(1)} collective-permute-done((bf16[64,256]{1,0:T(8,128)(2,1)S(1)}, bf16[64,256]{1,0:T(8,128)(2,1)S(1)}, u32[]{:S(2)}, u32[]{:S(2)}) %collective-permute-start.47) | collective-permute-done | bytes 32800 | tf_op jit(solution)/shard_map/ppermute | solution.py:25
  188.5 3.8 %collective-permute-done.49 = bf16[64,256]{1,0:T(8,128)(2,1)S(1)} collective-permute-done((bf16[64,256]{1,0:T(8,128)(2,1)S(1)}, bf16[64,256]{1,0:T(8,128)(2,1)S(1)}, u32[]{:S(2)}, u32[]{:S(2)}) %collective-permute-start.49) | collective-permute-done | bytes 32800 | tf_op jit(solution)/shard_map/ppermute | solution.py:25
  (185 shorter events, 71.1 us)
Async XLA Ops:
  2.4 12.3 %collective-permute-start.1 = (bf16[384,256]{1,0:T(8,128)(2,1)S(1)}, bf16[384,256]{1,0:T(8,128)(2,1)S(1)}, u32[]{:S(2)}, u32[]{:S(2)}) collective-permute-start(bf16[384,256]{1,0:T(8,128)(2,1)S(1)} %fusion.9.rest_0_), channel_id=1, source_target_pairs={{0,32},{32,0},{64,96},{96,64},{128,160},{160,128},{192,224},{224,1... | collective-permute-start | bytes 589832 | tf_op jit(solution)/shard_map/ppermute | solution.py:25
  9.7 8.2 %collective-permute-start.3 = (bf16[384,256]{1,0:T(8,128)(2,1)S(1)}, bf16[384,256]{1,0:T(8,128)(2,1)S(1)}, u32[]{:S(2)}, u32[]{:S(2)}) collective-permute-start(bf16[384,256]{1,0:T(8,128)(2,1)S(1)} %fusion.9.rest_0_), channel_id=1, source_target_pairs={{0,192},{32,224},{64,128},{96,160},{128,64},{160,96},{192,0},{224,... | collective-permute-start | bytes 589832 | tf_op jit(solution)/shard_map/ppermute | solution.py:25
  38.9 17.9 %collective-permute-start.12 = (bf16[32,128,256]{2,1,0:T(8,128)(2,1)S(1)}, bf16[32,128,256]{2,1,0:T(8,128)(2,1)S(1)}, u32[]{:S(2)}, u32[]{:S(2)}) collective-permute-start(bf16[32,128,256]{2,1,0:T(8,128)(2,1)S(1)} %forward2.1), channel_id=1, source_target_pairs={{0,1},{1,0},{2,3},{3,2},{4,5},{5,4},{6,7},{7,6},{8,9},{9,8},{10,11... | collective-permute-start | bytes 6291464 | tf_op jit(solution)/shard_map/ppermute | solution.py:25
  40.4 8.3 %collective-permute-start.9 = (bf16[2,2,128,256]{3,2,1,0:T(8,128)(2,1)S(1)}, bf16[2,2,128,256]{3,2,1,0:T(8,128)(2,1)S(1)}, u32[]{:S(2)}, u32[]{:S(2)}) collective-permute-start(bf16[2,2,128,256]{3,2,1,0:T(8,128)(2,1)S(1)} %get-tuple-element.97), channel_id=1, source_target_pairs={{0,6},{1,7},{2,4},{3,5},{4,2},{5,3},{6,0},{7,1},{8,14},{9,15},{10,... | collective-permute-start | bytes 786440 | tf_op jit(solution)/shard_map/ppermute | solution.py:25
  41.8 8.4 %collective-permute-start.8 = (bf16[2,2,128,256]{3,2,1,0:T(8,128)(2,1)S(1)}, bf16[2,2,128,256]{3,2,1,0:T(8,128)(2,1)S(1)}, u32[]{:S(2)}, u32[]{:S(2)}) collective-permute-start(bf16[2,2,128,256]{3,2,1,0:T(8,128)(2,1)S(1)} %get-tuple-element.98), channel_id=1, source_target_pairs={{0,2},{1,3},{2,0},{3,1},{4,6},{5,7},{6,4},{7,5},{8,10},{9,11},{10,... | collective-permute-start | bytes 786440 | tf_op jit(solution)/shard_map/ppermute | solution.py:25
  58.4 17.7 %collective-permute-start.16 = (bf16[2,2,256,256]{3,2,1,0:T(8,128)(2,1)S(1)}, bf16[2,2,256,256]{3,2,1,0:T(8,128)(2,1)}, u32[]{:S(2)}, u32[]{:S(2)}) collective-permute-start(bf16[2,2,256,256]{3,2,1,0:T(8,128)(2,1)S(1)} %get-tuple-element.58), channel_id=1, source_target_pairs={{0,2},{1,3},{2,0},{3,1},{4,6},{5,7},{6,4},{7,5},{8,10},{9,11},{10,... | collective-permute-start | bytes 1572872 | tf_op jit(solution)/shard_map/ppermute | solution.py:25
  59.6 16.4 %collective-permute-start.17 = (bf16[2,2,256,256]{3,2,1,0:T(8,128)(2,1)S(1)}, bf16[2,2,256,256]{3,2,1,0:T(8,128)(2,1)}, u32[]{:S(2)}, u32[]{:S(2)}) collective-permute-start(bf16[2,2,256,256]{3,2,1,0:T(8,128)(2,1)S(1)} %get-tuple-element.59), channel_id=1, source_target_pairs={{0,6},{1,7},{2,4},{3,5},{4,2},{5,3},{6,0},{7,1},{8,14},{9,15},{10,... | collective-permute-start | bytes 1572872 | tf_op jit(solution)/shard_map/ppermute | solution.py:25
  61.4 11.2 %collective-permute-start.13 = (bf16[128,256]{1,0:T(8,128)(2,1)S(1)}, bf16[128,256]{1,0:T(8,128)(2,1)}, u32[]{:S(2)}, u32[]{:S(2)}) collective-permute-start(bf16[128,256]{1,0:T(8,128)(2,1)S(1)} %fusion.26), channel_id=1, source_target_pairs={{0,8},{1,9},{2,10},{3,11},{4,12},{5,13},{6,14},{7,15},{8,0},{9,1},... | collective-permute-start | bytes 196616 | tf_op jit(solution)/shard_map/ppermute | solution.py:25
  77.4 9.4 %collective-permute-start.18 = (bf16[2,256,256]{2,1,0:T(8,128)(2,1)S(1)}, bf16[2,256,256]{2,1,0:T(8,128)(2,1)S(1)}, u32[]{:S(2)}, u32[]{:S(2)}) collective-permute-start(bf16[2,256,256]{2,1,0:T(8,128)(2,1)S(1)} %get-tuple-element.62), channel_id=1, source_target_pairs={{0,6},{1,7},{2,4},{3,5},{4,2},{5,3},{6,0},{7,1},{8,14},{9,15},{10,... | collective-permute-start | bytes 786440 | tf_op jit(solution)/shard_map/ppermute | solution.py:25
  78.4 8.4 %collective-permute-start.19 = (bf16[2,256,256]{2,1,0:T(8,128)(2,1)S(1)}, bf16[2,256,256]{2,1,0:T(8,128)(2,1)S(1)}, u32[]{:S(2)}, u32[]{:S(2)}) collective-permute-start(bf16[2,256,256]{2,1,0:T(8,128)(2,1)S(1)} %get-tuple-element.63), channel_id=1, source_target_pairs={{0,2},{1,3},{2,0},{3,1},{4,6},{5,7},{6,4},{7,5},{8,10},{9,11},{10,... | collective-permute-start | bytes 786440 | tf_op jit(solution)/shard_map/ppermute | solution.py:25
  81.3 10.5 %collective-permute-start.25 = (bf16[128,256]{1,0:T(8,128)(2,1)S(1)}, bf16[128,256]{1,0:T(8,128)(2,1)S(1)}, u32[]{:S(2)}, u32[]{:S(2)}) collective-permute-start(bf16[128,256]{1,0:T(8,128)(2,1)S(1)} %fusion.1), channel_id=1, source_target_pairs={{0,24},{1,25},{2,26},{3,27},{4,28},{5,29},{6,30},{7,31},{8,16},{9,... | collective-permute-start | bytes 196616 | tf_op jit(solution)/shard_map/ppermute | solution.py:25
  84.9 8.5 %collective-permute-start.24 = (bf16[128,256]{1,0:T(8,128)(2,1)S(1)}, bf16[128,256]{1,0:T(8,128)(2,1)S(1)}, u32[]{:S(2)}, u32[]{:S(2)}) collective-permute-start(bf16[128,256]{1,0:T(8,128)(2,1)S(1)} %fusion.1), channel_id=1, source_target_pairs={{0,16},{1,17},{2,18},{3,19},{4,20},{5,21},{6,22},{7,23},{8,24},{9,... | collective-permute-start | bytes 196616 | tf_op jit(solution)/shard_map/ppermute | solution.py:25
  88.6 8.3 %collective-permute-start.20 = (bf16[256,256]{1,0:T(8,128)(2,1)S(1)}, bf16[256,256]{1,0:T(8,128)(2,1)S(1)}, u32[]{:S(2)}, u32[]{:S(2)}) collective-permute-start(bf16[256,256]{1,0:T(8,128)(2,1)S(1)} %get-tuple-element.69), channel_id=1, source_target_pairs={{0,8},{1,9},{2,10},{3,11},{4,12},{5,13},{6,14},{7,15},{8,0},{9,1},... | collective-permute-start | bytes 393224 | tf_op jit(solution)/shard_map/ppermute | solution.py:25
  91.0 9.7 %collective-permute-start.21 = (bf16[256,256]{1,0:T(8,128)(2,1)S(1)}, bf16[256,256]{1,0:T(8,128)(2,1)S(1)}, u32[]{:S(2)}, u32[]{:S(2)}) collective-permute-start(bf16[256,256]{1,0:T(8,128)(2,1)S(1)} %get-tuple-element.70), channel_id=1, source_target_pairs={{0,16},{1,17},{2,18},{3,19},{4,20},{5,21},{6,22},{7,23},{8,24},{9,... | collective-permute-start | bytes 393224 | tf_op jit(solution)/shard_map/ppermute | solution.py:25
  91.8 8.8 %collective-permute-start.22 = (bf16[256,256]{1,0:T(8,128)(2,1)S(1)}, bf16[256,256]{1,0:T(8,128)(2,1)S(1)}, u32[]{:S(2)}, u32[]{:S(2)}) collective-permute-start(bf16[256,256]{1,0:T(8,128)(2,1)S(1)} %get-tuple-element.71), channel_id=1, source_target_pairs={{0,24},{1,25},{2,26},{3,27},{4,28},{5,29},{6,30},{7,31},{8,16},{9,... | collective-permute-start | bytes 393224 | tf_op jit(solution)/shard_map/ppermute | solution.py:25
  93.5 12.9 %collective-permute-start.30 = (bf16[512,256]{1,0:T(8,128)(2,1)S(1)}, bf16[512,256]{1,0:T(8,128)(2,1)S(1)}, u32[]{:S(2)}, u32[]{:S(2)}) collective-permute-start(bf16[512,256]{1,0:T(8,128)(2,1)S(1)} %pad_maximum_fusion.4.rest_0_), channel_id=1, source_target_pairs={{0,6},{1,7},{2,4},{3,5},{4,2},{5,3},{6,0},{7,1},{8,14},{9,15},{10,... | collective-permute-start | bytes 786440 | tf_op jit(solution)/shard_map/ppermute | solution.py:25
  94.2 12.2 %collective-permute-start.29 = (bf16[512,256]{1,0:T(8,128)(2,1)S(1)}, bf16[512,256]{1,0:T(8,128)(2,1)S(1)}, u32[]{:S(2)}, u32[]{:S(2)}) collective-permute-start(bf16[512,256]{1,0:T(8,128)(2,1)S(1)} %pad_maximum_fusion.4.rest_0_), channel_id=1, source_target_pairs={{0,2},{1,3},{2,0},{3,1},{4,6},{5,7},{6,4},{7,5},{8,10},{9,11},{10,... | collective-permute-start | bytes 786440 | tf_op jit(solution)/shard_map/ppermute | solution.py:25
  101.9 12.4 %collective-permute-start.26 = (bf16[320,256]{1,0:T(8,128)(2,1)S(1)}, bf16[320,256]{1,0:T(8,128)(2,1)S(1)}, u32[]{:S(2)}, u32[]{:S(2)}) collective-permute-start(bf16[320,256]{1,0:T(8,128)(2,1)S(1)} %get-tuple-element.75), channel_id=1, source_target_pairs={{0,8},{1,9},{2,10},{3,11},{4,12},{5,13},{6,14},{7,15},{8,0},{9,1},... | collective-permute-start | bytes 491528 | tf_op jit(solution)/shard_map/ppermute | solution.py:25
  103.9 13.5 %collective-permute-start.27 = (bf16[320,256]{1,0:T(8,128)(2,1)S(1)}, bf16[320,256]{1,0:T(8,128)(2,1)S(1)}, u32[]{:S(2)}, u32[]{:S(2)}) collective-permute-start(bf16[320,256]{1,0:T(8,128)(2,1)S(1)} %get-tuple-element.76), channel_id=1, source_target_pairs={{0,16},{1,17},{2,18},{3,19},{4,20},{5,21},{6,22},{7,23},{8,24},{9,... | collective-permute-start | bytes 491528 | tf_op jit(solution)/shard_map/ppermute | solution.py:25
  105.0 12.5 %collective-permute-start.28 = (bf16[320,256]{1,0:T(8,128)(2,1)S(1)}, bf16[320,256]{1,0:T(8,128)(2,1)S(1)}, u32[]{:S(2)}, u32[]{:S(2)}) collective-permute-start(bf16[320,256]{1,0:T(8,128)(2,1)S(1)} %get-tuple-element.77), channel_id=1, source_target_pairs={{0,24},{1,25},{2,26},{3,27},{4,28},{5,29},{6,30},{7,31},{8,16},{9,... | collective-permute-start | bytes 491528 | tf_op jit(solution)/shard_map/ppermute | solution.py:25
  117.5 12.0 %collective-permute-start.34 = (bf16[1088,256]{1,0:T(8,128)(2,1)S(1)}, bf16[1088,256]{1,0:T(8,128)(2,1)S(1)}, u32[]{:S(2)}, u32[]{:S(2)}) collective-permute-start(bf16[1088,256]{1,0:T(8,128)(2,1)S(1)} %fusion.27.rest_0_), channel_id=1, source_target_pairs={{0,6},{1,7},{2,4},{3,5},{4,2},{5,3},{6,0},{7,1},{8,14},{9,15},{10,... | collective-permute-start | bytes 1671176 | tf_op jit(solution)/shard_map/ppermute | solution.py:25
  119.6 11.1 %collective-permute-start.33 = (bf16[1088,256]{1,0:T(8,128)(2,1)S(1)}, bf16[1088,256]{1,0:T(8,128)(2,1)S(1)}, u32[]{:S(2)}, u32[]{:S(2)}) collective-permute-start(bf16[1088,256]{1,0:T(8,128)(2,1)S(1)} %fusion.27.rest_0_), channel_id=1, source_target_pairs={{0,2},{1,3},{2,0},{3,1},{4,6},{5,7},{6,4},{7,5},{8,10},{9,11},{10,... | collective-permute-start | bytes 1671176 | tf_op jit(solution)/shard_map/ppermute | solution.py:25
  130.9 12.5 %collective-permute-start.38 = (bf16[3072,256]{1,0:T(8,128)(2,1)S(1)}, bf16[3072,256]{1,0:T(8,128)(2,1)S(1)}, u32[]{:S(2)}, u32[]{:S(2)}) collective-permute-start(bf16[3072,256]{1,0:T(8,128)(2,1)S(1)} %pad_maximum_fusion), channel_id=1, source_target_pairs={{0,1},{1,0},{2,3},{3,2},{4,5},{5,4},{6,7},{7,6},{8,9},{9,8},{10,11... | collective-permute-start | bytes 4718600 | tf_op jit(solution)/shard_map/ppermute | solution.py:25
  131.0 9.5 %collective-permute-start.36 = (bf16[576,256]{1,0:T(8,128)(2,1)S(1)}, bf16[576,256]{1,0:T(8,128)(2,1)S(1)}, u32[]{:S(2)}, u32[]{:S(2)}) collective-permute-start(bf16[576,256]{1,0:T(8,128)(2,1)S(1)} %pad_maximum_fusion.3), channel_id=1, source_target_pairs={{0,6},{1,7},{2,4},{3,5},{4,2},{5,3},{6,0},{7,1},{8,14},{9,15},{10,... | collective-permute-start | bytes 884744 | tf_op jit(solution)/shard_map/ppermute | solution.py:25
  132.1 9.1 %collective-permute-start.37 = (bf16[512,256]{1,0:T(8,128)(2,1)S(1)}, bf16[512,256]{1,0:T(8,128)(2,1)S(1)}, u32[]{:S(2)}, u32[]{:S(2)}) collective-permute-start(bf16[512,256]{1,0:T(8,128)(2,1)S(1)} %slice.314), channel_id=1, source_target_pairs={{0,2},{1,3},{2,0},{3,1},{4,6},{5,7},{6,4},{7,5},{8,10},{9,11},{10,... | collective-permute-start | bytes 786440 | tf_op jit(solution)/shard_map/ppermute | solution.py:25
  141.3 9.8 %collective-permute-start.39 = (bf16[1024,256]{1,0:T(8,128)(2,1)S(1)}, bf16[1024,256]{1,0:T(8,128)(2,1)S(1)}, u32[]{:S(2)}, u32[]{:S(2)}) collective-permute-start(bf16[1024,256]{1,0:T(8,128)(2,1)S(1)} %pad_maximum_fusion.1), channel_id=1, source_target_pairs={{0,1},{1,0},{2,3},{3,2},{4,5},{5,4},{6,7},{7,6},{8,9},{9,8},{10,11... | collective-permute-start | bytes 1572872 | tf_op jit(solution)/shard_map/ppermute | solution.py:25
  143.4 13.4 %collective-permute-start.41 = (f32[64,256]{1,0:T(8,128)S(1)}, f32[64,256]{1,0:T(8,128)S(1)}, u32[]{:S(2)}, u32[]{:S(2)}) collective-permute-start(f32[64,256]{1,0:T(8,128)S(1)} %add.280), channel_id=1, source_target_pairs={{0,32},{32,0},{64,96},{96,64},{128,160},{160,128},{192,224},{224,1... | collective-permute-start | bytes 196616 | tf_op jit(solution)/shard_map/ppermute | solution.py:25
  153.7 13.2 %collective-permute-start.43 = (bf16[2,384,256]{2,1,0:T(8,128)(2,1)S(1)}, bf16[2,384,256]{2,1,0:T(8,128)(2,1)S(1)}, u32[]{:S(2)}, u32[]{:S(2)}) collective-permute-start(bf16[2,384,256]{2,1,0:T(8,128)(2,1)S(1)} %bitcast.130), channel_id=1, source_target_pairs={{0,192},{32,224},{64,128},{96,160},{128,64},{160,96},{192,0},{224,... | collective-permute-start | bytes 1179656 | tf_op jit(solution)/shard_map/ppermute | solution.py:25
  156.9 14.4 %collective-permute-start.42 = (bf16[832,256]{1,0:T(8,128)(2,1)S(1)}, bf16[832,256]{1,0:T(8,128)(2,1)S(1)}, u32[]{:S(2)}, u32[]{:S(2)}) collective-permute-start(bf16[832,256]{1,0:T(8,128)(2,1)S(1)} %pad_maximum_fusion.2), channel_id=1, source_target_pairs={{0,64},{32,96},{64,0},{96,32},{128,192},{160,224},{192,128},{224,1... | collective-permute-start | bytes 1277960 | tf_op jit(solution)/shard_map/ppermute | solution.py:25
  167.0 8.2 %collective-permute-start.45 = (bf16[384,256]{1,0:T(8,128)(2,1)S(1)}, bf16[384,256]{1,0:T(8,128)(2,1)S(1)}, u32[]{:S(2)}, u32[]{:S(2)}) collective-permute-start(bf16[384,256]{1,0:T(8,128)(2,1)S(1)} %fusion.13), channel_id=1, source_target_pairs={{0,64},{32,96},{64,0},{96,32},{128,192},{160,224},{192,128},{224,1... | collective-permute-start | bytes 589832 | tf_op jit(solution)/shard_map/ppermute | solution.py:25
  175.3 17.7 %collective-permute-start.46 = (bf16[384,256]{1,0:T(8,128)(2,1)S(1)}, bf16[384,256]{1,0:T(8,128)(2,1)S(1)}, u32[]{:S(2)}, u32[]{:S(2)}) collective-permute-start(bf16[384,256]{1,0:T(8,128)(2,1)S(1)} %fusion.12), channel_id=1, source_target_pairs={{0,32},{32,0},{64,96},{96,64},{128,160},{160,128},{192,224},{224,1... | collective-permute-start | bytes 589832 | tf_op jit(solution)/shard_map/ppermute | solution.py:25
  179.2 9.2 %collective-permute-start.48 = (bf16[64,256]{1,0:T(8,128)(2,1)S(1)}, bf16[64,256]{1,0:T(8,128)(2,1)S(1)}, u32[]{:S(2)}, u32[]{:S(2)}) collective-permute-start(bf16[64,256]{1,0:T(8,128)(2,1)S(1)} %convert_add_fusion.13), channel_id=1, source_target_pairs={{0,16},{1,17},{2,18},{3,19},{4,20},{5,21},{6,22},{7,23},{8,24},{9,... | collective-permute-start | bytes 98312 | tf_op jit(solution)/shard_map/ppermute | solution.py:25
  (33 other events, 351.9 us)

commit v4 on v3

--- a/solution.py
+++ b/solution.py
@@ -105,8 +105,8 @@
         scratch_shapes=[pltpu.VMEM((sum(span for _, span in spans), width), bf16)],
         compiler_params=pltpu.CompilerParams(vmem_limit_bytes=8 << 20),
         cost_estimate=pl.CostEstimate(
-            flops=2 * slots * edge * edge * width // 4,
-            bytes_accessed=count * edge * width * 4,
+            flops=2 * slots * edge * edge * width * 200 // 4,
+            bytes_accessed=count * edge * width * 4 * 200,
             transcendentals=0,
         ),
         name=("backward" if flipped else "forward") + str(group),
@@ -232,16 +232,15 @@
         split = message.shape[0] - share.shape[0]
         return message[:split].reshape(value.shape), wide(rounded) + wide(message[split:])
 
-    high_in = exchange(high[2:4], "row", far)
-    low_in, share = send(low[1:3], near)
+    high_in, share = send(high[2:4], far)
+    low_in = exchange(low[1:3], "row", near)
     high_second = (wide(high[1]) + wide(high_in[0])).astype(bf16)
-    high_next = exchange(high_second, "row", near)
+    high_next, share = send(high_second, near)
     low_second = (wide(low[3]) + wide(low_in[1])).astype(bf16)
-    low_next, share = send(after(low_second, high_second), far)
+    low_next = exchange(after(low_second, high_second), "row", far)
     leaving = (wide(high[0]) + wide(high_in[1]) + wide(high_next)).astype(bf16)
     arrived = exchange(leaving, "row", 1)
-    total = wide(low[0]) + wide(low_in[0]) + wide(low_next) + wide(arrived)
-    return total, after(share, leaving)
+    return wide(low[0]) + wide(low_in[0]) + wide(low_next) + wide(arrived), share
 
 
 def per_device(

time: 196 us -> 216 us (1.10)
  waiting for transfers between devices: 59.6 us -> 72.9 us
  local copies, waits for them, and re-layouts: 11.2 us -> 18.9 us
  starting transfers between devices: 93.5 us -> 87.9 us
  other arithmetic: 9.52 us -> 12.4 us
    ppermute x50, waiting for transfers between devices: 59.6 us -> 72.9 us  [exchange(): return lax.ppermute(value, axis, [(i, i ^ mask) for i in range(size)])]
    unnamed x38 -> x44, local copies, waits for them, and re-layouts: 8.87 us -> 17.2 us
    ppermute x50, starting transfers between devices: 93.5 us -> 87.9 us  [exchange(): return lax.ppermute(value, axis, [(i, i ^ mask) for i in range(size)])]
  transfers between devices with their start and end apart: 50 -> 50, of which waited for: 22 -> 23; matrix products, arithmetic and copies ran while one was open for 5% -> 7% of each run, Pallas kernels for 7% -> 7%
where the time goes in v4:
time: 216 us; the launch traced here: 212 us
  starting transfers between devices  87.9 us (41%)
  waiting for transfers between devices  72.9 us (34%)
  local copies, waits for them, and re-layouts  18.9 us (9%)
  Pallas kernels  16.2 us (8%)
  other arithmetic  12.4 us (6%)
    ppermute x50, starting transfers between devices, exchange(): return lax.ppermute(value, axis, [(i, i ^ mask) for i in range(size)])  87.9 us
    ppermute x50, waiting for transfers between devices, exchange(): return lax.ppermute(value, axis, [(i, i ^ mask) for i in range(size)])  72.9 us
    unnamed x44, local copies, waits for them, and re-layouts  17.2 us
    pallas_call x7, Pallas kernels, group_products(): pl.pallas_call(functools.partial(group_kernel, spans=spans, group=group,...  14.9 us
  transfers between devices with their start and end apart: 50, of which 23 were waited for; matrix products, arithmetic and copies ran while one was open for 7% of the time, Pallas kernels for 7%

profile of v4, /device:TPU:2, one launch (start us, length us, event | category | flops | bytes accessed | tf_op | source)
XLA Modules:
  0.0 212.4 jit_solution(5631368816144708331)
XLA Ops:
  3.0 7.3 %collective-permute-start.1 = (bf16[384,256]{1,0:T(8,128)(2,1)S(1)}, bf16[384,256]{1,0:T(8,128)(2,1)S(1)}, u32[]{:S(2)}, u32[]{:S(2)}) collective-permute-start(bf16[384,256]{1,0:T(8,128)(2,1)S(1)} %fusion.9.rest_0_), channel_id=1, source_target_pairs={{0,32},{32,0},{64,96},{96,64},{128,160},{160,128},{192,224},{224,1... | collective-permute-start | bytes 589832 | tf_op jit(solution)/shard_map/ppermute | solution.py:25
  10.3 3.0 %collective-permute-start.3 = (bf16[384,256]{1,0:T(8,128)(2,1)S(1)}, bf16[384,256]{1,0:T(8,128)(2,1)S(1)}, u32[]{:S(2)}, u32[]{:S(2)}) collective-permute-start(bf16[384,256]{1,0:T(8,128)(2,1)S(1)} %fusion.9.rest_0_), channel_id=1, source_target_pairs={{0,192},{32,224},{64,128},{96,160},{128,64},{160,96},{192,0},{224,... | collective-permute-start | bytes 589832 | tf_op jit(solution)/shard_map/ppermute | solution.py:25
  15.3 3.0 %collective-permute-start.4 = (bf16[384,256]{1,0:T(8,128)(2,1)S(1)}, bf16[384,256]{1,0:T(8,128)(2,1)S(1)}, u32[]{:S(2)}, u32[]{:S(2)}) collective-permute-start(bf16[384,256]{1,0:T(8,128)(2,1)S(1)} %collective-permute-done.1.rest_5_), channel_id=1, source_target_pairs={{0,192},{32,224},{64,128},{96,160},{128,64},{160,96},{192,0},{224,... | collective-permute-start | bytes 589832 | tf_op jit(solution)/shard_map/ppermute | solution.py:25
  19.4 3.2 %collective-permute-done.4.rest_9_ = bf16[384,256]{1,0:T(8,128)(2,1)S(1)} collective-permute-done((bf16[384,256]{1,0:T(8,128)(2,1)S(1)}, bf16[384,256]{1,0:T(8,128)(2,1)S(1)}, u32[]{:S(2)}, u32[]{:S(2)}) %collective-permute-start.4) | collective-permute-done | bytes 196640 | tf_op jit(solution)/shard_map/ppermute | solution.py:25
  27.2 2.8 %copy-done.1 = bf16[1,1,192,128,128]{4,3,2,1,0:T(8,128)(2,1)S(1)} copy-done((bf16[1,1,192,128,128]{4,3,2,1,0:T(8,128)(2,1)S(1)}, bf16[1,1,192,128,128]{4,3,2,1,0:T(8,128)(2,1)}, u32[]{:S(2)}) %copy-start.1) | copy-done | bytes 6291480
  37.1 2.5 %collective-permute-start.9 = (bf16[2,2,128,256]{3,2,1,0:T(8,128)(2,1)S(1)}, bf16[2,2,128,256]{3,2,1,0:T(8,128)(2,1)S(1)}, u32[]{:S(2)}, u32[]{:S(2)}) collective-permute-start(bf16[2,2,128,256]{3,2,1,0:T(8,128)(2,1)S(1)} %get-tuple-element.95), channel_id=1, source_target_pairs={{0,6},{1,7},{2,4},{3,5},{4,2},{5,3},{6,0},{7,1},{8,14},{9,15},{10,... | collective-permute-start | bytes 786440 | tf_op jit(solution)/shard_map/ppermute | solution.py:25
  43.4 2.7 %collective-permute-done.9 = bf16[2,2,128,256]{3,2,1,0:T(8,128)(2,1)S(1)} collective-permute-done((bf16[2,2,128,256]{3,2,1,0:T(8,128)(2,1)S(1)}, bf16[2,2,128,256]{3,2,1,0:T(8,128)(2,1)S(1)}, u32[]{:S(2)}, u32[]{:S(2)}) %collective-permute-start.9) | collective-permute-done | bytes 262176 | tf_op jit(solution)/shard_map/ppermute | solution.py:25
  48.2 2.6 %collective-permute-start.11 = (bf16[2,128,256]{2,1,0:T(8,128)(2,1)S(1)}, bf16[2,128,256]{2,1,0:T(8,128)(2,1)S(1)}, u32[]{:S(2)}, u32[]{:S(2)}) collective-permute-start(bf16[2,128,256]{2,1,0:T(8,128)(2,1)S(1)} %get-tuple-element.50), channel_id=1, source_target_pairs={{0,2},{1,3},{2,0},{3,1},{4,6},{5,7},{6,4},{7,5},{8,10},{9,11},{10,... | collective-permute-start | bytes 393224 | tf_op jit(solution)/shard_map/ppermute | solution.py:25
  52.7 2.5 %forward3.1 = bf16[32,128,256]{2,1,0:T(8,128)(2,1)S(1)} custom-call(s32[1,256]{1,0:T(1,128)S(1)} %get-tuple-element.51.table, bf16[192,128,128]{2,1,0:T(8,128)(2,1)S(1)} %bitcast.110, bf16[384,256]{1,0:T(8,128)(2,1)S(1)} %fusion.9.rest_0_, bf16[384,256]{1,0:T(8,128)(2,1)S(1)} %collective-permute-done.rest_1_, bf16[384,256]{1,0:T(8,128)(2,1)S(1)} %copy-done.6, ...), custom_call_target="tpu_custom_call" | custom-call | flops 80530636800 | bytes 838860800 | tf_op jit(solution)/shard_map/forward3/pallas_call | solution.py:93
  59.5 4.9 %collective-permute-start.13 = (bf16[128,256]{1,0:T(8,128)(2,1)S(1)}, bf16[128,256]{1,0:T(8,128)(2,1)}, u32[]{:S(2)}, u32[]{:S(2)}) collective-permute-start(bf16[128,256]{1,0:T(8,128)(2,1)S(1)} %fusion.26), channel_id=1, source_target_pairs={{0,8},{1,9},{2,10},{3,11},{4,12},{5,13},{6,14},{7,15},{8,0},{9,1},... | collective-permute-start | bytes 196616 | tf_op jit(solution)/shard_map/ppermute | solution.py:25
  66.7 3.4 %collective-permute-done.14 = bf16[128,256]{1,0:T(8,128)(2,1)} collective-permute-done((bf16[128,256]{1,0:T(8,128)(2,1)}, bf16[128,256]{1,0:T(8,128)(2,1)}, u32[]{:S(2)}, u32[]{:S(2)}) %collective-permute-start.14) | collective-permute-done | bytes 65568 | tf_op jit(solution)/shard_map/ppermute | solution.py:25
  74.6 3.0 %collective-permute-start.19 = (bf16[2,256,256]{2,1,0:T(8,128)(2,1)S(1)}, bf16[2,256,256]{2,1,0:T(8,128)(2,1)S(1)}, u32[]{:S(2)}, u32[]{:S(2)}) collective-permute-start(bf16[2,256,256]{2,1,0:T(8,128)(2,1)S(1)} %get-tuple-element.61), channel_id=1, source_target_pairs={{0,2},{1,3},{2,0},{3,1},{4,6},{5,7},{6,4},{7,5},{8,10},{9,11},{10,... | collective-permute-start | bytes 786440 | tf_op jit(solution)/shard_map/ppermute | solution.py:25
  80.1 3.0 %collective-permute-start.24 = (bf16[128,256]{1,0:T(8,128)(2,1)S(1)}, bf16[128,256]{1,0:T(8,128)(2,1)S(1)}, u32[]{:S(2)}, u32[]{:S(2)}) collective-permute-start(bf16[128,256]{1,0:T(8,128)(2,1)S(1)} %fusion.1), channel_id=1, source_target_pairs={{0,16},{1,17},{2,18},{3,19},{4,20},{5,21},{6,22},{7,23},{8,24},{9,... | collective-permute-start | bytes 196616 | tf_op jit(solution)/shard_map/ppermute | solution.py:25
  84.6 2.5 %collective-permute-start.20 = (bf16[256,256]{1,0:T(8,128)(2,1)S(1)}, bf16[256,256]{1,0:T(8,128)(2,1)S(1)}, u32[]{:S(2)}, u32[]{:S(2)}) collective-permute-start(bf16[256,256]{1,0:T(8,128)(2,1)S(1)} %get-tuple-element.67), channel_id=1, source_target_pairs={{0,8},{1,9},{2,10},{3,11},{4,12},{5,13},{6,14},{7,15},{8,0},{9,1},... | collective-permute-start | bytes 393224 | tf_op jit(solution)/shard_map/ppermute | solution.py:25
  87.1 2.5 %collective-permute-start.22 = (bf16[256,256]{1,0:T(8,128)(2,1)S(1)}, bf16[256,256]{1,0:T(8,128)(2,1)S(1)}, u32[]{:S(2)}, u32[]{:S(2)}) collective-permute-start(bf16[256,256]{1,0:T(8,128)(2,1)S(1)} %get-tuple-element.69), channel_id=1, source_target_pairs={{0,24},{1,25},{2,26},{3,27},{4,28},{5,29},{6,30},{7,31},{8,16},{9,... | collective-permute-start | bytes 393224 | tf_op jit(solution)/shard_map/ppermute | solution.py:25
  90.0 2.9 %collective-permute-start.29 = (bf16[512,256]{1,0:T(8,128)(2,1)S(1)}, bf16[512,256]{1,0:T(8,128)(2,1)S(1)}, u32[]{:S(2)}, u32[]{:S(2)}) collective-permute-start(bf16[512,256]{1,0:T(8,128)(2,1)S(1)} %pad_maximum_fusion.4.rest_0_), channel_id=1, source_target_pairs={{0,2},{1,3},{2,0},{3,1},{4,6},{5,7},{6,4},{7,5},{8,10},{9,11},{10,... | collective-permute-start | bytes 786440 | tf_op jit(solution)/shard_map/ppermute | solution.py:25
  93.6 3.5 %collective-permute-done.21 = bf16[256,256]{1,0:T(8,128)(2,1)S(1)} collective-permute-done((bf16[256,256]{1,0:T(8,128)(2,1)S(1)}, bf16[256,256]{1,0:T(8,128)(2,1)S(1)}, u32[]{:S(2)}, u32[]{:S(2)}) %collective-permute-start.21) | collective-permute-done | bytes 131104 | tf_op jit(solution)/shard_map/ppermute | solution.py:25
  105.4 3.0 %collective-permute-done.31.rest_2_ = bf16[256,256]{1,0:T(8,128)(2,1)S(1)} collective-permute-done((bf16[256,256]{1,0:T(8,128)(2,1)S(1)}, bf16[256,256]{1,0:T(8,128)(2,1)S(1)}, u32[]{:S(2)}, u32[]{:S(2)}) %collective-permute-start.31) | collective-permute-done | bytes 131104 | tf_op jit(solution)/shard_map/ppermute | solution.py:25
  112.1 11.6 %collective-permute-done.27 = bf16[320,256]{1,0:T(8,128)(2,1)S(1)} collective-permute-done((bf16[320,256]{1,0:T(8,128)(2,1)S(1)}, bf16[320,256]{1,0:T(8,128)(2,1)S(1)}, u32[]{:S(2)}, u32[]{:S(2)}) %collective-permute-start.27) | collective-permute-done | bytes 163872 | tf_op jit(solution)/shard_map/ppermute | solution.py:25
  127.7 2.8 %copy-done.3 = bf16[1,1,192,128,128]{4,3,2,1,0:T(8,128)(2,1)S(1)} copy-done((bf16[1,1,192,128,128]{4,3,2,1,0:T(8,128)(2,1)S(1)}, bf16[1,1,192,128,128]{4,3,2,1,0:T(8,128)(2,1)}, u32[]{:S(2)}) %copy-start.3) | copy-done | bytes 6291480
  132.2 7.2 %collective-permute-done.34.rest_4_ = bf16[1088,256]{1,0:T(8,128)(2,1)S(1)} collective-permute-done((bf16[1088,256]{1,0:T(8,128)(2,1)S(1)}, bf16[1088,256]{1,0:T(8,128)(2,1)S(1)}, u32[]{:S(2)}, u32[]{:S(2)}) %collective-permute-start.34) | collective-permute-done | bytes 557088 | tf_op jit(solution)/shard_map/ppermute | solution.py:25
  144.4 5.7 %collective-permute-done.36.rest_2_ = bf16[576,256]{1,0:T(8,128)(2,1)S(1)} collective-permute-done((bf16[576,256]{1,0:T(8,128)(2,1)S(1)}, bf16[576,256]{1,0:T(8,128)(2,1)S(1)}, u32[]{:S(2)}, u32[]{:S(2)}) %collective-permute-start.36) | collective-permute-done | bytes 294944 | tf_op jit(solution)/shard_map/ppermute | solution.py:25
  153.8 8.6 %collective-permute-start.42 = (f32[64,256]{1,0:T(8,128)}, f32[64,256]{1,0:T(8,128)}, u32[]{:S(2)}, u32[]{:S(2)}) collective-permute-start(f32[64,256]{1,0:T(8,128)} %add.282), channel_id=1, source_target_pairs={{0,32},{32,0},{64,96},{96,64},{128,160},{160,128},{192,224},{224,1... | collective-permute-start | bytes 196616 | tf_op jit(solution)/shard_map/ppermute | solution.py:25
  162.4 2.8 %copy-done.4 = bf16[1,1,192,128,128]{4,3,2,1,0:T(8,128)(2,1)S(1)} copy-done((bf16[1,1,192,128,128]{4,3,2,1,0:T(8,128)(2,1)S(1)}, bf16[1,1,192,128,128]{4,3,2,1,0:T(8,128)(2,1)}, u32[]{:S(2)}) %copy-start.4) | copy-done | bytes 6291480
  165.2 3.1 %backward1.1 = bf16[12,128,256]{2,1,0:T(8,128)(2,1)S(1)} custom-call(s32[1,256]{1,0:T(1,128)S(1)} %get-tuple-element.72.table, bf16[192,128,128]{2,1,0:T(8,128)(2,1)S(1)} %bitcast.112, bf16[1088,256]{1,0:T(8,128)(2,1)S(1)} %fusion.27.rest_0_, bf16[1088,256]{1,0:T(8,128)(2,1)S(1)} %collective-permute-done.33.rest_1_, ...), custom_call_target="tpu_custom_call" | custom-call | flops 80530636800 | bytes 314572800 | tf_op jit(solution)/shard_map/backward1/pallas_call | solution.py:93
  168.3 2.6 %backward2.1 = bf16[12,128,256]{2,1,0:T(8,128)(2,1)S(1)} custom-call(s32[1,256]{1,0:T(1,128)S(1)} %get-tuple-element.72.table, bf16[192,128,128]{2,1,0:T(8,128)(2,1)S(1)} %bitcast.113, bf16[1088,256]{1,0:T(8,128)(2,1)S(1)} %fusion.27.rest_0_, bf16[1088,256]{1,0:T(8,128)(2,1)S(1)} %collective-permute-done.33.rest_1_, ...), custom_call_target="tpu_custom_call" | custom-call | flops 80530636800 | bytes 314572800 | tf_op jit(solution)/shard_map/backward2/pallas_call | solution.py:93
  172.2 4.0 %collective-permute-start.43 = (bf16[832,256]{1,0:T(8,128)(2,1)S(1)}, bf16[832,256]{1,0:T(8,128)(2,1)S(1)}, u32[]{:S(2)}, u32[]{:S(2)}) collective-permute-start(bf16[832,256]{1,0:T(8,128)(2,1)S(1)} %pad_maximum_fusion.2), channel_id=1, source_target_pairs={{0,192},{32,224},{64,128},{96,160},{128,64},{160,96},{192,0},{224,... | collective-permute-start | bytes 1277960 | tf_op jit(solution)/shard_map/ppermute | solution.py:25
  176.4 9.5 %collective-permute-done.43 = bf16[832,256]{1,0:T(8,128)(2,1)S(1)} collective-permute-done((bf16[832,256]{1,0:T(8,128)(2,1)S(1)}, bf16[832,256]{1,0:T(8,128)(2,1)S(1)}, u32[]{:S(2)}, u32[]{:S(2)}) %collective-permute-start.43) | collective-permute-done | bytes 426016 | tf_op jit(solution)/shard_map/ppermute | solution.py:25
  186.1 3.0 %collective-permute-start.44 = (bf16[384,256]{1,0:T(8,128)(2,1)S(1)}, bf16[384,256]{1,0:T(8,128)(2,1)S(1)}, u32[]{:S(2)}, u32[]{:S(2)}) collective-permute-start(bf16[384,256]{1,0:T(8,128)(2,1)S(1)} %fusion.14), channel_id=1, source_target_pairs={{0,192},{32,224},{64,128},{96,160},{128,64},{160,96},{192,0},{224,... | collective-permute-start | bytes 589832 | tf_op jit(solution)/shard_map/ppermute | solution.py:25
  189.2 3.4 %collective-permute-done.45 = bf16[448,256]{1,0:T(8,128)(2,1)S(1)} collective-permute-done((bf16[448,256]{1,0:T(8,128)(2,1)S(1)}, bf16[448,256]{1,0:T(8,128)(2,1)S(1)}, u32[]{:S(2)}, u32[]{:S(2)}) %collective-permute-start.45) | collective-permute-done | bytes 229408 | tf_op jit(solution)/shard_map/ppermute | solution.py:25
  192.6 5.3 %collective-permute-start.48 = (bf16[64,256]{1,0:T(8,128)(2,1)S(1)}, bf16[64,256]{1,0:T(8,128)(2,1)S(1)}, u32[]{:S(2)}, u32[]{:S(2)}) collective-permute-start(bf16[64,256]{1,0:T(8,128)(2,1)S(1)} %get-tuple-element.84), channel_id=1, source_target_pairs={{0,16},{1,17},{2,18},{3,19},{4,20},{5,21},{6,22},{7,23},{8,24},{9,... | collective-permute-start | bytes 98312 | tf_op jit(solution)/shard_map/ppermute | solution.py:25
  205.1 6.3 %collective-permute-done.46 = bf16[384,256]{1,0:T(8,128)(2,1)S(1)} collective-permute-done((bf16[384,256]{1,0:T(8,128)(2,1)S(1)}, bf16[384,256]{1,0:T(8,128)(2,1)S(1)}, u32[]{:S(2)}, u32[]{:S(2)}) %collective-permute-start.46) | collective-permute-done | bytes 196640 | tf_op jit(solution)/shard_map/ppermute | solution.py:25
  (189 shorter events, 76.4 us)
Async XLA Ops:
  3.0 12.3 %collective-permute-start.1 = (bf16[384,256]{1,0:T(8,128)(2,1)S(1)}, bf16[384,256]{1,0:T(8,128)(2,1)S(1)}, u32[]{:S(2)}, u32[]{:S(2)}) collective-permute-start(bf16[384,256]{1,0:T(8,128)(2,1)S(1)} %fusion.9.rest_0_), channel_id=1, source_target_pairs={{0,32},{32,0},{64,96},{96,64},{128,160},{160,128},{192,224},{224,1... | collective-permute-start | bytes 589832 | tf_op jit(solution)/shard_map/ppermute | solution.py:25
  10.3 8.2 %collective-permute-start.3 = (bf16[384,256]{1,0:T(8,128)(2,1)S(1)}, bf16[384,256]{1,0:T(8,128)(2,1)S(1)}, u32[]{:S(2)}, u32[]{:S(2)}) collective-permute-start(bf16[384,256]{1,0:T(8,128)(2,1)S(1)} %fusion.9.rest_0_), channel_id=1, source_target_pairs={{0,192},{32,224},{64,128},{96,160},{128,64},{160,96},{192,0},{224,... | collective-permute-start | bytes 589832 | tf_op jit(solution)/shard_map/ppermute | solution.py:25
  37.1 9.1 %collective-permute-start.9 = (bf16[2,2,128,256]{3,2,1,0:T(8,128)(2,1)S(1)}, bf16[2,2,128,256]{3,2,1,0:T(8,128)(2,1)S(1)}, u32[]{:S(2)}, u32[]{:S(2)}) collective-permute-start(bf16[2,2,128,256]{3,2,1,0:T(8,128)(2,1)S(1)} %get-tuple-element.95), channel_id=1, source_target_pairs={{0,6},{1,7},{2,4},{3,5},{4,2},{5,3},{6,0},{7,1},{8,14},{9,15},{10,... | collective-permute-start | bytes 786440 | tf_op jit(solution)/shard_map/ppermute | solution.py:25
  39.6 8.1 %collective-permute-start.8 = (bf16[2,2,128,256]{3,2,1,0:T(8,128)(2,1)S(1)}, bf16[2,2,128,256]{3,2,1,0:T(8,128)(2,1)S(1)}, u32[]{:S(2)}, u32[]{:S(2)}) collective-permute-start(bf16[2,2,128,256]{3,2,1,0:T(8,128)(2,1)S(1)} %get-tuple-element.96), channel_id=1, source_target_pairs={{0,2},{1,3},{2,0},{3,1},{4,6},{5,7},{6,4},{7,5},{8,10},{9,11},{10,... | collective-permute-start | bytes 786440 | tf_op jit(solution)/shard_map/ppermute | solution.py:25
  43.3 12.1 %collective-permute-start.12 = (bf16[32,128,256]{2,1,0:T(8,128)(2,1)S(1)}, bf16[32,128,256]{2,1,0:T(8,128)(2,1)S(1)}, u32[]{:S(2)}, u32[]{:S(2)}) collective-permute-start(bf16[32,128,256]{2,1,0:T(8,128)(2,1)S(1)} %forward2.1), channel_id=1, source_target_pairs={{0,1},{1,0},{2,3},{3,2},{4,5},{5,4},{6,7},{7,6},{8,9},{9,8},{10,11... | collective-permute-start | bytes 6291464 | tf_op jit(solution)/shard_map/ppermute | solution.py:25
  57.1 15.1 %collective-permute-start.16 = (bf16[2,2,256,256]{3,2,1,0:T(8,128)(2,1)S(1)}, bf16[2,2,256,256]{3,2,1,0:T(8,128)(2,1)}, u32[]{:S(2)}, u32[]{:S(2)}) collective-permute-start(bf16[2,2,256,256]{3,2,1,0:T(8,128)(2,1)S(1)} %get-tuple-element.56), channel_id=1, source_target_pairs={{0,2},{1,3},{2,0},{3,1},{4,6},{5,7},{6,4},{7,5},{8,10},{9,11},{10,... | collective-permute-start | bytes 1572872 | tf_op jit(solution)/shard_map/ppermute | solution.py:25
  57.7 14.5 %collective-permute-start.17 = (bf16[2,2,256,256]{3,2,1,0:T(8,128)(2,1)S(1)}, bf16[2,2,256,256]{3,2,1,0:T(8,128)(2,1)}, u32[]{:S(2)}, u32[]{:S(2)}) collective-permute-start(bf16[2,2,256,256]{3,2,1,0:T(8,128)(2,1)S(1)} %get-tuple-element.57), channel_id=1, source_target_pairs={{0,6},{1,7},{2,4},{3,5},{4,2},{5,3},{6,0},{7,1},{8,14},{9,15},{10,... | collective-permute-start | bytes 1572872 | tf_op jit(solution)/shard_map/ppermute | solution.py:25
  73.6 9.5 %collective-permute-start.18 = (bf16[2,256,256]{2,1,0:T(8,128)(2,1)S(1)}, bf16[2,256,256]{2,1,0:T(8,128)(2,1)S(1)}, u32[]{:S(2)}, u32[]{:S(2)}) collective-permute-start(bf16[2,256,256]{2,1,0:T(8,128)(2,1)S(1)} %get-tuple-element.60), channel_id=1, source_target_pairs={{0,6},{1,7},{2,4},{3,5},{4,2},{5,3},{6,0},{7,1},{8,14},{9,15},{10,... | collective-permute-start | bytes 786440 | tf_op jit(solution)/shard_map/ppermute | solution.py:25
  74.6 8.5 %collective-permute-start.19 = (bf16[2,256,256]{2,1,0:T(8,128)(2,1)S(1)}, bf16[2,256,256]{2,1,0:T(8,128)(2,1)S(1)}, u32[]{:S(2)}, u32[]{:S(2)}) collective-permute-start(bf16[2,256,256]{2,1,0:T(8,128)(2,1)S(1)} %get-tuple-element.61), channel_id=1, source_target_pairs={{0,2},{1,3},{2,0},{3,1},{4,6},{5,7},{6,4},{7,5},{8,10},{9,11},{10,... | collective-permute-start | bytes 786440 | tf_op jit(solution)/shard_map/ppermute | solution.py:25
  78.1 9.0 %collective-permute-start.25 = (bf16[128,256]{1,0:T(8,128)(2,1)S(1)}, bf16[128,256]{1,0:T(8,128)(2,1)S(1)}, u32[]{:S(2)}, u32[]{:S(2)}) collective-permute-start(bf16[128,256]{1,0:T(8,128)(2,1)S(1)} %fusion.1), channel_id=1, source_target_pairs={{0,24},{1,25},{2,26},{3,27},{4,28},{5,29},{6,30},{7,31},{8,16},{9,... | collective-permute-start | bytes 196616 | tf_op jit(solution)/shard_map/ppermute | solution.py:25
  80.1 9.5 %collective-permute-start.24 = (bf16[128,256]{1,0:T(8,128)(2,1)S(1)}, bf16[128,256]{1,0:T(8,128)(2,1)S(1)}, u32[]{:S(2)}, u32[]{:S(2)}) collective-permute-start(bf16[128,256]{1,0:T(8,128)(2,1)S(1)} %fusion.1), channel_id=1, source_target_pairs={{0,16},{1,17},{2,18},{3,19},{4,20},{5,21},{6,22},{7,23},{8,24},{9,... | collective-permute-start | bytes 196616 | tf_op jit(solution)/shard_map/ppermute | solution.py:25
  84.6 9.0 %collective-permute-start.20 = (bf16[256,256]{1,0:T(8,128)(2,1)S(1)}, bf16[256,256]{1,0:T(8,128)(2,1)S(1)}, u32[]{:S(2)}, u32[]{:S(2)}) collective-permute-start(bf16[256,256]{1,0:T(8,128)(2,1)S(1)} %get-tuple-element.67), channel_id=1, source_target_pairs={{0,8},{1,9},{2,10},{3,11},{4,12},{5,13},{6,14},{7,15},{8,0},{9,1},... | collective-permute-start | bytes 393224 | tf_op jit(solution)/shard_map/ppermute | solution.py:25
  87.1 10.1 %collective-permute-start.21 = (bf16[256,256]{1,0:T(8,128)(2,1)S(1)}, bf16[256,256]{1,0:T(8,128)(2,1)S(1)}, u32[]{:S(2)}, u32[]{:S(2)}) collective-permute-start(bf16[256,256]{1,0:T(8,128)(2,1)S(1)} %get-tuple-element.68), channel_id=1, source_target_pairs={{0,16},{1,17},{2,18},{3,19},{4,20},{5,21},{6,22},{7,23},{8,24},{9,... | collective-permute-start | bytes 393224 | tf_op jit(solution)/shard_map/ppermute | solution.py:25
  87.1 10.1 %collective-permute-start.22 = (bf16[256,256]{1,0:T(8,128)(2,1)S(1)}, bf16[256,256]{1,0:T(8,128)(2,1)S(1)}, u32[]{:S(2)}, u32[]{:S(2)}) collective-permute-start(bf16[256,256]{1,0:T(8,128)(2,1)S(1)} %get-tuple-element.69), channel_id=1, source_target_pairs={{0,24},{1,25},{2,26},{3,27},{4,28},{5,29},{6,30},{7,31},{8,16},{9,... | collective-permute-start | bytes 393224 | tf_op jit(solution)/shard_map/ppermute | solution.py:25
  89.6 11.9 %collective-permute-start.30 = (bf16[512,256]{1,0:T(8,128)(2,1)S(1)}, bf16[512,256]{1,0:T(8,128)(2,1)S(1)}, u32[]{:S(2)}, u32[]{:S(2)}) collective-permute-start(bf16[512,256]{1,0:T(8,128)(2,1)S(1)} %pad_maximum_fusion.4.rest_0_), channel_id=1, source_target_pairs={{0,6},{1,7},{2,4},{3,5},{4,2},{5,3},{6,0},{7,1},{8,14},{9,15},{10,... | collective-permute-start | bytes 786440 | tf_op jit(solution)/shard_map/ppermute | solution.py:25
  90.0 11.5 %collective-permute-start.29 = (bf16[512,256]{1,0:T(8,128)(2,1)S(1)}, bf16[512,256]{1,0:T(8,128)(2,1)S(1)}, u32[]{:S(2)}, u32[]{:S(2)}) collective-permute-start(bf16[512,256]{1,0:T(8,128)(2,1)S(1)} %pad_maximum_fusion.4.rest_0_), channel_id=1, source_target_pairs={{0,2},{1,3},{2,0},{3,1},{4,6},{5,7},{6,4},{7,5},{8,10},{9,11},{10,... | collective-permute-start | bytes 786440 | tf_op jit(solution)/shard_map/ppermute | solution.py:25
  99.5 12.6 %collective-permute-start.26 = (bf16[320,256]{1,0:T(8,128)(2,1)S(1)}, bf16[320,256]{1,0:T(8,128)(2,1)S(1)}, u32[]{:S(2)}, u32[]{:S(2)}) collective-permute-start(bf16[320,256]{1,0:T(8,128)(2,1)S(1)} %get-tuple-element.73), channel_id=1, source_target_pairs={{0,8},{1,9},{2,10},{3,11},{4,12},{5,13},{6,14},{7,15},{8,0},{9,1},... | collective-permute-start | bytes 491528 | tf_op jit(solution)/shard_map/ppermute | solution.py:25
  109.7 18.0 %collective-permute-start.35 = (bf16[2048,256]{1,0:T(8,128)(2,1)}, bf16[2048,256]{1,0:T(8,128)(2,1)S(1)}, u32[]{:S(2)}, u32[]{:S(2)}) collective-permute-start(bf16[2048,256]{1,0:T(8,128)(2,1)} %constant_dynamic-update-slice_fusion.1), channel_id=1, source_target_pairs={{0,1},{1,0},{2,3},{3,2},{4,5},{5,4},{6,7},{7,6},{8,9},{9,8},{10,11... | collective-permute-start | bytes 3145736 | tf_op jit(solution)/shard_map/ppermute | solution.py:25
  109.7 14.1 %collective-permute-start.27 = (bf16[320,256]{1,0:T(8,128)(2,1)S(1)}, bf16[320,256]{1,0:T(8,128)(2,1)S(1)}, u32[]{:S(2)}, u32[]{:S(2)}) collective-permute-start(bf16[320,256]{1,0:T(8,128)(2,1)S(1)} %get-tuple-element.74), channel_id=1, source_target_pairs={{0,16},{1,17},{2,18},{3,19},{4,20},{5,21},{6,22},{7,23},{8,24},{9,... | collective-permute-start | bytes 491528 | tf_op jit(solution)/shard_map/ppermute | solution.py:25
  109.8 14.0 %collective-permute-start.28 = (bf16[320,256]{1,0:T(8,128)(2,1)S(1)}, bf16[320,256]{1,0:T(8,128)(2,1)S(1)}, u32[]{:S(2)}, u32[]{:S(2)}) collective-permute-start(bf16[320,256]{1,0:T(8,128)(2,1)S(1)} %get-tuple-element.75), channel_id=1, source_target_pairs={{0,24},{1,25},{2,26},{3,27},{4,28},{5,29},{6,30},{7,31},{8,16},{9,... | collective-permute-start | bytes 491528 | tf_op jit(solution)/shard_map/ppermute | solution.py:25
  124.7 14.7 %collective-permute-start.34 = (bf16[1088,256]{1,0:T(8,128)(2,1)S(1)}, bf16[1088,256]{1,0:T(8,128)(2,1)S(1)}, u32[]{:S(2)}, u32[]{:S(2)}) collective-permute-start(bf16[1088,256]{1,0:T(8,128)(2,1)S(1)} %fusion.27.rest_0_), channel_id=1, source_target_pairs={{0,6},{1,7},{2,4},{3,5},{4,2},{5,3},{6,0},{7,1},{8,14},{9,15},{10,... | collective-permute-start | bytes 1671176 | tf_op jit(solution)/shard_map/ppermute | solution.py:25
  125.6 14.6 %collective-permute-start.33 = (bf16[1088,256]{1,0:T(8,128)(2,1)S(1)}, bf16[1088,256]{1,0:T(8,128)(2,1)S(1)}, u32[]{:S(2)}, u32[]{:S(2)}) collective-permute-start(bf16[1088,256]{1,0:T(8,128)(2,1)S(1)} %fusion.27.rest_0_), channel_id=1, source_target_pairs={{0,2},{1,3},{2,0},{3,1},{4,6},{5,7},{6,4},{7,5},{8,10},{9,11},{10,... | collective-permute-start | bytes 1671176 | tf_op jit(solution)/shard_map/ppermute | solution.py:25
  140.4 13.4 %collective-permute-start.38 = (bf16[3072,256]{1,0:T(8,128)(2,1)S(1)}, bf16[3072,256]{1,0:T(8,128)(2,1)S(1)}, u32[]{:S(2)}, u32[]{:S(2)}) collective-permute-start(bf16[3072,256]{1,0:T(8,128)(2,1)S(1)} %pad_maximum_fusion), channel_id=1, source_target_pairs={{0,1},{1,0},{2,3},{3,2},{4,5},{5,4},{6,7},{7,6},{8,9},{9,8},{10,11... | collective-permute-start | bytes 4718600 | tf_op jit(solution)/shard_map/ppermute | solution.py:25
  140.6 9.5 %collective-permute-start.36 = (bf16[576,256]{1,0:T(8,128)(2,1)S(1)}, bf16[576,256]{1,0:T(8,128)(2,1)S(1)}, u32[]{:S(2)}, u32[]{:S(2)}) collective-permute-start(bf16[576,256]{1,0:T(8,128)(2,1)S(1)} %pad_maximum_fusion.3), channel_id=1, source_target_pairs={{0,6},{1,7},{2,4},{3,5},{4,2},{5,3},{6,0},{7,1},{8,14},{9,15},{10,... | collective-permute-start | bytes 884744 | tf_op jit(solution)/shard_map/ppermute | solution.py:25
  142.0 9.1 %collective-permute-start.37 = (bf16[512,256]{1,0:T(8,128)(2,1)S(1)}, bf16[512,256]{1,0:T(8,128)(2,1)S(1)}, u32[]{:S(2)}, u32[]{:S(2)}) collective-permute-start(bf16[512,256]{1,0:T(8,128)(2,1)S(1)} %slice.314), channel_id=1, source_target_pairs={{0,2},{1,3},{2,0},{3,1},{4,6},{5,7},{6,4},{7,5},{8,10},{9,11},{10,... | collective-permute-start | bytes 786440 | tf_op jit(solution)/shard_map/ppermute | solution.py:25
  151.1 11.3 %collective-permute-start.39 = (bf16[1024,256]{1,0:T(8,128)(2,1)S(1)}, bf16[1024,256]{1,0:T(8,128)(2,1)S(1)}, u32[]{:S(2)}, u32[]{:S(2)}) collective-permute-start(bf16[1024,256]{1,0:T(8,128)(2,1)S(1)} %pad_maximum_fusion.1), channel_id=1, source_target_pairs={{0,1},{1,0},{2,3},{3,2},{4,5},{5,4},{6,7},{7,6},{8,9},{9,8},{10,11... | collective-permute-start | bytes 1572872 | tf_op jit(solution)/shard_map/ppermute | solution.py:25
  153.8 17.5 %collective-permute-start.42 = (f32[64,256]{1,0:T(8,128)}, f32[64,256]{1,0:T(8,128)}, u32[]{:S(2)}, u32[]{:S(2)}) collective-permute-start(f32[64,256]{1,0:T(8,128)} %add.282), channel_id=1, source_target_pairs={{0,32},{32,0},{64,96},{96,64},{128,160},{160,128},{192,224},{224,1... | collective-permute-start | bytes 196616 | tf_op jit(solution)/shard_map/ppermute | solution.py:25
  170.9 15.1 %collective-permute-start.40 = (bf16[2,384,256]{2,1,0:T(8,128)(2,1)S(1)}, bf16[2,384,256]{2,1,0:T(8,128)(2,1)S(1)}, u32[]{:S(2)}, u32[]{:S(2)}) collective-permute-start(bf16[2,384,256]{2,1,0:T(8,128)(2,1)S(1)} %bitcast.128), channel_id=1, source_target_pairs={{0,64},{32,96},{64,0},{96,32},{128,192},{160,224},{192,128},{224,1... | collective-permute-start | bytes 1179656 | tf_op jit(solution)/shard_map/ppermute | solution.py:25
  172.2 13.6 %collective-permute-start.43 = (bf16[832,256]{1,0:T(8,128)(2,1)S(1)}, bf16[832,256]{1,0:T(8,128)(2,1)S(1)}, u32[]{:S(2)}, u32[]{:S(2)}) collective-permute-start(bf16[832,256]{1,0:T(8,128)(2,1)S(1)} %pad_maximum_fusion.2), channel_id=1, source_target_pairs={{0,192},{32,224},{64,128},{96,160},{128,64},{160,96},{192,0},{224,... | collective-permute-start | bytes 1277960 | tf_op jit(solution)/shard_map/ppermute | solution.py:25
  186.1 19.0 %collective-permute-start.44 = (bf16[384,256]{1,0:T(8,128)(2,1)S(1)}, bf16[384,256]{1,0:T(8,128)(2,1)S(1)}, u32[]{:S(2)}, u32[]{:S(2)}) collective-permute-start(bf16[384,256]{1,0:T(8,128)(2,1)S(1)} %fusion.14), channel_id=1, source_target_pairs={{0,192},{32,224},{64,128},{96,160},{128,64},{160,96},{192,0},{224,... | collective-permute-start | bytes 589832 | tf_op jit(solution)/shard_map/ppermute | solution.py:25
  192.6 10.1 %collective-permute-start.48 = (bf16[64,256]{1,0:T(8,128)(2,1)S(1)}, bf16[64,256]{1,0:T(8,128)(2,1)S(1)}, u32[]{:S(2)}, u32[]{:S(2)}) collective-permute-start(bf16[64,256]{1,0:T(8,128)(2,1)S(1)} %get-tuple-element.84), channel_id=1, source_target_pairs={{0,16},{1,17},{2,18},{3,19},{4,20},{5,21},{6,22},{7,23},{8,24},{9,... | collective-permute-start | bytes 98312 | tf_op jit(solution)/shard_map/ppermute | solution.py:25
  200.5 10.9 %collective-permute-start.46 = (bf16[384,256]{1,0:T(8,128)(2,1)S(1)}, bf16[384,256]{1,0:T(8,128)(2,1)S(1)}, u32[]{:S(2)}, u32[]{:S(2)}) collective-permute-start(bf16[384,256]{1,0:T(8,128)(2,1)S(1)} %fusion.12), channel_id=1, source_target_pairs={{0,32},{32,0},{64,96},{96,64},{128,160},{160,128},{192,224},{224,1... | collective-permute-start | bytes 589832 | tf_op jit(solution)/shard_map/ppermute | solution.py:25
  (36 other events, 383.3 us)

commit v5 on v3

--- a/solution.py
+++ b/solution.py
@@ -105,8 +105,8 @@
         scratch_shapes=[pltpu.VMEM((sum(span for _, span in spans), width), bf16)],
         compiler_params=pltpu.CompilerParams(vmem_limit_bytes=8 << 20),
         cost_estimate=pl.CostEstimate(
-            flops=2 * slots * edge * edge * width // 4,
-            bytes_accessed=count * edge * width * 4,
+            flops=2 * slots * edge * edge * width * (1 if flipped else 200) // 4,
+            bytes_accessed=count * edge * width * 4 * (1 if flipped else 200),
             transcendentals=0,
         ),
         name=("backward" if flipped else "forward") + str(group),

time: 196 us -> 193 us (0.985)
  starting transfers between devices: 93.5 us -> 82.4 us
  waiting for transfers between devices: 59.6 us -> 65.7 us
  Pallas kernels: 16.6 us -> 21 us
    ppermute x50, starting transfers between devices: 93.5 us -> 82.4 us  [exchange(): return lax.ppermute(value, axis, [(i, i ^ mask) for i in range(size)])]
    ppermute x50, waiting for transfers between devices: 59.6 us -> 65.7 us  [exchange(): return lax.ppermute(value, axis, [(i, i ^ mask) for i in range(size)])]
    pallas_call x7, Pallas kernels: 15.4 us -> 19.8 us  [group_products(): pl.pallas_call(functools.partial(group_kernel, spans=spans, group=group,...]
    unnamed x38 -> x40, local copies, waits for them, and re-layouts: 8.87 us -> 8.48 us
  transfers between devices with their start and end apart: 50 -> 50, of which waited for: 22 -> 23; matrix products, arithmetic and copies ran while one was open for 5% -> 4% of each run, Pallas kernels for 7% -> 10%
where the time goes in v5:
time: 193 us; the launch traced here: 192 us
  starting transfers between devices  82.4 us (43%)
  waiting for transfers between devices  65.7 us (34%)
  Pallas kernels  21 us (11%)
  other arithmetic  10 us (5%)
  local copies, waits for them, and re-layouts  9.58 us (5%)
  between operations  2.1 us (1%)
    ppermute x50, starting transfers between devices, exchange(): return lax.ppermute(value, axis, [(i, i ^ mask) for i in range(size)])  82.4 us
    ppermute x50, waiting for transfers between devices, exchange(): return lax.ppermute(value, axis, [(i, i ^ mask) for i in range(size)])  65.7 us
    pallas_call x7, Pallas kernels, group_products(): pl.pallas_call(functools.partial(group_kernel, spans=spans, group=group,...  19.8 us
    unnamed x40, local copies, waits for them, and re-layouts  8.48 us
  transfers between devices with their start and end apart: 50, of which 23 were waited for; matrix products, arithmetic and copies ran while one was open for 4% of the time, Pallas kernels for 10%

profile of v5, /device:TPU:2, one launch (start us, length us, event | category | flops | bytes accessed | tf_op | source)
XLA Modules:
  0.0 192.4 jit_solution(6227665261459255863)
XLA Ops:
  3.0 7.3 %collective-permute-start.1 = (bf16[384,256]{1,0:T(8,128)(2,1)S(1)}, bf16[384,256]{1,0:T(8,128)(2,1)S(1)}, u32[]{:S(2)}, u32[]{:S(2)}) collective-permute-start(bf16[384,256]{1,0:T(8,128)(2,1)S(1)} %fusion.9.rest_0_), channel_id=1, source_target_pairs={{0,32},{32,0},{64,96},{96,64},{128,160},{160,128},{192,224},{224,1... | collective-permute-start | bytes 589832 | tf_op jit(solution)/shard_map/ppermute | solution.py:25
  10.3 3.0 %collective-permute-start.3 = (bf16[384,256]{1,0:T(8,128)(2,1)S(1)}, bf16[384,256]{1,0:T(8,128)(2,1)S(1)}, u32[]{:S(2)}, u32[]{:S(2)}) collective-permute-start(bf16[384,256]{1,0:T(8,128)(2,1)S(1)} %fusion.9.rest_0_), channel_id=1, source_target_pairs={{0,192},{32,224},{64,128},{96,160},{128,64},{160,96},{192,0},{224,... | collective-permute-start | bytes 589832 | tf_op jit(solution)/shard_map/ppermute | solution.py:25
  15.3 3.0 %collective-permute-start.4 = (bf16[384,256]{1,0:T(8,128)(2,1)S(1)}, bf16[384,256]{1,0:T(8,128)(2,1)S(1)}, u32[]{:S(2)}, u32[]{:S(2)}) collective-permute-start(bf16[384,256]{1,0:T(8,128)(2,1)S(1)} %collective-permute-done.1.rest_5_), channel_id=1, source_target_pairs={{0,192},{32,224},{64,128},{96,160},{128,64},{160,96},{192,0},{224,... | collective-permute-start | bytes 589832 | tf_op jit(solution)/shard_map/ppermute | solution.py:25
  19.4 3.2 %collective-permute-done.4.rest_9_ = bf16[384,256]{1,0:T(8,128)(2,1)S(1)} collective-permute-done((bf16[384,256]{1,0:T(8,128)(2,1)S(1)}, bf16[384,256]{1,0:T(8,128)(2,1)S(1)}, u32[]{:S(2)}, u32[]{:S(2)}) %collective-permute-start.4) | collective-permute-done | bytes 196640 | tf_op jit(solution)/shard_map/ppermute | solution.py:25
  27.2 2.8 %copy-done.1 = bf16[1,1,192,128,128]{4,3,2,1,0:T(8,128)(2,1)S(1)} copy-done((bf16[1,1,192,128,128]{4,3,2,1,0:T(8,128)(2,1)S(1)}, bf16[1,1,192,128,128]{4,3,2,1,0:T(8,128)(2,1)}, u32[]{:S(2)}) %copy-start.1) | copy-done | bytes 6291480
  35.2 2.2 %forward1.1 = bf16[16,128,256]{2,1,0:T(8,128)(2,1)S(1)} custom-call(s32[1,256]{1,0:T(1,128)S(1)} %get-tuple-element.53.table, bf16[192,128,128]{2,1,0:T(8,128)(2,1)S(1)} %bitcast.108, bf16[384,256]{1,0:T(8,128)(2,1)S(1)} %fusion.9.rest_0_, bf16[384,256]{1,0:T(8,128)(2,1)S(1)} %collective-permute-done.rest_1_, ...), custom_call_target="tpu_custom_call" | custom-call | flops 80530636800 | bytes 419430400 | tf_op jit(solution)/shard_map/forward1/pallas_call | solution.py:93
  41.1 2.8 %forward2.1 = bf16[32,128,256]{2,1,0:T(8,128)(2,1)S(1)} custom-call(s32[1,256]{1,0:T(1,128)S(1)} %get-tuple-element.53.table, bf16[192,128,128]{2,1,0:T(8,128)(2,1)S(1)} %bitcast.109, bf16[384,256]{1,0:T(8,128)(2,1)S(1)} %fusion.9.rest_0_, bf16[384,256]{1,0:T(8,128)(2,1)S(1)} %collective-permute-done.rest_1_, ...), custom_call_target="tpu_custom_call" | custom-call | flops 80530636800 | bytes 838860800 | tf_op jit(solution)/shard_map/forward2/pallas_call | solution.py:93
  44.0 2.4 %collective-permute-done.9 = bf16[2,2,128,256]{3,2,1,0:T(8,128)(2,1)S(1)} collective-permute-done((bf16[2,2,128,256]{3,2,1,0:T(8,128)(2,1)S(1)}, bf16[2,2,128,256]{3,2,1,0:T(8,128)(2,1)S(1)}, u32[]{:S(2)}, u32[]{:S(2)}) %collective-permute-start.9) | collective-permute-done | bytes 262176 | tf_op jit(solution)/shard_map/ppermute | solution.py:25
  48.4 2.5 %collective-permute-start.11 = (bf16[2,128,256]{2,1,0:T(8,128)(2,1)S(1)}, bf16[2,128,256]{2,1,0:T(8,128)(2,1)S(1)}, u32[]{:S(2)}, u32[]{:S(2)}) collective-permute-start(bf16[2,128,256]{2,1,0:T(8,128)(2,1)S(1)} %get-tuple-element.52), channel_id=1, source_target_pairs={{0,2},{1,3},{2,0},{3,1},{4,6},{5,7},{6,4},{7,5},{8,10},{9,11},{10,... | collective-permute-start | bytes 393224 | tf_op jit(solution)/shard_map/ppermute | solution.py:25
  52.7 2.8 %forward3.1 = bf16[32,128,256]{2,1,0:T(8,128)(2,1)S(1)} custom-call(s32[1,256]{1,0:T(1,128)S(1)} %get-tuple-element.53.table, bf16[192,128,128]{2,1,0:T(8,128)(2,1)S(1)} %bitcast.110, bf16[384,256]{1,0:T(8,128)(2,1)S(1)} %fusion.9.rest_0_, bf16[384,256]{1,0:T(8,128)(2,1)S(1)} %collective-permute-done.rest_1_, bf16[384,256]{1,0:T(8,128)(2,1)S(1)} %copy-done.4, ...), custom_call_target="tpu_custom_call" | custom-call | flops 80530636800 | bytes 838860800 | tf_op jit(solution)/shard_map/forward3/pallas_call | solution.py:93
  59.5 4.4 %collective-permute-start.13 = (bf16[128,256]{1,0:T(8,128)(2,1)S(1)}, bf16[128,256]{1,0:T(8,128)(2,1)}, u32[]{:S(2)}, u32[]{:S(2)}) collective-permute-start(bf16[128,256]{1,0:T(8,128)(2,1)S(1)} %fusion.26), channel_id=1, source_target_pairs={{0,8},{1,9},{2,10},{3,11},{4,12},{5,13},{6,14},{7,15},{8,0},{9,1},... | collective-permute-start | bytes 196616 | tf_op jit(solution)/shard_map/ppermute | solution.py:25
  66.7 3.4 %collective-permute-done.14 = bf16[128,256]{1,0:T(8,128)(2,1)} collective-permute-done((bf16[128,256]{1,0:T(8,128)(2,1)}, bf16[128,256]{1,0:T(8,128)(2,1)}, u32[]{:S(2)}, u32[]{:S(2)}) %collective-permute-start.14) | collective-permute-done | bytes 65568 | tf_op jit(solution)/shard_map/ppermute | solution.py:25
  75.2 3.1 %collective-permute-start.19 = (bf16[2,256,256]{2,1,0:T(8,128)(2,1)S(1)}, bf16[2,256,256]{2,1,0:T(8,128)(2,1)S(1)}, u32[]{:S(2)}, u32[]{:S(2)}) collective-permute-start(bf16[2,256,256]{2,1,0:T(8,128)(2,1)S(1)} %get-tuple-element.63), channel_id=1, source_target_pairs={{0,2},{1,3},{2,0},{3,1},{4,6},{5,7},{6,4},{7,5},{8,10},{9,11},{10,... | collective-permute-start | bytes 786440 | tf_op jit(solution)/shard_map/ppermute | solution.py:25
  78.7 3.2 %collective-permute-start.25 = (bf16[128,256]{1,0:T(8,128)(2,1)S(1)}, bf16[128,256]{1,0:T(8,128)(2,1)S(1)}, u32[]{:S(2)}, u32[]{:S(2)}) collective-permute-start(bf16[128,256]{1,0:T(8,128)(2,1)S(1)} %fusion.1), channel_id=1, source_target_pairs={{0,24},{1,25},{2,26},{3,27},{4,28},{5,29},{6,30},{7,31},{8,16},{9,... | collective-permute-start | bytes 196616 | tf_op jit(solution)/shard_map/ppermute | solution.py:25
  86.0 2.5 %collective-permute-start.21 = (bf16[256,256]{1,0:T(8,128)(2,1)S(1)}, bf16[256,256]{1,0:T(8,128)(2,1)S(1)}, u32[]{:S(2)}, u32[]{:S(2)}) collective-permute-start(bf16[256,256]{1,0:T(8,128)(2,1)S(1)} %get-tuple-element.70), channel_id=1, source_target_pairs={{0,16},{1,17},{2,18},{3,19},{4,20},{5,21},{6,22},{7,23},{8,24},{9,... | collective-permute-start | bytes 393224 | tf_op jit(solution)/shard_map/ppermute | solution.py:25
  90.1 2.5 %collective-permute-start.29 = (bf16[512,256]{1,0:T(8,128)(2,1)S(1)}, bf16[512,256]{1,0:T(8,128)(2,1)S(1)}, u32[]{:S(2)}, u32[]{:S(2)}) collective-permute-start(bf16[512,256]{1,0:T(8,128)(2,1)S(1)} %pad_maximum_fusion.4.rest_0_), channel_id=1, source_target_pairs={{0,2},{1,3},{2,0},{3,1},{4,6},{5,7},{6,4},{7,5},{8,10},{9,11},{10,... | collective-permute-start | bytes 786440 | tf_op jit(solution)/shard_map/ppermute | solution.py:25
  92.7 4.5 %collective-permute-done.21 = bf16[256,256]{1,0:T(8,128)(2,1)S(1)} collective-permute-done((bf16[256,256]{1,0:T(8,128)(2,1)S(1)}, bf16[256,256]{1,0:T(8,128)(2,1)S(1)}, u32[]{:S(2)}, u32[]{:S(2)}) %collective-permute-start.21) | collective-permute-done | bytes 131104 | tf_op jit(solution)/shard_map/ppermute | solution.py:25
  105.0 4.2 %collective-permute-done.31.rest_2_ = bf16[256,256]{1,0:T(8,128)(2,1)S(1)} collective-permute-done((bf16[256,256]{1,0:T(8,128)(2,1)S(1)}, bf16[256,256]{1,0:T(8,128)(2,1)S(1)}, u32[]{:S(2)}, u32[]{:S(2)}) %collective-permute-start.31) | collective-permute-done | bytes 131104 | tf_op jit(solution)/shard_map/ppermute | solution.py:25
  109.3 4.1 %collective-permute-done.27 = bf16[320,256]{1,0:T(8,128)(2,1)S(1)} collective-permute-done((bf16[320,256]{1,0:T(8,128)(2,1)S(1)}, bf16[320,256]{1,0:T(8,128)(2,1)S(1)}, u32[]{:S(2)}, u32[]{:S(2)}) %collective-permute-start.27) | collective-permute-done | bytes 163872 | tf_op jit(solution)/shard_map/ppermute | solution.py:25
  116.6 3.2 %backward0.1.rest_10_ = f32[24,128,256]{2,1,0:T(8,128)S(1)} custom-call(s32[1,256]{1,0:T(1,128)S(1)} %get-tuple-element.83.table, bf16[192,128,128]{2,1,0:T(8,128)(2,1)S(1)} %bitcast.113, bf16[512,256]{1,0:T(8,128)(2,1)S(1)} %pad_maximum_fusion.4.rest_0_, bf16[512,256]{1,0:T(8,128)(2,1)S(1)} %collective-permute-done.29.rest_1_, ...), custom_call_target="tpu_custom_call" | custom-call | flops 402653184 | bytes 3145728 | tf_op jit(solution)/shard_map/backward0/pallas_call | solution.py:93
  119.8 6.4 %collective-permute-done.34.rest_4_ = bf16[1088,256]{1,0:T(8,128)(2,1)S(1)} collective-permute-done((bf16[1088,256]{1,0:T(8,128)(2,1)S(1)}, bf16[1088,256]{1,0:T(8,128)(2,1)S(1)}, u32[]{:S(2)}, u32[]{:S(2)}) %collective-permute-start.34) | collective-permute-done | bytes 557088 | tf_op jit(solution)/shard_map/ppermute | solution.py:25
  130.1 7.4 %collective-permute-done.36.rest_2_ = bf16[576,256]{1,0:T(8,128)(2,1)S(1)} collective-permute-done((bf16[576,256]{1,0:T(8,128)(2,1)S(1)}, bf16[576,256]{1,0:T(8,128)(2,1)S(1)}, u32[]{:S(2)}, u32[]{:S(2)}) %collective-permute-start.36) | collective-permute-done | bytes 294944 | tf_op jit(solution)/shard_map/ppermute | solution.py:25
  139.7 8.8 %collective-permute-start.41 = (f32[64,256]{1,0:T(8,128)S(1)}, f32[64,256]{1,0:T(8,128)S(1)}, u32[]{:S(2)}, u32[]{:S(2)}) collective-permute-start(f32[64,256]{1,0:T(8,128)S(1)} %add.280), channel_id=1, source_target_pairs={{0,32},{32,0},{64,96},{96,64},{128,160},{160,128},{192,224},{224,1... | collective-permute-start | bytes 196616 | tf_op jit(solution)/shard_map/ppermute | solution.py:25
  148.5 3.6 %backward1.1 = bf16[12,128,256]{2,1,0:T(8,128)(2,1)S(1)} custom-call(s32[1,256]{1,0:T(1,128)S(1)} %get-tuple-element.83.table, bf16[192,128,128]{2,1,0:T(8,128)(2,1)S(1)} %bitcast.114, bf16[1088,256]{1,0:T(8,128)(2,1)S(1)} %fusion.27.rest_0_, bf16[1088,256]{1,0:T(8,128)(2,1)S(1)} %collective-permute-done.33.rest_1_, ...), custom_call_target="tpu_custom_call" | custom-call | flops 402653184 | bytes 1572864 | tf_op jit(solution)/shard_map/backward1/pallas_call | solution.py:93
  153.0 3.1 %backward2.1 = bf16[12,128,256]{2,1,0:T(8,128)(2,1)S(1)} custom-call(s32[1,256]{1,0:T(1,128)S(1)} %get-tuple-element.83.table, bf16[192,128,128]{2,1,0:T(8,128)(2,1)S(1)} %bitcast.115, bf16[1088,256]{1,0:T(8,128)(2,1)S(1)} %fusion.27.rest_0_, bf16[1088,256]{1,0:T(8,128)(2,1)S(1)} %collective-permute-done.33.rest_1_, ...), custom_call_target="tpu_custom_call" | custom-call | flops 402653184 | bytes 1572864 | tf_op jit(solution)/shard_map/backward2/pallas_call | solution.py:93
  156.2 2.7 %collective-permute-start.42 = (bf16[832,256]{1,0:T(8,128)(2,1)S(1)}, bf16[832,256]{1,0:T(8,128)(2,1)S(1)}, u32[]{:S(2)}, u32[]{:S(2)}) collective-permute-start(bf16[832,256]{1,0:T(8,128)(2,1)S(1)} %pad_maximum_fusion.2), channel_id=1, source_target_pairs={{0,64},{32,96},{64,0},{96,32},{128,192},{160,224},{192,128},{224,1... | collective-permute-start | bytes 1277960 | tf_op jit(solution)/shard_map/ppermute | solution.py:25
  158.9 4.4 %collective-permute-done.43 = bf16[2,384,256]{2,1,0:T(8,128)(2,1)S(1)} collective-permute-done((bf16[2,384,256]{2,1,0:T(8,128)(2,1)S(1)}, bf16[2,384,256]{2,1,0:T(8,128)(2,1)S(1)}, u32[]{:S(2)}, u32[]{:S(2)}) %collective-permute-start.43) | collective-permute-done | bytes 393248 | tf_op jit(solution)/shard_map/ppermute | solution.py:25
  164.4 5.2 %collective-permute-done.42 = bf16[832,256]{1,0:T(8,128)(2,1)S(1)} collective-permute-done((bf16[832,256]{1,0:T(8,128)(2,1)S(1)}, bf16[832,256]{1,0:T(8,128)(2,1)S(1)}, u32[]{:S(2)}, u32[]{:S(2)}) %collective-permute-start.42) | collective-permute-done | bytes 426016 | tf_op jit(solution)/shard_map/ppermute | solution.py:25
  173.1 3.9 %collective-permute-done.44 = bf16[448,256]{1,0:T(8,128)(2,1)S(1)} collective-permute-done((bf16[448,256]{1,0:T(8,128)(2,1)S(1)}, bf16[448,256]{1,0:T(8,128)(2,1)S(1)}, u32[]{:S(2)}, u32[]{:S(2)}) %collective-permute-start.44) | collective-permute-done | bytes 229408 | tf_op jit(solution)/shard_map/ppermute | solution.py:25
  177.0 6.0 %collective-permute-start.48 = (bf16[64,256]{1,0:T(8,128)(2,1)S(1)}, bf16[64,256]{1,0:T(8,128)(2,1)S(1)}, u32[]{:S(2)}, u32[]{:S(2)}) collective-permute-start(bf16[64,256]{1,0:T(8,128)(2,1)S(1)} %convert_add_fusion.13), channel_id=1, source_target_pairs={{0,16},{1,17},{2,18},{3,19},{4,20},{5,21},{6,22},{7,23},{8,24},{9,... | collective-permute-start | bytes 98312 | tf_op jit(solution)/shard_map/ppermute | solution.py:25
  184.6 2.7 %collective-permute-done.47 = bf16[64,256]{1,0:T(8,128)(2,1)S(1)} collective-permute-done((bf16[64,256]{1,0:T(8,128)(2,1)S(1)}, bf16[64,256]{1,0:T(8,128)(2,1)S(1)}, u32[]{:S(2)}, u32[]{:S(2)}) %collective-permute-start.47) | collective-permute-done | bytes 32800 | tf_op jit(solution)/shard_map/ppermute | solution.py:25
  187.4 3.3 %collective-permute-done.49 = bf16[64,256]{1,0:T(8,128)(2,1)S(1)} collective-permute-done((bf16[64,256]{1,0:T(8,128)(2,1)S(1)}, bf16[64,256]{1,0:T(8,128)(2,1)S(1)}, u32[]{:S(2)}, u32[]{:S(2)}) %collective-permute-start.49) | collective-permute-done | bytes 32800 | tf_op jit(solution)/shard_map/ppermute | solution.py:25
  (187 shorter events, 66.0 us)
Async XLA Ops:
  3.0 12.3 %collective-permute-start.1 = (bf16[384,256]{1,0:T(8,128)(2,1)S(1)}, bf16[384,256]{1,0:T(8,128)(2,1)S(1)}, u32[]{:S(2)}, u32[]{:S(2)}) collective-permute-start(bf16[384,256]{1,0:T(8,128)(2,1)S(1)} %fusion.9.rest_0_), channel_id=1, source_target_pairs={{0,32},{32,0},{64,96},{96,64},{128,160},{160,128},{192,224},{224,1... | collective-permute-start | bytes 589832 | tf_op jit(solution)/shard_map/ppermute | solution.py:25
  10.3 8.2 %collective-permute-start.3 = (bf16[384,256]{1,0:T(8,128)(2,1)S(1)}, bf16[384,256]{1,0:T(8,128)(2,1)S(1)}, u32[]{:S(2)}, u32[]{:S(2)}) collective-permute-start(bf16[384,256]{1,0:T(8,128)(2,1)S(1)} %fusion.9.rest_0_), channel_id=1, source_target_pairs={{0,192},{32,224},{64,128},{96,160},{128,64},{160,96},{192,0},{224,... | collective-permute-start | bytes 589832 | tf_op jit(solution)/shard_map/ppermute | solution.py:25
  38.0 8.4 %collective-permute-start.9 = (bf16[2,2,128,256]{3,2,1,0:T(8,128)(2,1)S(1)}, bf16[2,2,128,256]{3,2,1,0:T(8,128)(2,1)S(1)}, u32[]{:S(2)}, u32[]{:S(2)}) collective-permute-start(bf16[2,2,128,256]{3,2,1,0:T(8,128)(2,1)S(1)} %get-tuple-element.97), channel_id=1, source_target_pairs={{0,6},{1,7},{2,4},{3,5},{4,2},{5,3},{6,0},{7,1},{8,14},{9,15},{10,... | collective-permute-start | bytes 786440 | tf_op jit(solution)/shard_map/ppermute | solution.py:25
  39.3 8.1 %collective-permute-start.8 = (bf16[2,2,128,256]{3,2,1,0:T(8,128)(2,1)S(1)}, bf16[2,2,128,256]{3,2,1,0:T(8,128)(2,1)S(1)}, u32[]{:S(2)}, u32[]{:S(2)}) collective-permute-start(bf16[2,2,128,256]{3,2,1,0:T(8,128)(2,1)S(1)} %get-tuple-element.98), channel_id=1, source_target_pairs={{0,2},{1,3},{2,0},{3,1},{4,6},{5,7},{6,4},{7,5},{8,10},{9,11},{10,... | collective-permute-start | bytes 786440 | tf_op jit(solution)/shard_map/ppermute | solution.py:25
  43.9 11.8 %collective-permute-start.12 = (bf16[32,128,256]{2,1,0:T(8,128)(2,1)S(1)}, bf16[32,128,256]{2,1,0:T(8,128)(2,1)S(1)}, u32[]{:S(2)}, u32[]{:S(2)}) collective-permute-start(bf16[32,128,256]{2,1,0:T(8,128)(2,1)S(1)} %forward2.1), channel_id=1, source_target_pairs={{0,1},{1,0},{2,3},{3,2},{4,5},{5,4},{6,7},{7,6},{8,9},{9,8},{10,11... | collective-permute-start | bytes 6291464 | tf_op jit(solution)/shard_map/ppermute | solution.py:25
  47.5 8.0 %collective-permute-start.10 = (bf16[2,128,256]{2,1,0:T(8,128)(2,1)S(1)}, bf16[2,128,256]{2,1,0:T(8,128)(2,1)S(1)}, u32[]{:S(2)}, u32[]{:S(2)}) collective-permute-start(bf16[2,128,256]{2,1,0:T(8,128)(2,1)S(1)} %get-tuple-element.51), channel_id=1, source_target_pairs={{0,6},{1,7},{2,4},{3,5},{4,2},{5,3},{6,0},{7,1},{8,14},{9,15},{10,... | collective-permute-start | bytes 393224 | tf_op jit(solution)/shard_map/ppermute | solution.py:25
  57.4 15.2 %collective-permute-start.16 = (bf16[2,2,256,256]{3,2,1,0:T(8,128)(2,1)S(1)}, bf16[2,2,256,256]{3,2,1,0:T(8,128)(2,1)}, u32[]{:S(2)}, u32[]{:S(2)}) collective-permute-start(bf16[2,2,256,256]{3,2,1,0:T(8,128)(2,1)S(1)} %get-tuple-element.58), channel_id=1, source_target_pairs={{0,2},{1,3},{2,0},{3,1},{4,6},{5,7},{6,4},{7,5},{8,10},{9,11},{10,... | collective-permute-start | bytes 1572872 | tf_op jit(solution)/shard_map/ppermute | solution.py:25
  57.7 14.9 %collective-permute-start.17 = (bf16[2,2,256,256]{3,2,1,0:T(8,128)(2,1)S(1)}, bf16[2,2,256,256]{3,2,1,0:T(8,128)(2,1)}, u32[]{:S(2)}, u32[]{:S(2)}) collective-permute-start(bf16[2,2,256,256]{3,2,1,0:T(8,128)(2,1)S(1)} %get-tuple-element.59), channel_id=1, source_target_pairs={{0,6},{1,7},{2,4},{3,5},{4,2},{5,3},{6,0},{7,1},{8,14},{9,15},{10,... | collective-permute-start | bytes 1572872 | tf_op jit(solution)/shard_map/ppermute | solution.py:25
  74.0 9.2 %collective-permute-start.18 = (bf16[2,256,256]{2,1,0:T(8,128)(2,1)S(1)}, bf16[2,256,256]{2,1,0:T(8,128)(2,1)S(1)}, u32[]{:S(2)}, u32[]{:S(2)}) collective-permute-start(bf16[2,256,256]{2,1,0:T(8,128)(2,1)S(1)} %get-tuple-element.62), channel_id=1, source_target_pairs={{0,6},{1,7},{2,4},{3,5},{4,2},{5,3},{6,0},{7,1},{8,14},{9,15},{10,... | collective-permute-start | bytes 786440 | tf_op jit(solution)/shard_map/ppermute | solution.py:25
  75.2 8.0 %collective-permute-start.19 = (bf16[2,256,256]{2,1,0:T(8,128)(2,1)S(1)}, bf16[2,256,256]{2,1,0:T(8,128)(2,1)S(1)}, u32[]{:S(2)}, u32[]{:S(2)}) collective-permute-start(bf16[2,256,256]{2,1,0:T(8,128)(2,1)S(1)} %get-tuple-element.63), channel_id=1, source_target_pairs={{0,2},{1,3},{2,0},{3,1},{4,6},{5,7},{6,4},{7,5},{8,10},{9,11},{10,... | collective-permute-start | bytes 786440 | tf_op jit(solution)/shard_map/ppermute | solution.py:25
  78.7 9.8 %collective-permute-start.25 = (bf16[128,256]{1,0:T(8,128)(2,1)S(1)}, bf16[128,256]{1,0:T(8,128)(2,1)S(1)}, u32[]{:S(2)}, u32[]{:S(2)}) collective-permute-start(bf16[128,256]{1,0:T(8,128)(2,1)S(1)} %fusion.1), channel_id=1, source_target_pairs={{0,24},{1,25},{2,26},{3,27},{4,28},{5,29},{6,30},{7,31},{8,16},{9,... | collective-permute-start | bytes 196616 | tf_op jit(solution)/shard_map/ppermute | solution.py:25
  84.7 8.0 %collective-permute-start.20 = (bf16[256,256]{1,0:T(8,128)(2,1)S(1)}, bf16[256,256]{1,0:T(8,128)(2,1)S(1)}, u32[]{:S(2)}, u32[]{:S(2)}) collective-permute-start(bf16[256,256]{1,0:T(8,128)(2,1)S(1)} %get-tuple-element.69), channel_id=1, source_target_pairs={{0,8},{1,9},{2,10},{3,11},{4,12},{5,13},{6,14},{7,15},{8,0},{9,1},... | collective-permute-start | bytes 393224 | tf_op jit(solution)/shard_map/ppermute | solution.py:25
  86.0 11.1 %collective-permute-start.21 = (bf16[256,256]{1,0:T(8,128)(2,1)S(1)}, bf16[256,256]{1,0:T(8,128)(2,1)S(1)}, u32[]{:S(2)}, u32[]{:S(2)}) collective-permute-start(bf16[256,256]{1,0:T(8,128)(2,1)S(1)} %get-tuple-element.70), channel_id=1, source_target_pairs={{0,16},{1,17},{2,18},{3,19},{4,20},{5,21},{6,22},{7,23},{8,24},{9,... | collective-permute-start | bytes 393224 | tf_op jit(solution)/shard_map/ppermute | solution.py:25
  88.4 8.7 %collective-permute-start.22 = (bf16[256,256]{1,0:T(8,128)(2,1)S(1)}, bf16[256,256]{1,0:T(8,128)(2,1)S(1)}, u32[]{:S(2)}, u32[]{:S(2)}) collective-permute-start(bf16[256,256]{1,0:T(8,128)(2,1)S(1)} %get-tuple-element.71), channel_id=1, source_target_pairs={{0,24},{1,25},{2,26},{3,27},{4,28},{5,29},{6,30},{7,31},{8,16},{9,... | collective-permute-start | bytes 393224 | tf_op jit(solution)/shard_map/ppermute | solution.py:25
  89.2 13.7 %collective-permute-start.30 = (bf16[512,256]{1,0:T(8,128)(2,1)S(1)}, bf16[512,256]{1,0:T(8,128)(2,1)S(1)}, u32[]{:S(2)}, u32[]{:S(2)}) collective-permute-start(bf16[512,256]{1,0:T(8,128)(2,1)S(1)} %pad_maximum_fusion.4.rest_0_), channel_id=1, source_target_pairs={{0,6},{1,7},{2,4},{3,5},{4,2},{5,3},{6,0},{7,1},{8,14},{9,15},{10,... | collective-permute-start | bytes 786440 | tf_op jit(solution)/shard_map/ppermute | solution.py:25
  90.1 12.8 %collective-permute-start.29 = (bf16[512,256]{1,0:T(8,128)(2,1)S(1)}, bf16[512,256]{1,0:T(8,128)(2,1)S(1)}, u32[]{:S(2)}, u32[]{:S(2)}) collective-permute-start(bf16[512,256]{1,0:T(8,128)(2,1)S(1)} %pad_maximum_fusion.4.rest_0_), channel_id=1, source_target_pairs={{0,2},{1,3},{2,0},{3,1},{4,6},{5,7},{6,4},{7,5},{8,10},{9,11},{10,... | collective-permute-start | bytes 786440 | tf_op jit(solution)/shard_map/ppermute | solution.py:25
  98.4 10.9 %collective-permute-start.26 = (bf16[320,256]{1,0:T(8,128)(2,1)S(1)}, bf16[320,256]{1,0:T(8,128)(2,1)S(1)}, u32[]{:S(2)}, u32[]{:S(2)}) collective-permute-start(bf16[320,256]{1,0:T(8,128)(2,1)S(1)} %get-tuple-element.75), channel_id=1, source_target_pairs={{0,8},{1,9},{2,10},{3,11},{4,12},{5,13},{6,14},{7,15},{8,0},{9,1},... | collective-permute-start | bytes 491528 | tf_op jit(solution)/shard_map/ppermute | solution.py:25
  100.4 13.1 %collective-permute-start.27 = (bf16[320,256]{1,0:T(8,128)(2,1)S(1)}, bf16[320,256]{1,0:T(8,128)(2,1)S(1)}, u32[]{:S(2)}, u32[]{:S(2)}) collective-permute-start(bf16[320,256]{1,0:T(8,128)(2,1)S(1)} %get-tuple-element.76), channel_id=1, source_target_pairs={{0,16},{1,17},{2,18},{3,19},{4,20},{5,21},{6,22},{7,23},{8,24},{9,... | collective-permute-start | bytes 491528 | tf_op jit(solution)/shard_map/ppermute | solution.py:25
  101.5 12.0 %collective-permute-start.28 = (bf16[320,256]{1,0:T(8,128)(2,1)S(1)}, bf16[320,256]{1,0:T(8,128)(2,1)S(1)}, u32[]{:S(2)}, u32[]{:S(2)}) collective-permute-start(bf16[320,256]{1,0:T(8,128)(2,1)S(1)} %get-tuple-element.77), channel_id=1, source_target_pairs={{0,24},{1,25},{2,26},{3,27},{4,28},{5,29},{6,30},{7,31},{8,16},{9,... | collective-permute-start | bytes 491528 | tf_op jit(solution)/shard_map/ppermute | solution.py:25
  113.6 12.6 %collective-permute-start.34 = (bf16[1088,256]{1,0:T(8,128)(2,1)S(1)}, bf16[1088,256]{1,0:T(8,128)(2,1)S(1)}, u32[]{:S(2)}, u32[]{:S(2)}) collective-permute-start(bf16[1088,256]{1,0:T(8,128)(2,1)S(1)} %fusion.27.rest_0_), channel_id=1, source_target_pairs={{0,6},{1,7},{2,4},{3,5},{4,2},{5,3},{6,0},{7,1},{8,14},{9,15},{10,... | collective-permute-start | bytes 1671176 | tf_op jit(solution)/shard_map/ppermute | solution.py:25
  115.0 12.7 %collective-permute-start.33 = (bf16[1088,256]{1,0:T(8,128)(2,1)S(1)}, bf16[1088,256]{1,0:T(8,128)(2,1)S(1)}, u32[]{:S(2)}, u32[]{:S(2)}) collective-permute-start(bf16[1088,256]{1,0:T(8,128)(2,1)S(1)} %fusion.27.rest_0_), channel_id=1, source_target_pairs={{0,2},{1,3},{2,0},{3,1},{4,6},{5,7},{6,4},{7,5},{8,10},{9,11},{10,... | collective-permute-start | bytes 1671176 | tf_op jit(solution)/shard_map/ppermute | solution.py:25
  127.9 11.8 %collective-permute-start.38 = (bf16[3072,256]{1,0:T(8,128)(2,1)S(1)}, bf16[3072,256]{1,0:T(8,128)(2,1)S(1)}, u32[]{:S(2)}, u32[]{:S(2)}) collective-permute-start(bf16[3072,256]{1,0:T(8,128)(2,1)S(1)} %pad_maximum_fusion), channel_id=1, source_target_pairs={{0,1},{1,0},{2,3},{3,2},{4,5},{5,4},{6,7},{7,6},{8,9},{9,8},{10,11... | collective-permute-start | bytes 4718600 | tf_op jit(solution)/shard_map/ppermute | solution.py:25
  128.0 9.5 %collective-permute-start.36 = (bf16[576,256]{1,0:T(8,128)(2,1)S(1)}, bf16[576,256]{1,0:T(8,128)(2,1)S(1)}, u32[]{:S(2)}, u32[]{:S(2)}) collective-permute-start(bf16[576,256]{1,0:T(8,128)(2,1)S(1)} %pad_maximum_fusion.3), channel_id=1, source_target_pairs={{0,6},{1,7},{2,4},{3,5},{4,2},{5,3},{6,0},{7,1},{8,14},{9,15},{10,... | collective-permute-start | bytes 884744 | tf_op jit(solution)/shard_map/ppermute | solution.py:25
  128.7 8.8 %collective-permute-start.37 = (bf16[512,256]{1,0:T(8,128)(2,1)S(1)}, bf16[512,256]{1,0:T(8,128)(2,1)S(1)}, u32[]{:S(2)}, u32[]{:S(2)}) collective-permute-start(bf16[512,256]{1,0:T(8,128)(2,1)S(1)} %slice.314), channel_id=1, source_target_pairs={{0,2},{1,3},{2,0},{3,1},{4,6},{5,7},{6,4},{7,5},{8,10},{9,11},{10,... | collective-permute-start | bytes 786440 | tf_op jit(solution)/shard_map/ppermute | solution.py:25
  137.6 10.9 %collective-permute-start.39 = (bf16[1024,256]{1,0:T(8,128)(2,1)S(1)}, bf16[1024,256]{1,0:T(8,128)(2,1)S(1)}, u32[]{:S(2)}, u32[]{:S(2)}) collective-permute-start(bf16[1024,256]{1,0:T(8,128)(2,1)S(1)} %pad_maximum_fusion.1), channel_id=1, source_target_pairs={{0,1},{1,0},{2,3},{3,2},{4,5},{5,4},{6,7},{7,6},{8,9},{9,8},{10,11... | collective-permute-start | bytes 1572872 | tf_op jit(solution)/shard_map/ppermute | solution.py:25
  139.7 16.4 %collective-permute-start.41 = (f32[64,256]{1,0:T(8,128)S(1)}, f32[64,256]{1,0:T(8,128)S(1)}, u32[]{:S(2)}, u32[]{:S(2)}) collective-permute-start(f32[64,256]{1,0:T(8,128)S(1)} %add.280), channel_id=1, source_target_pairs={{0,32},{32,0},{64,96},{96,64},{128,160},{160,128},{192,224},{224,1... | collective-permute-start | bytes 196616 | tf_op jit(solution)/shard_map/ppermute | solution.py:25
  152.2 11.2 %collective-permute-start.43 = (bf16[2,384,256]{2,1,0:T(8,128)(2,1)S(1)}, bf16[2,384,256]{2,1,0:T(8,128)(2,1)S(1)}, u32[]{:S(2)}, u32[]{:S(2)}) collective-permute-start(bf16[2,384,256]{2,1,0:T(8,128)(2,1)S(1)} %bitcast.130), channel_id=1, source_target_pairs={{0,192},{32,224},{64,128},{96,160},{128,64},{160,96},{192,0},{224,... | collective-permute-start | bytes 1179656 | tf_op jit(solution)/shard_map/ppermute | solution.py:25
  156.2 13.3 %collective-permute-start.42 = (bf16[832,256]{1,0:T(8,128)(2,1)S(1)}, bf16[832,256]{1,0:T(8,128)(2,1)S(1)}, u32[]{:S(2)}, u32[]{:S(2)}) collective-permute-start(bf16[832,256]{1,0:T(8,128)(2,1)S(1)} %pad_maximum_fusion.2), channel_id=1, source_target_pairs={{0,64},{32,96},{64,0},{96,32},{128,192},{160,224},{192,128},{224,1... | collective-permute-start | bytes 1277960 | tf_op jit(solution)/shard_map/ppermute | solution.py:25
  163.4 9.2 %collective-permute-start.45 = (bf16[384,256]{1,0:T(8,128)(2,1)S(1)}, bf16[384,256]{1,0:T(8,128)(2,1)S(1)}, u32[]{:S(2)}, u32[]{:S(2)}) collective-permute-start(bf16[384,256]{1,0:T(8,128)(2,1)S(1)} %fusion.13), channel_id=1, source_target_pairs={{0,64},{32,96},{64,0},{96,32},{128,192},{160,224},{192,128},{224,1... | collective-permute-start | bytes 589832 | tf_op jit(solution)/shard_map/ppermute | solution.py:25
  172.7 18.7 %collective-permute-start.46 = (bf16[384,256]{1,0:T(8,128)(2,1)S(1)}, bf16[384,256]{1,0:T(8,128)(2,1)S(1)}, u32[]{:S(2)}, u32[]{:S(2)}) collective-permute-start(bf16[384,256]{1,0:T(8,128)(2,1)S(1)} %fusion.12), channel_id=1, source_target_pairs={{0,32},{32,0},{64,96},{96,64},{128,160},{160,128},{192,224},{224,1... | collective-permute-start | bytes 589832 | tf_op jit(solution)/shard_map/ppermute | solution.py:25
  177.0 10.4 %collective-permute-start.48 = (bf16[64,256]{1,0:T(8,128)(2,1)S(1)}, bf16[64,256]{1,0:T(8,128)(2,1)S(1)}, u32[]{:S(2)}, u32[]{:S(2)}) collective-permute-start(bf16[64,256]{1,0:T(8,128)(2,1)S(1)} %convert_add_fusion.13), channel_id=1, source_target_pairs={{0,16},{1,17},{2,18},{3,19},{4,20},{5,21},{6,22},{7,23},{8,24},{9,... | collective-permute-start | bytes 98312 | tf_op jit(solution)/shard_map/ppermute | solution.py:25
  183.0 7.7 %collective-permute-start.49 = (bf16[64,256]{1,0:T(8,128)(2,1)S(1)}, bf16[64,256]{1,0:T(8,128)(2,1)S(1)}, u32[]{:S(2)}, u32[]{:S(2)}) collective-permute-start(bf16[64,256]{1,0:T(8,128)(2,1)S(1)} %convert_add_fusion.13), channel_id=1, source_target_pairs={{0,24},{1,25},{2,26},{3,27},{4,28},{5,29},{6,30},{7,31},{8,16},{9,... | collective-permute-start | bytes 98312 | tf_op jit(solution)/shard_map/ppermute | solution.py:25
  (34 other events, 417.0 us)

commit v6 on v5

--- a/solution.py
+++ b/solution.py
@@ -237,11 +237,11 @@
     high_second = (wide(high[1]) + wide(high_in[0])).astype(bf16)
     high_next = exchange(high_second, "row", near)
     low_second = (wide(low[3]) + wide(low_in[1])).astype(bf16)
-    low_next, share = send(after(low_second, high_second), far)
+    low_next, share = send(low_second, far)
     leaving = (wide(high[0]) + wide(high_in[1]) + wide(high_next)).astype(bf16)
     arrived = exchange(leaving, "row", 1)
     total = wide(low[0]) + wide(low_in[0]) + wide(low_next) + wide(arrived)
-    return total, after(share, leaving)
+    return total, share
 
 
 def per_device(

time: 193 us -> 196 us (1.016)
  starting transfers between devices: 82.4 us -> 86 us
    ppermute x50, starting transfers between devices: 82.4 us -> 86 us  [exchange(): return lax.ppermute(value, axis, [(i, i ^ mask) for i in range(size)])]
  transfers between devices with their start and end apart: 50 -> 50, of which waited for: 23 -> 21; matrix products, arithmetic and copies ran while one was open for 4% -> 4% of each run, Pallas kernels for 10% -> 10%
where the time goes in v6:
time: 196 us; the launch traced here: 194 us
  starting transfers between devices  86 us (44%)
  waiting for transfers between devices  64.8 us (33%)
  Pallas kernels  20.5 us (10%)
  other arithmetic  10 us (5%)
  local copies, waits for them, and re-layouts  9.57 us (5%)
  between operations  2.09 us (1%)
    ppermute x50, starting transfers between devices, exchange(): return lax.ppermute(value, axis, [(i, i ^ mask) for i in range(size)])  86 us
    ppermute x50, waiting for transfers between devices, exchange(): return lax.ppermute(value, axis, [(i, i ^ mask) for i in range(size)])  64.8 us
    pallas_call x7, Pallas kernels, group_products(): pl.pallas_call(functools.partial(group_kernel, spans=spans, group=group,...  19.3 us
    unnamed x40, local copies, waits for them, and re-layouts  8.48 us
  transfers between devices with their start and end apart: 50, of which 21 were waited for; matrix products, arithmetic and copies ran while one was open for 4% of the time, Pallas kernels for 10%

profile of v6, /device:TPU:2, one launch (start us, length us, event | category | flops | bytes accessed | tf_op | source)
XLA Modules:
  0.0 194.4 jit_solution(9499979093701332532)
XLA Ops:
  3.0 7.3 %collective-permute-start.1 = (bf16[384,256]{1,0:T(8,128)(2,1)S(1)}, bf16[384,256]{1,0:T(8,128)(2,1)S(1)}, u32[]{:S(2)}, u32[]{:S(2)}) collective-permute-start(bf16[384,256]{1,0:T(8,128)(2,1)S(1)} %fusion.9.rest_0_), channel_id=1, source_target_pairs={{0,32},{32,0},{64,96},{96,64},{128,160},{160,128},{192,224},{224,1... | collective-permute-start | bytes 589832 | tf_op jit(solution)/shard_map/ppermute | solution.py:25
  10.3 3.0 %collective-permute-start.3 = (bf16[384,256]{1,0:T(8,128)(2,1)S(1)}, bf16[384,256]{1,0:T(8,128)(2,1)S(1)}, u32[]{:S(2)}, u32[]{:S(2)}) collective-permute-start(bf16[384,256]{1,0:T(8,128)(2,1)S(1)} %fusion.9.rest_0_), channel_id=1, source_target_pairs={{0,192},{32,224},{64,128},{96,160},{128,64},{160,96},{192,0},{224,... | collective-permute-start | bytes 589832 | tf_op jit(solution)/shard_map/ppermute | solution.py:25
  15.3 3.0 %collective-permute-start.4 = (bf16[384,256]{1,0:T(8,128)(2,1)S(1)}, bf16[384,256]{1,0:T(8,128)(2,1)S(1)}, u32[]{:S(2)}, u32[]{:S(2)}) collective-permute-start(bf16[384,256]{1,0:T(8,128)(2,1)S(1)} %collective-permute-done.1.rest_5_), channel_id=1, source_target_pairs={{0,192},{32,224},{64,128},{96,160},{128,64},{160,96},{192,0},{224,... | collective-permute-start | bytes 589832 | tf_op jit(solution)/shard_map/ppermute | solution.py:25
  19.4 3.2 %collective-permute-done.4.rest_9_ = bf16[384,256]{1,0:T(8,128)(2,1)S(1)} collective-permute-done((bf16[384,256]{1,0:T(8,128)(2,1)S(1)}, bf16[384,256]{1,0:T(8,128)(2,1)S(1)}, u32[]{:S(2)}, u32[]{:S(2)}) %collective-permute-start.4) | collective-permute-done | bytes 196640 | tf_op jit(solution)/shard_map/ppermute | solution.py:25
  27.2 2.8 %copy-done.1 = bf16[1,1,192,128,128]{4,3,2,1,0:T(8,128)(2,1)S(1)} copy-done((bf16[1,1,192,128,128]{4,3,2,1,0:T(8,128)(2,1)S(1)}, bf16[1,1,192,128,128]{4,3,2,1,0:T(8,128)(2,1)}, u32[]{:S(2)}) %copy-start.1) | copy-done | bytes 6291480
  40.5 2.8 %forward2.1 = bf16[32,128,256]{2,1,0:T(8,128)(2,1)S(1)} custom-call(s32[1,256]{1,0:T(1,128)S(1)} %get-tuple-element.51.table, bf16[192,128,128]{2,1,0:T(8,128)(2,1)S(1)} %bitcast.109, bf16[384,256]{1,0:T(8,128)(2,1)S(1)} %fusion.9.rest_0_, bf16[384,256]{1,0:T(8,128)(2,1)S(1)} %collective-permute-done.rest_1_, ...), custom_call_target="tpu_custom_call" | custom-call | flops 80530636800 | bytes 838860800 | tf_op jit(solution)/shard_map/forward2/pallas_call | solution.py:93
  43.4 2.7 %collective-permute-done.9 = bf16[2,2,128,256]{3,2,1,0:T(8,128)(2,1)S(1)} collective-permute-done((bf16[2,2,128,256]{3,2,1,0:T(8,128)(2,1)S(1)}, bf16[2,2,128,256]{3,2,1,0:T(8,128)(2,1)S(1)}, u32[]{:S(2)}, u32[]{:S(2)}) %collective-permute-start.9) | collective-permute-done | bytes 262176 | tf_op jit(solution)/shard_map/ppermute | solution.py:25
  48.1 2.2 %collective-permute-start.11 = (bf16[2,128,256]{2,1,0:T(8,128)(2,1)S(1)}, bf16[2,128,256]{2,1,0:T(8,128)(2,1)S(1)}, u32[]{:S(2)}, u32[]{:S(2)}) collective-permute-start(bf16[2,128,256]{2,1,0:T(8,128)(2,1)S(1)} %get-tuple-element.50), channel_id=1, source_target_pairs={{0,2},{1,3},{2,0},{3,1},{4,6},{5,7},{6,4},{7,5},{8,10},{9,11},{10,... | collective-permute-start | bytes 393224 | tf_op jit(solution)/shard_map/ppermute | solution.py:25
  52.1 3.1 %forward3.1 = bf16[32,128,256]{2,1,0:T(8,128)(2,1)S(1)} custom-call(s32[1,256]{1,0:T(1,128)S(1)} %get-tuple-element.51.table, bf16[192,128,128]{2,1,0:T(8,128)(2,1)S(1)} %bitcast.110, bf16[384,256]{1,0:T(8,128)(2,1)S(1)} %fusion.9.rest_0_, bf16[384,256]{1,0:T(8,128)(2,1)S(1)} %collective-permute-done.rest_1_, bf16[384,256]{1,0:T(8,128)(2,1)S(1)} %copy-done.4, ...), custom_call_target="tpu_custom_call" | custom-call | flops 80530636800 | bytes 838860800 | tf_op jit(solution)/shard_map/forward3/pallas_call | solution.py:93
  59.0 5.9 %collective-permute-start.13 = (bf16[128,256]{1,0:T(8,128)(2,1)S(1)}, bf16[128,256]{1,0:T(8,128)(2,1)}, u32[]{:S(2)}, u32[]{:S(2)}) collective-permute-start(bf16[128,256]{1,0:T(8,128)(2,1)S(1)} %fusion.26), channel_id=1, source_target_pairs={{0,8},{1,9},{2,10},{3,11},{4,12},{5,13},{6,14},{7,15},{8,0},{9,1},... | collective-permute-start | bytes 196616 | tf_op jit(solution)/shard_map/ppermute | solution.py:25
  67.3 3.5 %collective-permute-done.14 = bf16[128,256]{1,0:T(8,128)(2,1)} collective-permute-done((bf16[128,256]{1,0:T(8,128)(2,1)}, bf16[128,256]{1,0:T(8,128)(2,1)}, u32[]{:S(2)}, u32[]{:S(2)}) %collective-permute-start.14) | collective-permute-done | bytes 65568 | tf_op jit(solution)/shard_map/ppermute | solution.py:25
  75.2 2.6 %collective-permute-start.19 = (bf16[2,256,256]{2,1,0:T(8,128)(2,1)S(1)}, bf16[2,256,256]{2,1,0:T(8,128)(2,1)S(1)}, u32[]{:S(2)}, u32[]{:S(2)}) collective-permute-start(bf16[2,256,256]{2,1,0:T(8,128)(2,1)S(1)} %get-tuple-element.61), channel_id=1, source_target_pairs={{0,2},{1,3},{2,0},{3,1},{4,6},{5,7},{6,4},{7,5},{8,10},{9,11},{10,... | collective-permute-start | bytes 786440 | tf_op jit(solution)/shard_map/ppermute | solution.py:25
  78.2 3.4 %collective-permute-start.25 = (bf16[128,256]{1,0:T(8,128)(2,1)S(1)}, bf16[128,256]{1,0:T(8,128)(2,1)S(1)}, u32[]{:S(2)}, u32[]{:S(2)}) collective-permute-start(bf16[128,256]{1,0:T(8,128)(2,1)S(1)} %fusion.1), channel_id=1, source_target_pairs={{0,24},{1,25},{2,26},{3,27},{4,28},{5,29},{6,30},{7,31},{8,16},{9,... | collective-permute-start | bytes 196616 | tf_op jit(solution)/shard_map/ppermute | solution.py:25
  85.0 2.6 %collective-permute-start.20 = (bf16[256,256]{1,0:T(8,128)(2,1)S(1)}, bf16[256,256]{1,0:T(8,128)(2,1)S(1)}, u32[]{:S(2)}, u32[]{:S(2)}) collective-permute-start(bf16[256,256]{1,0:T(8,128)(2,1)S(1)} %get-tuple-element.67), channel_id=1, source_target_pairs={{0,8},{1,9},{2,10},{3,11},{4,12},{5,13},{6,14},{7,15},{8,0},{9,1},... | collective-permute-start | bytes 393224 | tf_op jit(solution)/shard_map/ppermute | solution.py:25
  91.5 2.4 %collective-permute-start.29 = (bf16[512,256]{1,0:T(8,128)(2,1)S(1)}, bf16[512,256]{1,0:T(8,128)(2,1)S(1)}, u32[]{:S(2)}, u32[]{:S(2)}) collective-permute-start(bf16[512,256]{1,0:T(8,128)(2,1)S(1)} %pad_maximum_fusion.4.rest_0_), channel_id=1, source_target_pairs={{0,2},{1,3},{2,0},{3,1},{4,6},{5,7},{6,4},{7,5},{8,10},{9,11},{10,... | collective-permute-start | bytes 786440 | tf_op jit(solution)/shard_map/ppermute | solution.py:25
  93.9 4.4 %collective-permute-done.21 = bf16[256,256]{1,0:T(8,128)(2,1)S(1)} collective-permute-done((bf16[256,256]{1,0:T(8,128)(2,1)S(1)}, bf16[256,256]{1,0:T(8,128)(2,1)S(1)}, u32[]{:S(2)}, u32[]{:S(2)}) %collective-permute-start.21) | collective-permute-done | bytes 131104 | tf_op jit(solution)/shard_map/ppermute | solution.py:25
  101.7 2.4 %collective-permute-start.28 = (bf16[320,256]{1,0:T(8,128)(2,1)S(1)}, bf16[320,256]{1,0:T(8,128)(2,1)S(1)}, u32[]{:S(2)}, u32[]{:S(2)}) collective-permute-start(bf16[320,256]{1,0:T(8,128)(2,1)S(1)} %get-tuple-element.75), channel_id=1, source_target_pairs={{0,24},{1,25},{2,26},{3,27},{4,28},{5,29},{6,30},{7,31},{8,16},{9,... | collective-permute-start | bytes 491528 | tf_op jit(solution)/shard_map/ppermute | solution.py:25
  106.8 4.1 %collective-permute-done.31.rest_2_ = bf16[256,256]{1,0:T(8,128)(2,1)S(1)} collective-permute-done((bf16[256,256]{1,0:T(8,128)(2,1)S(1)}, bf16[256,256]{1,0:T(8,128)(2,1)S(1)}, u32[]{:S(2)}, u32[]{:S(2)}) %collective-permute-start.31) | collective-permute-done | bytes 131104 | tf_op jit(solution)/shard_map/ppermute | solution.py:25
  111.0 3.1 %collective-permute-done.27 = bf16[320,256]{1,0:T(8,128)(2,1)S(1)} collective-permute-done((bf16[320,256]{1,0:T(8,128)(2,1)S(1)}, bf16[320,256]{1,0:T(8,128)(2,1)S(1)}, u32[]{:S(2)}, u32[]{:S(2)}) %collective-permute-start.27) | collective-permute-done | bytes 163872 | tf_op jit(solution)/shard_map/ppermute | solution.py:25
  115.9 2.3 %collective-permute-start.33 = (bf16[1088,256]{1,0:T(8,128)(2,1)S(1)}, bf16[1088,256]{1,0:T(8,128)(2,1)S(1)}, u32[]{:S(2)}, u32[]{:S(2)}) collective-permute-start(bf16[1088,256]{1,0:T(8,128)(2,1)S(1)} %fusion.27.rest_0_), channel_id=1, source_target_pairs={{0,2},{1,3},{2,0},{3,1},{4,6},{5,7},{6,4},{7,5},{8,10},{9,11},{10,... | collective-permute-start | bytes 1671176 | tf_op jit(solution)/shard_map/ppermute | solution.py:25
  118.3 3.2 %backward0.1.rest_10_ = f32[24,128,256]{2,1,0:T(8,128)S(1)} custom-call(s32[1,256]{1,0:T(1,128)S(1)} %get-tuple-element.81.table, bf16[192,128,128]{2,1,0:T(8,128)(2,1)S(1)} %bitcast.113, bf16[512,256]{1,0:T(8,128)(2,1)S(1)} %pad_maximum_fusion.4.rest_0_, bf16[512,256]{1,0:T(8,128)(2,1)S(1)} %collective-permute-done.29.rest_1_, ...), custom_call_target="tpu_custom_call" | custom-call | flops 402653184 | bytes 3145728 | tf_op jit(solution)/shard_map/backward0/pallas_call | solution.py:93
  121.5 5.9 %collective-permute-done.34.rest_4_ = bf16[1088,256]{1,0:T(8,128)(2,1)S(1)} collective-permute-done((bf16[1088,256]{1,0:T(8,128)(2,1)S(1)}, bf16[1088,256]{1,0:T(8,128)(2,1)S(1)}, u32[]{:S(2)}, u32[]{:S(2)}) %collective-permute-start.34) | collective-permute-done | bytes 557088 | tf_op jit(solution)/shard_map/ppermute | solution.py:25
  131.2 2.4 %collective-permute-start.37 = (bf16[512,256]{1,0:T(8,128)(2,1)S(1)}, bf16[512,256]{1,0:T(8,128)(2,1)S(1)}, u32[]{:S(2)}, u32[]{:S(2)}) collective-permute-start(bf16[512,256]{1,0:T(8,128)(2,1)S(1)} %slice.314), channel_id=1, source_target_pairs={{0,2},{1,3},{2,0},{3,1},{4,6},{5,7},{6,4},{7,5},{8,10},{9,11},{10,... | collective-permute-start | bytes 786440 | tf_op jit(solution)/shard_map/ppermute | solution.py:25
  133.6 5.4 %collective-permute-done.36.rest_2_ = bf16[576,256]{1,0:T(8,128)(2,1)S(1)} collective-permute-done((bf16[576,256]{1,0:T(8,128)(2,1)S(1)}, bf16[576,256]{1,0:T(8,128)(2,1)S(1)}, u32[]{:S(2)}, u32[]{:S(2)}) %collective-permute-start.36) | collective-permute-done | bytes 294944 | tf_op jit(solution)/shard_map/ppermute | solution.py:25
  142.4 4.8 %collective-permute-start.41 = (f32[64,256]{1,0:T(8,128)S(1)}, f32[64,256]{1,0:T(8,128)S(1)}, u32[]{:S(2)}, u32[]{:S(2)}) collective-permute-start(f32[64,256]{1,0:T(8,128)S(1)} %add.280), channel_id=1, source_target_pairs={{0,32},{32,0},{64,96},{96,64},{128,160},{160,128},{192,224},{224,1... | collective-permute-start | bytes 196616 | tf_op jit(solution)/shard_map/ppermute | solution.py:25
  147.2 3.1 %backward1.1 = bf16[12,128,256]{2,1,0:T(8,128)(2,1)S(1)} custom-call(s32[1,256]{1,0:T(1,128)S(1)} %get-tuple-element.81.table, bf16[192,128,128]{2,1,0:T(8,128)(2,1)S(1)} %bitcast.114, bf16[1088,256]{1,0:T(8,128)(2,1)S(1)} %fusion.27.rest_0_, bf16[1088,256]{1,0:T(8,128)(2,1)S(1)} %collective-permute-done.33.rest_1_, ...), custom_call_target="tpu_custom_call" | custom-call | flops 402653184 | bytes 1572864 | tf_op jit(solution)/shard_map/backward1/pallas_call | solution.py:93
  152.3 3.1 %backward2.1 = bf16[12,128,256]{2,1,0:T(8,128)(2,1)S(1)} custom-call(s32[1,256]{1,0:T(1,128)S(1)} %get-tuple-element.81.table, bf16[192,128,128]{2,1,0:T(8,128)(2,1)S(1)} %bitcast.115, bf16[1088,256]{1,0:T(8,128)(2,1)S(1)} %fusion.27.rest_0_, bf16[1088,256]{1,0:T(8,128)(2,1)S(1)} %collective-permute-done.33.rest_1_, ...), custom_call_target="tpu_custom_call" | custom-call | flops 402653184 | bytes 1572864 | tf_op jit(solution)/shard_map/backward2/pallas_call | solution.py:93
  157.5 9.4 %collective-permute-done.42 = bf16[832,256]{1,0:T(8,128)(2,1)S(1)} collective-permute-done((bf16[832,256]{1,0:T(8,128)(2,1)S(1)}, bf16[832,256]{1,0:T(8,128)(2,1)S(1)}, u32[]{:S(2)}, u32[]{:S(2)}) %collective-permute-start.42) | collective-permute-done | bytes 426016 | tf_op jit(solution)/shard_map/ppermute | solution.py:25
  166.9 2.8 %collective-permute-start.43 = (bf16[448,256]{1,0:T(8,128)(2,1)S(1)}, bf16[448,256]{1,0:T(8,128)(2,1)S(1)}, u32[]{:S(2)}, u32[]{:S(2)}) collective-permute-start(bf16[448,256]{1,0:T(8,128)(2,1)S(1)} %pad_maximum_fusion.5), channel_id=1, source_target_pairs={{0,192},{32,224},{64,128},{96,160},{128,64},{160,96},{192,0},{224,... | collective-permute-start | bytes 688136 | tf_op jit(solution)/shard_map/ppermute | solution.py:25
  171.0 3.5 %collective-permute-done.43 = bf16[448,256]{1,0:T(8,128)(2,1)S(1)} collective-permute-done((bf16[448,256]{1,0:T(8,128)(2,1)S(1)}, bf16[448,256]{1,0:T(8,128)(2,1)S(1)}, u32[]{:S(2)}, u32[]{:S(2)}) %collective-permute-start.43) | collective-permute-done | bytes 229408 | tf_op jit(solution)/shard_map/ppermute | solution.py:25
  174.6 4.7 %collective-permute-start.47 = (bf16[64,256]{1,0:T(8,128)(2,1)S(1)}, bf16[64,256]{1,0:T(8,128)(2,1)S(1)}, u32[]{:S(2)}, u32[]{:S(2)}) collective-permute-start(bf16[64,256]{1,0:T(8,128)(2,1)S(1)} %get-tuple-element.84), channel_id=1, source_target_pairs={{0,8},{1,9},{2,10},{3,11},{4,12},{5,13},{6,14},{7,15},{8,0},{9,1},... | collective-permute-start | bytes 98312 | tf_op jit(solution)/shard_map/ppermute | solution.py:25
  183.4 9.3 %collective-permute-done.48 = bf16[64,256]{1,0:T(8,128)(2,1)S(1)} collective-permute-done((bf16[64,256]{1,0:T(8,128)(2,1)S(1)}, bf16[64,256]{1,0:T(8,128)(2,1)S(1)}, u32[]{:S(2)}, u32[]{:S(2)}) %collective-permute-start.48) | collective-permute-done | bytes 32800 | tf_op jit(solution)/shard_map/ppermute | solution.py:25
  (186 shorter events, 68.0 us)
Async XLA Ops:
  3.0 12.3 %collective-permute-start.1 = (bf16[384,256]{1,0:T(8,128)(2,1)S(1)}, bf16[384,256]{1,0:T(8,128)(2,1)S(1)}, u32[]{:S(2)}, u32[]{:S(2)}) collective-permute-start(bf16[384,256]{1,0:T(8,128)(2,1)S(1)} %fusion.9.rest_0_), channel_id=1, source_target_pairs={{0,32},{32,0},{64,96},{96,64},{128,160},{160,128},{192,224},{224,1... | collective-permute-start | bytes 589832 | tf_op jit(solution)/shard_map/ppermute | solution.py:25
  10.3 8.2 %collective-permute-start.3 = (bf16[384,256]{1,0:T(8,128)(2,1)S(1)}, bf16[384,256]{1,0:T(8,128)(2,1)S(1)}, u32[]{:S(2)}, u32[]{:S(2)}) collective-permute-start(bf16[384,256]{1,0:T(8,128)(2,1)S(1)} %fusion.9.rest_0_), channel_id=1, source_target_pairs={{0,192},{32,224},{64,128},{96,160},{128,64},{160,96},{192,0},{224,... | collective-permute-start | bytes 589832 | tf_op jit(solution)/shard_map/ppermute | solution.py:25
  37.7 8.4 %collective-permute-start.9 = (bf16[2,2,128,256]{3,2,1,0:T(8,128)(2,1)S(1)}, bf16[2,2,128,256]{3,2,1,0:T(8,128)(2,1)S(1)}, u32[]{:S(2)}, u32[]{:S(2)}) collective-permute-start(bf16[2,2,128,256]{3,2,1,0:T(8,128)(2,1)S(1)} %get-tuple-element.95), channel_id=1, source_target_pairs={{0,6},{1,7},{2,4},{3,5},{4,2},{5,3},{6,0},{7,1},{8,14},{9,15},{10,... | collective-permute-start | bytes 786440 | tf_op jit(solution)/shard_map/ppermute | solution.py:25
  43.3 12.1 %collective-permute-start.12 = (bf16[32,128,256]{2,1,0:T(8,128)(2,1)S(1)}, bf16[32,128,256]{2,1,0:T(8,128)(2,1)S(1)}, u32[]{:S(2)}, u32[]{:S(2)}) collective-permute-start(bf16[32,128,256]{2,1,0:T(8,128)(2,1)S(1)} %forward2.1), channel_id=1, source_target_pairs={{0,1},{1,0},{2,3},{3,2},{4,5},{5,4},{6,7},{7,6},{8,9},{9,8},{10,11... | collective-permute-start | bytes 6291464 | tf_op jit(solution)/shard_map/ppermute | solution.py:25
  57.1 15.7 %collective-permute-start.16 = (bf16[2,2,256,256]{3,2,1,0:T(8,128)(2,1)S(1)}, bf16[2,2,256,256]{3,2,1,0:T(8,128)(2,1)}, u32[]{:S(2)}, u32[]{:S(2)}) collective-permute-start(bf16[2,2,256,256]{3,2,1,0:T(8,128)(2,1)S(1)} %get-tuple-element.56), channel_id=1, source_target_pairs={{0,2},{1,3},{2,0},{3,1},{4,6},{5,7},{6,4},{7,5},{8,10},{9,11},{10,... | collective-permute-start | bytes 1572872 | tf_op jit(solution)/shard_map/ppermute | solution.py:25
  58.3 14.4 %collective-permute-start.17 = (bf16[2,2,256,256]{3,2,1,0:T(8,128)(2,1)S(1)}, bf16[2,2,256,256]{3,2,1,0:T(8,128)(2,1)}, u32[]{:S(2)}, u32[]{:S(2)}) collective-permute-start(bf16[2,2,256,256]{3,2,1,0:T(8,128)(2,1)S(1)} %get-tuple-element.57), channel_id=1, source_target_pairs={{0,6},{1,7},{2,4},{3,5},{4,2},{5,3},{6,0},{7,1},{8,14},{9,15},{10,... | collective-permute-start | bytes 1572872 | tf_op jit(solution)/shard_map/ppermute | solution.py:25
  59.0 8.3 %collective-permute-start.13 = (bf16[128,256]{1,0:T(8,128)(2,1)S(1)}, bf16[128,256]{1,0:T(8,128)(2,1)}, u32[]{:S(2)}, u32[]{:S(2)}) collective-permute-start(bf16[128,256]{1,0:T(8,128)(2,1)S(1)} %fusion.26), channel_id=1, source_target_pairs={{0,8},{1,9},{2,10},{3,11},{4,12},{5,13},{6,14},{7,15},{8,0},{9,1},... | collective-permute-start | bytes 196616 | tf_op jit(solution)/shard_map/ppermute | solution.py:25
  74.2 9.3 %collective-permute-start.18 = (bf16[2,256,256]{2,1,0:T(8,128)(2,1)S(1)}, bf16[2,256,256]{2,1,0:T(8,128)(2,1)S(1)}, u32[]{:S(2)}, u32[]{:S(2)}) collective-permute-start(bf16[2,256,256]{2,1,0:T(8,128)(2,1)S(1)} %get-tuple-element.60), channel_id=1, source_target_pairs={{0,6},{1,7},{2,4},{3,5},{4,2},{5,3},{6,0},{7,1},{8,14},{9,15},{10,... | collective-permute-start | bytes 786440 | tf_op jit(solution)/shard_map/ppermute | solution.py:25
  75.2 8.4 %collective-permute-start.19 = (bf16[2,256,256]{2,1,0:T(8,128)(2,1)S(1)}, bf16[2,256,256]{2,1,0:T(8,128)(2,1)S(1)}, u32[]{:S(2)}, u32[]{:S(2)}) collective-permute-start(bf16[2,256,256]{2,1,0:T(8,128)(2,1)S(1)} %get-tuple-element.61), channel_id=1, source_target_pairs={{0,2},{1,3},{2,0},{3,1},{4,6},{5,7},{6,4},{7,5},{8,10},{9,11},{10,... | collective-permute-start | bytes 786440 | tf_op jit(solution)/shard_map/ppermute | solution.py:25
  78.2 10.2 %collective-permute-start.25 = (bf16[128,256]{1,0:T(8,128)(2,1)S(1)}, bf16[128,256]{1,0:T(8,128)(2,1)S(1)}, u32[]{:S(2)}, u32[]{:S(2)}) collective-permute-start(bf16[128,256]{1,0:T(8,128)(2,1)S(1)} %fusion.1), channel_id=1, source_target_pairs={{0,24},{1,25},{2,26},{3,27},{4,28},{5,29},{6,30},{7,31},{8,16},{9,... | collective-permute-start | bytes 196616 | tf_op jit(solution)/shard_map/ppermute | solution.py:25
  81.6 8.5 %collective-permute-start.24 = (bf16[128,256]{1,0:T(8,128)(2,1)S(1)}, bf16[128,256]{1,0:T(8,128)(2,1)S(1)}, u32[]{:S(2)}, u32[]{:S(2)}) collective-permute-start(bf16[128,256]{1,0:T(8,128)(2,1)S(1)} %fusion.1), channel_id=1, source_target_pairs={{0,16},{1,17},{2,18},{3,19},{4,20},{5,21},{6,22},{7,23},{8,24},{9,... | collective-permute-start | bytes 196616 | tf_op jit(solution)/shard_map/ppermute | solution.py:25
  85.0 8.9 %collective-permute-start.20 = (bf16[256,256]{1,0:T(8,128)(2,1)S(1)}, bf16[256,256]{1,0:T(8,128)(2,1)S(1)}, u32[]{:S(2)}, u32[]{:S(2)}) collective-permute-start(bf16[256,256]{1,0:T(8,128)(2,1)S(1)} %get-tuple-element.67), channel_id=1, source_target_pairs={{0,8},{1,9},{2,10},{3,11},{4,12},{5,13},{6,14},{7,15},{8,0},{9,1},... | collective-permute-start | bytes 393224 | tf_op jit(solution)/shard_map/ppermute | solution.py:25
  87.7 10.7 %collective-permute-start.21 = (bf16[256,256]{1,0:T(8,128)(2,1)S(1)}, bf16[256,256]{1,0:T(8,128)(2,1)S(1)}, u32[]{:S(2)}, u32[]{:S(2)}) collective-permute-start(bf16[256,256]{1,0:T(8,128)(2,1)S(1)} %get-tuple-element.68), channel_id=1, source_target_pairs={{0,16},{1,17},{2,18},{3,19},{4,20},{5,21},{6,22},{7,23},{8,24},{9,... | collective-permute-start | bytes 393224 | tf_op jit(solution)/shard_map/ppermute | solution.py:25
  88.4 10.0 %collective-permute-start.22 = (bf16[256,256]{1,0:T(8,128)(2,1)S(1)}, bf16[256,256]{1,0:T(8,128)(2,1)S(1)}, u32[]{:S(2)}, u32[]{:S(2)}) collective-permute-start(bf16[256,256]{1,0:T(8,128)(2,1)S(1)} %get-tuple-element.69), channel_id=1, source_target_pairs={{0,24},{1,25},{2,26},{3,27},{4,28},{5,29},{6,30},{7,31},{8,16},{9,... | collective-permute-start | bytes 393224 | tf_op jit(solution)/shard_map/ppermute | solution.py:25
  90.1 14.0 %collective-permute-start.30 = (bf16[512,256]{1,0:T(8,128)(2,1)S(1)}, bf16[512,256]{1,0:T(8,128)(2,1)S(1)}, u32[]{:S(2)}, u32[]{:S(2)}) collective-permute-start(bf16[512,256]{1,0:T(8,128)(2,1)S(1)} %pad_maximum_fusion.4.rest_0_), channel_id=1, source_target_pairs={{0,6},{1,7},{2,4},{3,5},{4,2},{5,3},{6,0},{7,1},{8,14},{9,15},{10,... | collective-permute-start | bytes 786440 | tf_op jit(solution)/shard_map/ppermute | solution.py:25
  91.5 12.7 %collective-permute-start.29 = (bf16[512,256]{1,0:T(8,128)(2,1)S(1)}, bf16[512,256]{1,0:T(8,128)(2,1)S(1)}, u32[]{:S(2)}, u32[]{:S(2)}) collective-permute-start(bf16[512,256]{1,0:T(8,128)(2,1)S(1)} %pad_maximum_fusion.4.rest_0_), channel_id=1, source_target_pairs={{0,2},{1,3},{2,0},{3,1},{4,6},{5,7},{6,4},{7,5},{8,10},{9,11},{10,... | collective-permute-start | bytes 786440 | tf_op jit(solution)/shard_map/ppermute | solution.py:25
  99.6 11.4 %collective-permute-start.26 = (bf16[320,256]{1,0:T(8,128)(2,1)S(1)}, bf16[320,256]{1,0:T(8,128)(2,1)S(1)}, u32[]{:S(2)}, u32[]{:S(2)}) collective-permute-start(bf16[320,256]{1,0:T(8,128)(2,1)S(1)} %get-tuple-element.73), channel_id=1, source_target_pairs={{0,8},{1,9},{2,10},{3,11},{4,12},{5,13},{6,14},{7,15},{8,0},{9,1},... | collective-permute-start | bytes 491528 | tf_op jit(solution)/shard_map/ppermute | solution.py:25
  101.7 12.5 %collective-permute-start.27 = (bf16[320,256]{1,0:T(8,128)(2,1)S(1)}, bf16[320,256]{1,0:T(8,128)(2,1)S(1)}, u32[]{:S(2)}, u32[]{:S(2)}) collective-permute-start(bf16[320,256]{1,0:T(8,128)(2,1)S(1)} %get-tuple-element.74), channel_id=1, source_target_pairs={{0,16},{1,17},{2,18},{3,19},{4,20},{5,21},{6,22},{7,23},{8,24},{9,... | collective-permute-start | bytes 491528 | tf_op jit(solution)/shard_map/ppermute | solution.py:25
  101.7 12.5 %collective-permute-start.28 = (bf16[320,256]{1,0:T(8,128)(2,1)S(1)}, bf16[320,256]{1,0:T(8,128)(2,1)S(1)}, u32[]{:S(2)}, u32[]{:S(2)}) collective-permute-start(bf16[320,256]{1,0:T(8,128)(2,1)S(1)} %get-tuple-element.75), channel_id=1, source_target_pairs={{0,24},{1,25},{2,26},{3,27},{4,28},{5,29},{6,30},{7,31},{8,16},{9,... | collective-permute-start | bytes 491528 | tf_op jit(solution)/shard_map/ppermute | solution.py:25
  114.2 13.2 %collective-permute-start.34 = (bf16[1088,256]{1,0:T(8,128)(2,1)S(1)}, bf16[1088,256]{1,0:T(8,128)(2,1)S(1)}, u32[]{:S(2)}, u32[]{:S(2)}) collective-permute-start(bf16[1088,256]{1,0:T(8,128)(2,1)S(1)} %fusion.27.rest_0_), channel_id=1, source_target_pairs={{0,6},{1,7},{2,4},{3,5},{4,2},{5,3},{6,0},{7,1},{8,14},{9,15},{10,... | collective-permute-start | bytes 1671176 | tf_op jit(solution)/shard_map/ppermute | solution.py:25
  115.9 13.3 %collective-permute-start.33 = (bf16[1088,256]{1,0:T(8,128)(2,1)S(1)}, bf16[1088,256]{1,0:T(8,128)(2,1)S(1)}, u32[]{:S(2)}, u32[]{:S(2)}) collective-permute-start(bf16[1088,256]{1,0:T(8,128)(2,1)S(1)} %fusion.27.rest_0_), channel_id=1, source_target_pairs={{0,2},{1,3},{2,0},{3,1},{4,6},{5,7},{6,4},{7,5},{8,10},{9,11},{10,... | collective-permute-start | bytes 1671176 | tf_op jit(solution)/shard_map/ppermute | solution.py:25
  129.3 13.1 %collective-permute-start.38 = (bf16[3072,256]{1,0:T(8,128)(2,1)S(1)}, bf16[3072,256]{1,0:T(8,128)(2,1)S(1)}, u32[]{:S(2)}, u32[]{:S(2)}) collective-permute-start(bf16[3072,256]{1,0:T(8,128)(2,1)S(1)} %pad_maximum_fusion), channel_id=1, source_target_pairs={{0,1},{1,0},{2,3},{3,2},{4,5},{5,4},{6,7},{7,6},{8,9},{9,8},{10,11... | collective-permute-start | bytes 4718600 | tf_op jit(solution)/shard_map/ppermute | solution.py:25
  129.5 9.5 %collective-permute-start.36 = (bf16[576,256]{1,0:T(8,128)(2,1)S(1)}, bf16[576,256]{1,0:T(8,128)(2,1)S(1)}, u32[]{:S(2)}, u32[]{:S(2)}) collective-permute-start(bf16[576,256]{1,0:T(8,128)(2,1)S(1)} %pad_maximum_fusion.3), channel_id=1, source_target_pairs={{0,6},{1,7},{2,4},{3,5},{4,2},{5,3},{6,0},{7,1},{8,14},{9,15},{10,... | collective-permute-start | bytes 884744 | tf_op jit(solution)/shard_map/ppermute | solution.py:25
  131.2 9.1 %collective-permute-start.37 = (bf16[512,256]{1,0:T(8,128)(2,1)S(1)}, bf16[512,256]{1,0:T(8,128)(2,1)S(1)}, u32[]{:S(2)}, u32[]{:S(2)}) collective-permute-start(bf16[512,256]{1,0:T(8,128)(2,1)S(1)} %slice.314), channel_id=1, source_target_pairs={{0,2},{1,3},{2,0},{3,1},{4,6},{5,7},{6,4},{7,5},{8,10},{9,11},{10,... | collective-permute-start | bytes 786440 | tf_op jit(solution)/shard_map/ppermute | solution.py:25
  142.4 13.0 %collective-permute-start.41 = (f32[64,256]{1,0:T(8,128)S(1)}, f32[64,256]{1,0:T(8,128)S(1)}, u32[]{:S(2)}, u32[]{:S(2)}) collective-permute-start(f32[64,256]{1,0:T(8,128)S(1)} %add.280), channel_id=1, source_target_pairs={{0,32},{32,0},{64,96},{96,64},{128,160},{160,128},{192,224},{224,1... | collective-permute-start | bytes 196616 | tf_op jit(solution)/shard_map/ppermute | solution.py:25
  150.3 19.4 %collective-permute-start.44 = (bf16[2,384,256]{2,1,0:T(8,128)(2,1)S(1)}, bf16[2,384,256]{2,1,0:T(8,128)(2,1)S(1)}, u32[]{:S(2)}, u32[]{:S(2)}) collective-permute-start(bf16[2,384,256]{2,1,0:T(8,128)(2,1)S(1)} %bitcast.130), channel_id=1, source_target_pairs={{0,192},{32,224},{64,128},{96,160},{128,64},{160,96},{192,0},{224,... | collective-permute-start | bytes 1179656 | tf_op jit(solution)/shard_map/ppermute | solution.py:25
  155.5 11.4 %collective-permute-start.42 = (bf16[832,256]{1,0:T(8,128)(2,1)S(1)}, bf16[832,256]{1,0:T(8,128)(2,1)S(1)}, u32[]{:S(2)}, u32[]{:S(2)}) collective-permute-start(bf16[832,256]{1,0:T(8,128)(2,1)S(1)} %pad_maximum_fusion.2), channel_id=1, source_target_pairs={{0,64},{32,96},{64,0},{96,32},{128,192},{160,224},{192,128},{224,1... | collective-permute-start | bytes 1277960 | tf_op jit(solution)/shard_map/ppermute | solution.py:25
  169.8 9.5 %collective-permute-start.45 = (bf16[384,256]{1,0:T(8,128)(2,1)S(1)}, bf16[384,256]{1,0:T(8,128)(2,1)S(1)}, u32[]{:S(2)}, u32[]{:S(2)}) collective-permute-start(bf16[384,256]{1,0:T(8,128)(2,1)S(1)} %fusion.11), channel_id=1, source_target_pairs={{0,64},{32,96},{64,0},{96,32},{128,192},{160,224},{192,128},{224,1... | collective-permute-start | bytes 589832 | tf_op jit(solution)/shard_map/ppermute | solution.py:25
  174.6 8.8 %collective-permute-start.47 = (bf16[64,256]{1,0:T(8,128)(2,1)S(1)}, bf16[64,256]{1,0:T(8,128)(2,1)S(1)}, u32[]{:S(2)}, u32[]{:S(2)}) collective-permute-start(bf16[64,256]{1,0:T(8,128)(2,1)S(1)} %get-tuple-element.84), channel_id=1, source_target_pairs={{0,8},{1,9},{2,10},{3,11},{4,12},{5,13},{6,14},{7,15},{8,0},{9,1},... | collective-permute-start | bytes 98312 | tf_op jit(solution)/shard_map/ppermute | solution.py:25
  179.4 14.1 %collective-permute-start.46 = (bf16[384,256]{1,0:T(8,128)(2,1)S(1)}, bf16[384,256]{1,0:T(8,128)(2,1)S(1)}, u32[]{:S(2)}, u32[]{:S(2)}) collective-permute-start(bf16[384,256]{1,0:T(8,128)(2,1)S(1)} %fusion.13), channel_id=1, source_target_pairs={{0,32},{32,0},{64,96},{96,64},{128,160},{160,128},{192,224},{224,1... | collective-permute-start | bytes 589832 | tf_op jit(solution)/shard_map/ppermute | solution.py:25
  181.0 11.7 %collective-permute-start.48 = (bf16[64,256]{1,0:T(8,128)(2,1)S(1)}, bf16[64,256]{1,0:T(8,128)(2,1)S(1)}, u32[]{:S(2)}, u32[]{:S(2)}) collective-permute-start(bf16[64,256]{1,0:T(8,128)(2,1)S(1)} %get-tuple-element.84), channel_id=1, source_target_pairs={{0,16},{1,17},{2,18},{3,19},{4,20},{5,21},{6,22},{7,23},{8,24},{9,... | collective-permute-start | bytes 98312 | tf_op jit(solution)/shard_map/ppermute | solution.py:25
  181.7 11.0 %collective-permute-start.49 = (bf16[64,256]{1,0:T(8,128)(2,1)S(1)}, bf16[64,256]{1,0:T(8,128)(2,1)S(1)}, u32[]{:S(2)}, u32[]{:S(2)}) collective-permute-start(bf16[64,256]{1,0:T(8,128)(2,1)S(1)} %get-tuple-element.84), channel_id=1, source_target_pairs={{0,24},{1,25},{2,26},{3,27},{4,28},{5,29},{6,30},{7,31},{8,16},{9,... | collective-permute-start | bytes 98312 | tf_op jit(solution)/shard_map/ppermute | solution.py:25
  (34 other events, 432.8 us)
